TPU v7x, 32 devices: a whole 2x2x4 slice. The times are simulated.
32 devices in a mesh: region: 8 (over z, y), member: 4 (over x, core).
Axes of the slice: x: 2, y: 2, z: 4, core: 2. Of those that a mesh axis runs over, the one named last changes fastest.
Arguments:
- ensemble: bfloat16 [256, 16384], P('member', 'region'), may hold values from -6 to 6
- reports: float32 [8, 1024], P('region'), may hold values from -6 to 6
- report_count: int32 [8], P('region'), may hold values from 128 to 1024, as said below
- report_cell: int32 [8, 1024], P('region'), may hold values from 0 to 16383, as said below
- report_weight: float32 [8, 16, 1024], P('region', 'member'), may hold values from 0.001 to 1
- blending: float32 [4, 16384], P(None, ('region', 'member')), may hold values from 0.02 to 1
Outputs:
- analysis: bfloat16 [16384, 256], P(('region', 'member'))
Inputs may be any that keep to these rules, and one draw needn't show every extreme that they name: `report_count`: the largest value 1024 is reached by some region in every draw. `report_cell`: every cell lies in the slot's own region, or in the first 128 cells of one of at most two other regions chosen for that region.
All inputs are finite; a program needn't handle non-finite values.
Results may differ from a plain program's by a relative error of at most 0.0055.
Values may be sent and summed in bfloat16 or wider, within the bound.
No kernel may reach another device: no remote copies, remote signals or barrier semaphores. Data moves between devices by JAX's collectives and lax.ppermute only.
A program may use at most 64 MiB of HBM per device.

v0:
```python
import jax
import jax.numpy as jnp
from jax import lax
from jax.sharding import PartitionSpec as P

MARGIN = 128
SWEEPS = 4


highest = lax.Precision.HIGHEST


def extended(block, sides, width):
    for axis, dim in sides:
        count = lax.axis_size(axis)
        forward = [(i, i + 1) for i in range(count - 1)]
        backward = [(target, source) for source, target in forward]
        low = lax.ppermute(
            lax.slice_in_dim(block, block.shape[dim] - width, None, axis=dim), axis, forward
        )
        high = lax.ppermute(lax.slice_in_dim(block, 0, width, axis=dim), axis, backward)
        block = jnp.concatenate([low, block, high], axis=dim)
    return block


def make_transform(products, forcing, members):
    identity = jnp.eye(members, dtype=jnp.float32)
    precision_mat = (members - 1.0) * identity[None] + products
    frobenius = jnp.sqrt(jnp.sum(precision_mat * precision_mat, axis=(1, 2)))
    current = precision_mat / frobenius[:, None, None]
    root_iter = jnp.broadcast_to(identity, current.shape)
    for iteration in range(SWEEPS):
        middle = 1.5 * identity[None] - 0.5 * jnp.einsum(
            "aij,ajk->aik", root_iter, current, precision=highest
        )
        current = jnp.einsum("aij,ajk->aik", current, middle, precision=highest)
        root_iter = jnp.einsum("aij,ajk->aik", middle, root_iter, precision=highest)
    inverse_root = root_iter / jnp.sqrt(frobenius)[:, None, None]
    inner_step = jnp.einsum("aij,aj->ai", inverse_root, forcing, precision=highest)
    mean_weights = jnp.einsum("aij,aj->ai", inverse_root, inner_step, precision=highest)
    return (mean_weights[:, :, None] + jnp.sqrt(members - 1.0) * inverse_root).astype(jnp.bfloat16)


def corner_layout(band_index, points_here, row_count):
    group_index = jnp.arange(4 * points_here, dtype=jnp.int32)
    upper_half = group_index // (2 * points_here)
    column_block = group_index // 2 % points_here
    right_half = group_index % 2
    row_base = jnp.clip(band_index - 1 + upper_half, 0, row_count - 2)
    col_base = jnp.clip(column_block - 1 + right_half, 0, points_here - 2)
    return (row_base, col_base)


def per_device(ensemble, reports, report_count, report_cell, report_weight, blending):
    local_members, cell_count = ensemble.shape
    groups = lax.axis_size("member")
    members = local_members * groups
    region = lax.axis_index("region")
    member = lax.axis_index("member")
    targets = report_cell[0]
    holder = targets // cell_count
    within = targets % cell_count
    is_local = holder == region
    local_values = jnp.take(ensemble, jnp.where(is_local, within, 0), axis=1).astype(jnp.float32)
    border = ensemble[:, :MARGIN]
    border_index = holder * MARGIN + jnp.minimum(within, MARGIN - 1)
    pieces = lax.all_gather(border, "region", axis=1, tiled=True)
    extent = pieces.shape[1]
    inside = (border_index >= 0) & (border_index < extent) & jnp.logical_not(is_local)
    picked = jnp.take(pieces, jnp.clip(border_index, 0, extent - 1), axis=1).astype(jnp.float32)
    remote = jnp.where(inside[None, :], picked, 0.0)
    at_reports = jnp.where(is_local[None, :], local_values, remote)
    report_mean = lax.psum(jnp.sum(at_reports, axis=0), "member") / members
    local_pert = (at_reports - report_mean[None, :]).astype(jnp.bfloat16)
    report_pert = lax.all_gather(local_pert, "member", axis=0, tiled=True)
    active = (jnp.arange(report_pert.shape[1]) < report_count[0]).astype(jnp.float32)
    weights = report_weight[0] * active[None, :]
    weighted = (report_pert[None, :, :] * weights[:, None, :]).astype(jnp.bfloat16)
    departure = (weights * (reports[0] - report_mean)[None, :]).astype(jnp.bfloat16)
    products = jnp.einsum("ako,jo->akj", weighted, report_pert, preferred_element_type=jnp.float32)
    forcing = jnp.einsum("ao,ko->ak", departure, report_pert, preferred_element_type=jnp.float32)
    transform = make_transform(products, forcing, members)
    points_here = transform.shape[0]
    groups_band = 4 * points_here
    slab_cells = cell_count // groups
    group_cells = slab_cells // groups_band
    mixing = blending / jnp.sum(blending, axis=0, keepdims=True)
    columns = lax.all_to_all(ensemble, "member", split_axis=1, concat_axis=0, tiled=True)
    cell_mean = jnp.sum(columns, axis=0, dtype=jnp.float32) / members
    anomaly = (columns - cell_mean[None, :]).astype(jnp.bfloat16)
    anomaly_view = anomaly.reshape(members, groups_band, group_cells)
    mix_view = mixing.reshape(4, groups_band, group_cells)
    neighbours = extended(transform[None], (("member", 0),), 1)
    stacked = neighbours.reshape(3 * points_here, members, members)
    row_base, col_base = corner_layout(member, points_here, groups)
    running = jnp.zeros((groups_band, group_cells, members), jnp.float32)
    for corner in range(4):
        row_step = corner // 2
        col_step = corner % 2
        chosen_index = (row_base + row_step - (member - 1)) * points_here + col_base + col_step
        chosen = jnp.take(stacked, chosen_index, axis=0)
        spread = jnp.einsum(
            "kgc,gkj->gcj", anomaly_view, chosen, preferred_element_type=jnp.float32
        )
        running = running + mix_view[corner][:, :, None] * spread
    blended = running.reshape(slab_cells, members)
    return (cell_mean[:, None] + blended).astype(jnp.bfloat16)


def solution(mesh):
    return jax.shard_map(
        per_device,
        mesh=mesh,
        in_specs=(
            P("member", "region"),
            P("region", None),
            P("region"),
            P("region", None),
            P("region", "member", None),
            P(None, ("region", "member")),
        ),
        out_specs=P(("region", "member"), None),
        check_vma=False,
    )
```

profile of v0, /device:TPU:0, one launch (start us, length us, event | category | flops | bytes accessed | tf_op | source)
XLA Modules:
  0.0 104.7 jit_solution(4873198254214473473)
XLA Ops:
  0.0 0.8 compare_select_fusion
  0.8 0.7 and_select_fusion.3
  1.6 1.2 %copy.24 = bf16[64,2048]{0,1:T(8,128)(2,1)S(1)} copy(bf16[64,2048]{1,0:T(8,128)(2,1)} %param.8) | data formatting | bytes 524288 | tf_op args[0]
  2.9 0.0 copy-start.7
  2.9 3.2 %gather_fusion = bf16[1024,64]{1,0:T(8,128)(2,1)S(1)} fusion(bf16[64,2048]{0,1:T(8,128)(2,1)S(1)} %copy.24, s32[1024]{0:T(1024)S(1)} %broadcast_clamp_fusion.1), kind=kCustom, calls=%fused_computation.4 | custom fusion | bytes 266240 | tf_op jit(solution)/shard_map/jit(_take)/gather | solution.py:64
  6.1 0.1 copy.25
  6.2 0.0 copy-done.4
  6.3 32.6 %all_gather.6 = bf16[64,1024]{0,1:T(8,128)(2,1)S(1)} all-gather(bf16[64,128]{0,1:T(8,128)(2,1)S(1)} %slice.37), channel_id=1, replica_groups=mesh['region'=8,'member'=4] {'region'}, dimensions={1}, use_global_device_ids=true | all-gather | bytes 147456 | tf_op jit(solution)/shard_map/all_gather | solution.py:67
  38.9 3.2 %gather_fusion.1 = bf16[1024,64]{1,0:T(8,128)(2,1)S(1)} fusion(bf16[64,1024]{0,1:T(8,128)(2,1)S(1)} %all_gather.6, s32[1024]{0:T(1024)S(1)} %broadcast_clamp_fusion), kind=kCustom, calls=%fused_computation.5 | custom fusion | bytes 266240 | tf_op jit(solution)/shard_map/jit(_take)/gather | solution.py:70
  42.1 0.1 copy.27
  42.2 0.1 and_reduce_fusion
  42.3 0.1 fusion.54
  42.3 5.7 %psum.7 = f32[1024]{0:T(1024)S(1)} all-reduce(f32[1024]{0:T(1024)S(1)} %fusion.54), channel_id=1, replica_groups=mesh['region'=8,'member'=4] {'member'}, use_global_device_ids=true, to_apply=%region_3.4 | all-reduce | flops 1024 | bytes 8192 | tf_op jit(solution)/shard_map/psum | solution.py:73
  48.0 0.0 copy-done.7
  48.0 0.1 fusion.56
  48.1 7.4 %all_gather.7 = bf16[256,1024]{1,0:T(8,128)(2,1)S(1)} all-gather(bf16[64,1024]{1,0:T(8,128)(2,1)S(1)} %fusion.56), channel_id=1, replica_groups=mesh['region'=8,'member'=4] {'member'}, dimensions={0}, use_global_device_ids=true | all-gather | bytes 655360 | tf_op jit(solution)/shard_map/all_gather | solution.py:75
  55.5 0.1 convert_element_type.67
  56.3 0.9 multiply_reduce_fusion
  57.2 1.2 %fusion.19 = f32[4,256,256]{2,1,0:T(8,128)S(1)} fusion(f32[256,256]{1,0:T(8,128)S(1)} %fusion.52, f32[256,256]{1,0:T(8,128)S(1)} %fusion.53, f32[4,256,256]{2,1,0:T(8,128)S(1)} %get-tuple-element.24, f32[4]{0:T(128)S(1)} %get-tuple-element.22), kind=kOutput, calls=%fused_computation.32 | convolution fusion | flops 806092800 | bytes 2621456 | tf_op jit(solution)/shard_map/aij,ajk->aik/dot_general | solution.py:33
  58.4 1.2 %fusion.55 = f32[4,256,256]{2,1,0:T(8,128)S(1)} fusion(f32[4,256,256]{2,1,0:T(8,128)S(1)} %fusion.19, f32[4,256,256]{2,1,0:T(8,128)S(1)} %get-tuple-element.24, f32[4]{0:T(128)S(1)} %get-tuple-element.22), kind=kOutput, calls=%fused_computation.66 | convolution fusion | flops 805568512 | bytes 3145744 | tf_op jit(solution)/shard_map/aij,ajk->aik/dot_general | solution.py:36
  59.6 1.1 %fusion.48 = f32[4,256,256]{2,1,0:T(8,128)S(1)} fusion(f32[4,256,256]{2,1,0:T(8,128)S(1)} %fusion.19, f32[256,256]{1,0:T(8,128)S(1)} %fusion.52), kind=kOutput, calls=%fused_computation.54 | convolution fusion | flops 805306368 | bytes 2359296 | tf_op jit(solution)/shard_map/aij,ajk->aik/dot_general | solution.py:37
  60.7 1.2 %fusion.18 = f32[4,256,256]{2,1,0:T(8,128)S(1)} fusion(f32[4,256,256]{2,1,0:T(8,128)S(1)} %fusion.48, f32[4,256,256]{2,1,0:T(8,128)S(1)} %fusion.55, f32[256,256]{1,0:T(8,128)S(1)} %fusion.53), kind=kOutput, calls=%fused_computation.30 | convolution fusion | flops 805830656 | bytes 3407872 | tf_op jit(solution)/shard_map/aij,ajk->aik/dot_general | solution.py:33
  61.9 1.1 %fusion.79 = f32[4,256,256]{2,1,0:T(8,128)S(1)} fusion(f32[4,256,256]{2,1,0:T(8,128)S(1)} %fusion.55, f32[4,256,256]{2,1,0:T(8,128)S(1)} %fusion.18), kind=kOutput, calls=%fused_computation.158 | convolution fusion | flops 805306368 | bytes 3145728 | tf_op jit(solution)/shard_map/aij,ajk->aik/dot_general | solution.py:36
  63.0 1.1 %fusion.78 = f32[4,256,256]{2,1,0:T(8,128)S(1)} fusion(f32[4,256,256]{2,1,0:T(8,128)S(1)} %fusion.18, f32[4,256,256]{2,1,0:T(8,128)S(1)} %fusion.48), kind=kOutput, calls=%fused_computation.157 | convolution fusion | flops 805306368 | bytes 3145728 | tf_op jit(solution)/shard_map/aij,ajk->aik/dot_general | solution.py:37
  64.2 1.2 %fusion.17 = f32[4,256,256]{2,1,0:T(8,128)S(1)} fusion(f32[4,256,256]{2,1,0:T(8,128)S(1)} %fusion.78, f32[4,256,256]{2,1,0:T(8,128)S(1)} %fusion.79, f32[256,256]{1,0:T(8,128)S(1)} %fusion.53), kind=kOutput, calls=%fused_computation.28 | convolution fusion | flops 805830656 | bytes 3407872 | tf_op jit(solution)/shard_map/aij,ajk->aik/dot_general | solution.py:33
  65.4 1.1 %fusion.81 = f32[4,256,256]{2,1,0:T(8,128)S(1)} fusion(f32[4,256,256]{2,1,0:T(8,128)S(1)} %fusion.79, f32[4,256,256]{2,1,0:T(8,128)S(1)} %fusion.17), kind=kOutput, calls=%fused_computation.160 | convolution fusion | flops 805306368 | bytes 3145728 | tf_op jit(solution)/shard_map/aij,ajk->aik/dot_general | solution.py:36
  66.5 1.1 %fusion.80 = f32[4,256,256]{2,1,0:T(8,128)S(1)} fusion(f32[4,256,256]{2,1,0:T(8,128)S(1)} %fusion.17, f32[4,256,256]{2,1,0:T(8,128)S(1)} %fusion.78), kind=kOutput, calls=%fused_computation.159 | convolution fusion | flops 805306368 | bytes 3145728 | tf_op jit(solution)/shard_map/aij,ajk->aik/dot_general | solution.py:37
  67.7 0.2 convolution_bitcast_fusion
  67.9 1.4 %fusion.16 = f32[4,256,256]{2,1,0:T(8,128)S(1)} fusion(f32[4,256,256]{2,1,0:T(8,128)S(1)} %fusion.80, f32[4,256,256]{2,1,0:T(8,128)S(1)} %fusion.81, f32[256,256]{1,0:T(8,128)S(1)} %fusion.53), kind=kOutput, calls=%fused_computation.26 | convolution fusion | flops 805830656 | bytes 3407872 | tf_op jit(solution)/shard_map/aij,ajk->aik/dot_general | solution.py:33
  69.3 1.1 %convolution_divide_fusion = f32[4,256,256]{2,1,0:T(8,128)S(1)} fusion(f32[4,256,256]{2,1,0:T(8,128)S(1)} %fusion.16, f32[4,256,256]{2,1,0:T(8,128)S(1)} %fusion.80, f32[4]{0:T(128)S(1)} %get-tuple-element.21), kind=kOutput, calls=%fused_computation.24 | convolution fusion | flops 805568512 | bytes 3145744 | tf_op jit(solution)/shard_map/aij,ajk->aik/dot_general | solution.py:37
  70.5 0.0 copy-start.3
  70.5 1.0 fusion.62
  71.5 1.0 fusion.60
  72.5 0.2 fusion.45
  72.7 2.3 %collective-permute-start = (bf16[1,4,256,256]{3,2,1,0:T(8,128)(2,1)S(1)}, bf16[1,4,256,256]{3,2,1,0:T(8,128)(2,1)S(1)}, u32[]{:S(2)}, u32[]{:S(2)}) collective-permute-start(bf16[1,4,256,256]{3,2,1,0:T(8,128)(2,1)S(1)} %fusion.45), channel_id=1, source_target_pairs={{0,1},{1,2},{2,3},{4,5},{5,6},{6,7},{8,9},{9,10},{10,11},{12,13},{... | collective-permute-start | bytes 1572872 | tf_op jit(solution)/shard_map/ppermute | solution.py:18
  75.0 1.3 %collective-permute-start.1 = (bf16[1,4,256,256]{3,2,1,0:T(8,128)(2,1)S(1)}, bf16[1,4,256,256]{3,2,1,0:T(8,128)(2,1)S(1)}, u32[]{:S(2)}, u32[]{:S(2)}) collective-permute-start(bf16[1,4,256,256]{3,2,1,0:T(8,128)(2,1)S(1)} %fusion.45), channel_id=1, source_target_pairs={{1,0},{2,1},{3,2},{5,4},{6,5},{7,6},{9,8},{10,9},{11,10},{13,12},{... | collective-permute-start | bytes 1572872 | tf_op jit(solution)/shard_map/ppermute | solution.py:21
  76.3 0.7 copy.40
  77.0 4.1 %all-to-all-start = ((bf16[64,4,512]{2,0,1:T(8,128)(2,1)}), bf16[64,4,512]{2,0,1:T(8,128)(2,1)S(1)}, u32[]{:S(2)}, u32[]{:S(2)}) async-start(bf16[64,4,512]{2,0,1:T(8,128)(2,1)} %bitcast.73), calls=%async_computation | async-start | bytes 524288 | tf_op jit(solution)/shard_map/all_to_all | solution.py:88
  81.3 0.1 mul.175
  81.4 0.1 mul.178
  81.5 0.1 mul.182
  81.6 0.1 mul.148
  81.7 7.4 %all-to-all-done = bf16[64,4,512]{2,0,1:T(8,128)(2,1)S(1)} async-done(((bf16[64,4,512]{2,0,1:T(8,128)(2,1)}), bf16[64,4,512]{2,0,1:T(8,128)(2,1)S(1)}, u32[]{:S(2)}, u32[]{:S(2)}) %all-to-all-start) | async-done | bytes 262176 | tf_op jit(solution)/shard_map/all_to_all | solution.py:88
  89.1 0.1 convert_reduce_fusion
  89.2 0.1 div.84
  89.3 0.1 convert_bitcast_fusion
  89.3 0.4 copy.23
  89.7 0.6 reshape.254
  90.3 0.1 subtract_convert_fusion
  90.5 0.0 collective-permute-done
  90.5 0.0 collective-permute-done.1
  90.5 0.2 pad_maximum_fusion
  90.7 2.0 %gather_fusion.3 = bf16[16,256,256]{2,1,0:T(8,128)(2,1)} fusion(bf16[12,256,256]{2,1,0:T(8,128)(2,1)S(1)} %bitcast.77, s32[1024]{0:T(1024)S(1)} %pad_clamp_fusion.2), kind=kCustom, calls=%fused_computation.1.clone | custom fusion | bytes 4194368 | tf_op jit(solution)/shard_map/jit(_take)/gather | solution.py:101
  92.7 2.0 %gather_fusion.4 = bf16[16,256,256]{2,1,0:T(8,128)(2,1)} fusion(bf16[12,256,256]{2,1,0:T(8,128)(2,1)S(1)} %bitcast.78, s32[1024]{0:T(1024)S(1)} %pad_clamp_fusion.1), kind=kCustom, calls=%fused_computation.2.clone | custom fusion | bytes 4194368 | tf_op jit(solution)/shard_map/jit(_take)/gather | solution.py:101
  94.7 2.0 %gather_fusion.5 = bf16[16,256,256]{2,1,0:T(8,128)(2,1)} fusion(bf16[12,256,256]{2,1,0:T(8,128)(2,1)S(1)} %bitcast.79, s32[1024]{0:T(1024)S(1)} %pad_clamp_fusion), kind=kCustom, calls=%fused_computation.3.clone | custom fusion | bytes 4194368 | tf_op jit(solution)/shard_map/jit(_take)/gather | solution.py:101
  96.7 2.0 %gather_fusion.2 = bf16[16,256,256]{2,1,0:T(8,128)(2,1)} fusion(bf16[12,256,256]{2,1,0:T(8,128)(2,1)S(1)} %bitcast.80, s32[1024]{0:T(1024)S(1)} %pad_clamp_fusion.3), kind=kCustom, calls=%fused_computation.clone | custom fusion | bytes 4194368 | tf_op jit(solution)/shard_map/jit(_take)/gather | solution.py:101
  98.7 2.3 %fusion.29 = f32[16,32,256]{2,1,0:T(8,128)S(1)} fusion(bf16[256,16,32]{0,2,1:T(8,128)(2,1)S(1)} %subtract_convert_fusion, bf16[16,256,256]{2,1,0:T(8,128)(2,1)} %gather_fusion.3, pred[16]{0:T(512)(128)(4,1)S(1)} %compare_and_fusion.4, f32[16,32]{1,0:T(8,128)S(1)} %mul.175), kind=kOutput, calls=%fused_computation.36 | convolution fusion | flops 68288512 | bytes 2885648 | tf_op jit(solution)/shard_map/kgc,gkj->gcj/dot_general | solution.py:102
  101.0 0.5 fusion.32
  101.5 0.0 copy-start
  101.5 1.0 copy-done.1
  102.6 0.5 fusion.35
  103.1 0.2 copy-done
  103.3 0.5 fusion.38
  103.9 0.8 fusion.46
  (36 shorter events, 0.3 us)
Async XLA Ops:
  0.0 6.2 %copy-start.4 = (s32[1,1024]{1,0:T(1,128)S(1)}, s32[1,1024]{1,0:T(1,128)}, u32[]{:S(2)}) copy-start(s32[1,1024]{1,0:T(1,128)} %param.11) | copy-start | bytes 12292
  2.9 45.1 %copy-start.7 = (f32[1,1024]{1,0:T(1,128)S(1)}, f32[1,1024]{1,0:T(1,128)}, u32[]{:S(2)}) copy-start(f32[1,1024]{1,0:T(1,128)} %param.9) | copy-start | bytes 12292
  38.8 17.5 %copy-start.6 = (f32[1,4,1024]{2,1,0:T(4,128)S(1)}, f32[1,4,1024]{2,1,0:T(4,128)}, u32[]{:S(2)}) copy-start(f32[1,4,1024]{2,1,0:T(4,128)} %param.12) | copy-start | bytes 49156
  70.5 5.8 %copy-start.3 = (bf16[64,2048]{1,0:T(8,128)(2,1)S(1)}, bf16[64,2048]{1,0:T(8,128)(2,1)}, u32[]{:S(2)}) copy-start(bf16[64,2048]{1,0:T(8,128)(2,1)} %param.8) | copy-start | bytes 786436
  71.5 9.8 %copy-start.5 = (f32[4,512]{1,0:T(4,128)S(1)}, f32[4,512]{1,0:T(4,128)}, u32[]{:S(2)}) copy-start(f32[4,512]{1,0:T(4,128)} %param.13) | copy-start | bytes 24580
  72.7 17.8 %collective-permute-start = (bf16[1,4,256,256]{3,2,1,0:T(8,128)(2,1)S(1)}, bf16[1,4,256,256]{3,2,1,0:T(8,128)(2,1)S(1)}, u32[]{:S(2)}, u32[]{:S(2)}) collective-permute-start(bf16[1,4,256,256]{3,2,1,0:T(8,128)(2,1)S(1)} %fusion.45), channel_id=1, source_target_pairs={{0,1},{1,2},{2,3},{4,5},{5,6},{6,7},{8,9},{9,10},{10,11},{12,13},{... | collective-permute-start | bytes 1572872 | tf_op jit(solution)/shard_map/ppermute | solution.py:18
  75.0 15.5 %collective-permute-start.1 = (bf16[1,4,256,256]{3,2,1,0:T(8,128)(2,1)S(1)}, bf16[1,4,256,256]{3,2,1,0:T(8,128)(2,1)S(1)}, u32[]{:S(2)}, u32[]{:S(2)}) collective-permute-start(bf16[1,4,256,256]{3,2,1,0:T(8,128)(2,1)S(1)} %fusion.45), channel_id=1, source_target_pairs={{1,0},{2,1},{3,2},{5,4},{6,5},{7,6},{9,8},{10,9},{11,10},{13,12},{... | collective-permute-start | bytes 1572872 | tf_op jit(solution)/shard_map/ppermute | solution.py:21
  77.0 12.1 %all-to-all-start = ((bf16[64,4,512]{2,0,1:T(8,128)(2,1)}), bf16[64,4,512]{2,0,1:T(8,128)(2,1)S(1)}, u32[]{:S(2)}, u32[]{:S(2)}) async-start(bf16[64,4,512]{2,0,1:T(8,128)(2,1)} %bitcast.73), calls=%async_computation | async-start | bytes 524288 | tf_op jit(solution)/shard_map/all_to_all | solution.py:88
  98.7 2.3 %copy-start.2 = (bf16[16,256,256]{2,1,0:T(8,128)(2,1)S(1)}, bf16[16,256,256]{2,1,0:T(8,128)(2,1)}, u32[]{:S(2)}) copy-start(bf16[16,256,256]{2,1,0:T(8,128)(2,1)} %gather_fusion.4) | copy-start | bytes 6291460
  101.0 1.6 %copy-start.1 = (bf16[16,256,256]{2,1,0:T(8,128)(2,1)S(1)}, bf16[16,256,256]{2,1,0:T(8,128)(2,1)}, u32[]{:S(2)}) copy-start(bf16[16,256,256]{2,1,0:T(8,128)(2,1)} %gather_fusion.5) | copy-start | bytes 6291460
  101.5 1.8 %copy-start = (bf16[16,256,256]{2,1,0:T(8,128)(2,1)S(1)}, bf16[16,256,256]{2,1,0:T(8,128)(2,1)}, u32[]{:S(2)}) copy-start(bf16[16,256,256]{2,1,0:T(8,128)(2,1)} %gather_fusion.2) | copy-start | bytes 6291460
where the time goes:
time: 105 us
  blocking collectives  45.6 us (43%)
  matrix products  19.8 us (19%)
  local copies, waits for them, and re-layouts  19.4 us (18%)
  starting transfers between devices  7.71 us (7%)
  waiting for transfers between devices  7.42 us (7%)
  other arithmetic  3.57 us (3%)
  between operations  1.12 us (1%)
    all_gather x1, blocking collectives, per_device(): pieces = lax.all_gather(border, 'region', axis=1, tiled=True)  32.6 us
    gather x4, local copies, waits for them, and re-layouts, per_device(): chosen = jnp.take(stacked, chosen_index, axis=0)  8.04 us
    all_to_all x1, waiting for transfers between devices, per_device(): lax.all_to_all(ensemble, 'member', split_axis=1, concat_axis=0, tiled=True)  7.41 us
    all_gather x1, blocking collectives, per_device(): report_pert = lax.all_gather(local_pert, 'member', axis=0, tiled=True)  7.41 us
    psum x1, blocking collectives, per_device(): report_mean = lax.psum(jnp.sum(at_reports, axis=0), 'member') / members  5.67 us
    dot_general x4, matrix products, make_transform(): jnp.einsum('aij,ajk->aik', root_iter, current, precision=highest)  4.92 us
    dot_general x4, matrix products, make_transform(): root_iter = jnp.einsum('aij,ajk->aik', middle, root_iter, precision=highest)  4.53 us
    all_to_all x1, starting transfers between devices, per_device(): lax.all_to_all(ensemble, 'member', split_axis=1, concat_axis=0, tiled=True)  4.14 us
  transfers between devices with their start and end apart: 3, of which 1 were waited for; matrix products, arithmetic and copies ran while one was open for 2% of the time, Pallas kernels for 0%

commit v1 on v0

v1 whole, which is shorter than its diff:
```python
import functools

import jax
import jax.numpy as jnp
from jax import lax
from jax.experimental import pallas as pl
from jax.experimental.pallas import tpu as pltpu
from jax.sharding import PartitionSpec as P

MARGIN = 128
LANES = 128
AXES = ("region", "member")

f32 = jnp.float32
bf16 = jnp.bfloat16

VMEM = pl.BlockSpec(memory_space=pltpu.VMEM)
SMEM = pl.BlockSpec(memory_space=pltpu.SMEM)


def dot_nn(a, b):
    return lax.dot_general(a, b, (((1,), (0,)), ((), ())), preferred_element_type=f32)


def dot_nt(a, b):
    return lax.dot_general(a, b, (((1,), (1,)), ((), ())), preferred_element_type=f32)


def split(x):
    high = x.astype(bf16)
    return high, (x - high.astype(f32)).astype(bf16)


def call(kernel, outs, smem_count, inputs, flops, moved, scratch=()):
    return pl.pallas_call(
        kernel,
        out_shape=[jax.ShapeDtypeStruct(s, d) for s, d in outs],
        in_specs=[SMEM] * smem_count + [VMEM] * (len(inputs) - smem_count),
        out_specs=[VMEM] * len(outs),
        scratch_shapes=list(scratch),
        cost_estimate=pl.CostEstimate(flops=flops, bytes_accessed=moved, transcendentals=0),
    )(*inputs)


def weights_kernel(rows, numbers, cell_ref, weight_ref, report_ref, out_ref):
    cell = cell_ref[...]
    points, slots = weight_ref.shape[1:]
    count = numbers[4]
    holder = cell // count
    within = cell - holder * count
    low = within % LANES
    high = jnp.where(
        holder == numbers[0],
        within // LANES,
        jnp.where(holder == numbers[1], rows - 2, rows - 1),
    )
    active = lax.broadcasted_iota(jnp.int32, (1, slots), 1) < numbers[3]
    weights = jnp.where(active, weight_ref[0], 0.0)
    values = jnp.concatenate([weights, weights * report_ref[...]], axis=0)
    low_hot = (lax.broadcasted_iota(jnp.int32, (LANES, slots), 0) == low).astype(f32).astype(bf16)
    chosen = jnp.concatenate(
        [jnp.where(high == row, values, 0.0) for row in range(rows)], axis=0
    )
    first, second = split(chosen)
    total = dot_nt(first, low_hot) + dot_nt(second, low_hot)
    out_ref[...] = total.reshape(rows, 2 * points, LANES)


def anomaly_kernel(offsets, numbers, *refs):
    pieces, (anomaly_ref, mean_ref) = refs[:-2], refs[-2:]
    rows = pieces[0].shape[0]
    members = rows * len(pieces)
    total = jnp.sum(pieces[0][...].astype(f32), axis=0, keepdims=True)
    for piece in pieces[1:]:
        total = total + jnp.sum(piece[...].astype(f32), axis=0, keepdims=True)
    mean = total / members
    mean_ref[...] = mean
    for offset, piece in zip(offsets, pieces):
        start = pl.multiple_of((numbers[0] ^ offset) * rows, rows)
        anomaly_ref[pl.ds(start, rows), :] = (piece[...].astype(f32) - mean).astype(bf16)


def products_kernel(anomaly_ref, mean_ref, table_ref, products_ref, forcing_ref):
    members, cells = anomaly_ref.shape
    points = products_ref.shape[0]
    chunk = min(cells, 2048)
    forcing = None
    for start in range(0, cells, chunk):
        block = anomaly_ref[:, start : start + chunk]
        departures = []
        for a in range(points):
            scaled = []
            for h in range(start // LANES, (start + chunk) // LANES):
                lanes = slice(h * LANES, (h + 1) * LANES)
                scaled.append(
                    (anomaly_ref[:, lanes].astype(f32) * table_ref[h, a : a + 1, :]).astype(bf16)
                )
            part = dot_nt(jnp.concatenate(scaled, axis=1), block)
            if start == 0:
                products_ref[a] = part
            else:
                products_ref[a] += part
        for h in range(start // LANES, (start + chunk) // LANES):
            lanes = slice(h * LANES, (h + 1) * LANES)
            tile = table_ref[h]
            departures.append(tile[points:, :] - tile[:points, :] * mean_ref[:, lanes])
        departure = jnp.concatenate(departures, axis=1)
        first, second = split(jnp.concatenate([departure, departure], axis=0))
        part = dot_nt(first, block) + dot_nt(second, block)
        forcing = part if forcing is None else forcing + part
    forcing_ref[...] = forcing


def transpose_kernel(numbers, anomaly_ref, mean_ref, own_ref, first_ref, second_ref, column_ref):
    members = anomaly_ref.shape[0]
    slab = own_ref.shape[0]
    half = second_ref.shape[0]
    for ref, start in ((own_ref, numbers[0]), (first_ref, numbers[1])):
        for u in range(2):
            part = anomaly_ref[:, pl.ds(pl.multiple_of(start + u * half, half), half)]
            ref[u * half : (u + 1) * half, :] = part.T
    part = anomaly_ref[:, pl.ds(pl.multiple_of(numbers[2], half), half)]
    second_ref[...] = part.T
    row = mean_ref[:, pl.ds(pl.multiple_of(numbers[0], half), slab)]
    column_ref[...] = jnp.broadcast_to(row, (8, slab)).T


def column_bases(points):
    return [min(max(b - 1 + v, 0), points - 2) for b in range(points) for v in range(2)]


def blended_parts(segments, transforms, points):
    half = segments[0][0].shape[0]
    bases = column_bases(points)
    size = half // len(bases)
    spans = []
    for v in range(points - 1):
        hits = [g for g, b in enumerate(bases) if b == v]
        spans.append((hits[0] * size, (hits[-1] + 1) * size))
    sums = [[None] * (points - 1) for _ in segments]
    for q in range(points):
        where = [v for v in (q - 1, q) if 0 <= v <= points - 2]
        rows = [
            (n, v, cells[spans[v][0] : spans[v][1], :])
            for n, (cells, _) in enumerate(segments)
            for v in where
        ]
        spread = dot_nn(jnp.concatenate([r[2] for r in rows], axis=0), transforms(q))
        at = 0
        for n, v, cells in rows:
            low, high = spans[v]
            term = segments[n][1][low:high, q : q + 1] * spread[at : at + high - low]
            sums[n][v] = term if sums[n][v] is None else sums[n][v] + term
            at += high - low
    return [jnp.concatenate(parts, axis=0) for parts in sums]


def transform_kernel(
    offsets, numbers, *refs
):
    count = len(offsets)
    pieces = refs[:count]
    (
        table_ref,
        products_ref,
        forcing_ref,
        first_ref,
        second_ref,
        first_mix,
        second_mix,
        transform_ref,
        to_first_ref,
        to_second_ref,
        margin_ref,
    ) = refs[count:]
    rows = pieces[0].shape[1]
    members = rows * count
    points = products_ref.shape[0]
    for offset, piece in zip(offsets, pieces):
        for j in range(2):
            start = pl.multiple_of((numbers[0] ^ offset ^ numbers[1 + j]) * rows, rows)
            margin_ref[pl.ds(start, rows), j * LANES : (j + 1) * LANES] = piece[j]
    values = margin_ref[...].astype(f32)
    mean = jnp.sum(values, axis=0, keepdims=True) / members
    pert = (values - mean).astype(bf16)
    pert_wide = pert.astype(f32)
    tiles = jnp.concatenate([table_ref[0], table_ref[1]], axis=1)
    departure = tiles[points:, :] - tiles[:points, :] * mean
    first, second = split(jnp.concatenate([departure, departure], axis=0))
    forcing = forcing_ref[...] + dot_nt(first, pert) + dot_nt(second, pert)
    forcing = forcing.T
    identity = lax.broadcasted_iota(jnp.int32, (members, members), 0) == lax.broadcasted_iota(
        jnp.int32, (members, members), 1
    )

    def plus(scalar, matrix):
        return matrix + jnp.where(identity, scalar, 0.0)

    def left(x):
        high, low = split(x)
        return jnp.concatenate([high, high, low], axis=1)

    def right(x):
        high, low = split(x)
        return jnp.concatenate([high, low, high], axis=0)

    span = range(points)
    matrix, scale = [], []
    for a in span:
        weighted = (pert_wide * tiles[a : a + 1, :]).astype(bf16)
        full = plus(members - 1.0, products_ref[a] + dot_nt(weighted, pert))
        square = jnp.sum(jnp.sum(full * full, axis=0, keepdims=True), axis=1, keepdims=True)
        frobenius = jnp.sqrt(square)
        matrix.append(full / frobenius)
        scale.append(1.0 / jnp.sqrt(frobenius))
    matrix_left = [left(x) for x in matrix]
    squared = [dot_nn(matrix_left[a], right(matrix[a])) for a in span]
    root = [
        plus(2.25, -2.4375 * matrix[a])
        + dot_nn(
            left(squared[a]),
            right(plus(1.6875, 0.0625 * squared[a] - 0.5625 * matrix[a])),
        )
        for a in span
    ]
    current = [dot_nn(matrix_left[a], right(root[a])) for a in span]
    root_left = [left(x) for x in root]
    middle = [plus(1.5, -0.5 * dot_nn(root_left[a], right(current[a]))) for a in span]
    middle_right = [right(x) for x in middle]
    current = [dot_nn(left(current[a]), middle_right[a]) for a in span]
    root = [dot_nn(root_left[a], middle_right[a]) for a in span]
    root_left = [left(x) for x in root]
    middle = [plus(1.5, -0.5 * dot_nn(root_left[a], right(current[a]))) for a in span]
    root = [dot_nn(root_left[a], right(middle[a])) for a in span]
    for a in span:
        inverse = root[a] * scale[a]
        inner = jnp.sum(inverse * forcing[:, a : a + 1], axis=0, keepdims=True)
        mean_weights = jnp.sum(inverse * inner, axis=1, keepdims=True)
        transform_ref[a] = (mean_weights + jnp.sqrt(members - 1.0) * inverse).astype(bf16)
    half = second_ref.shape[0]
    segments = [
        (first_ref[0:half, :], first_mix[0:half, :]),
        (first_ref[half:, :], first_mix[half:, :]),
        (second_ref[...], second_mix[...]),
    ]
    parts = blended_parts(segments, lambda q: transform_ref[q], points)
    to_first_ref[0:half, :] = parts[0].astype(bf16)
    to_first_ref[half:, :] = parts[1].astype(bf16)
    to_second_ref[...] = parts[2].astype(bf16)


def own_kernel(transform_ref, own_ref, own_mix, column_ref, out_ref):
    points = transform_ref.shape[0]
    half = own_ref.shape[0] // 2
    segments = [
        (own_ref[0:half, :], own_mix[0:half, :]),
        (own_ref[half:, :], own_mix[half:, :]),
    ]
    parts = blended_parts(segments, lambda q: transform_ref[q], points)
    for u in range(2):
        rows = slice(u * half, (u + 1) * half)
        out_ref[rows, :] = parts[u] + column_ref[rows, 0:1]


def mixing_columns(blending, band, row, row_count, points, valid):
    slab = blending.shape[1]
    half = slab // 2
    size = slab // (4 * points)
    mixing = blending / jnp.sum(blending, axis=0, keepdims=True)
    cell = jnp.arange(slab, dtype=jnp.int32)
    step = row - jnp.clip(band - 1 + cell // half, 0, row_count - 2)
    usable = valid & (step >= 0) & (step <= 1)
    group = cell % half // size
    base = jnp.clip(group // 2 - 1 + group % 2, 0, points - 2)
    pair = jnp.where(step == 0, mixing[0:2], mixing[2:4])
    pair = jnp.where(usable, pair, 0.0)
    rows = [
        jnp.where(base == q, pair[0], jnp.where(base == q - 1, pair[1], 0.0))
        for q in range(points)
    ]
    return jnp.stack(rows, axis=0).T


def per_device(ensemble, reports, report_count, report_cell, report_weight, blending):
    local_members, cell_count = ensemble.shape
    regions = lax.axis_size("region")
    groups = lax.axis_size("member")
    members = local_members * groups
    points = report_weight.shape[1]
    slots = reports.shape[1]
    slab = cell_count // groups
    half = slab // 2
    region = lax.axis_index("region")
    member = lax.axis_index("member")
    devices = regions * groups
    region_bits = regions.bit_length() - 1
    member_bits = groups.bit_length() - 1

    def swap(x, mask):
        return lax.ppermute(x, AXES, [(i, i ^ mask) for i in range(devices)])

    def across(i):
        position = i % groups
        other = (position + 1 if position % 2 else position - 1) % groups
        return i - position + other

    def cross(x):
        return lax.ppermute(x, AXES, [(i, across(i)) for i in range(devices)])

    member_masks = [(1 << k) | 1 for k in range(member_bits - 1, 0, -1)] + [1]

    border = ensemble[:, :MARGIN][None]
    for k in range(region_bits - 1, -1, -1):
        border = jnp.concatenate([border, swap(border, (groups << k) | 1)], axis=0)

    pieces, offsets = [ensemble], [0]
    for mask in member_masks:
        pieces = pieces + [swap(x, mask) for x in pieces]
        offsets = offsets + [offset ^ mask for offset in offsets]
    partner_blending = swap(blending, 1)
    other_blending = cross(blending)

    holder = report_cell[0] // cell_count
    outside = holder != region
    first_source = jnp.min(jnp.where(outside, holder, regions))
    second_source = jnp.max(jnp.where(outside, holder, -1))
    first_source = jnp.where(first_source == regions, region, first_source)
    second_source = jnp.where(second_source < 0, region, second_source)

    def place(source):
        distance = region ^ source
        index = jnp.int32(0)
        flips = jnp.int32(0)
        for k in range(region_bits):
            bit = (distance >> k) & 1
            index = index + (bit << (region_bits - 1 - k))
            flips = flips ^ bit
        return index, flips

    first_place, first_flip = place(first_source)
    second_place, second_flip = place(second_source)
    picked = jnp.concatenate(
        [
            lax.dynamic_slice_in_dim(border, first_place, 1, axis=0),
            lax.dynamic_slice_in_dim(border, second_place, 1, axis=0),
        ],
        axis=0,
    )
    margin_pieces = [picked]
    for mask in member_masks:
        if len(margin_pieces) == 1:
            margin_pieces = margin_pieces + [swap(margin_pieces[0], mask)]
        else:
            joined = swap(jnp.concatenate(margin_pieces, axis=0), mask)
            margin_pieces = margin_pieces + [
                joined[2 * i : 2 * i + 2] for i in range(len(margin_pieces))
            ]

    table_rows = cell_count // LANES + 2
    numbers = jnp.stack(
        [region, first_source, second_source, report_count[0], jnp.int32(cell_count)]
    )
    (table,) = call(
        functools.partial(weights_kernel, table_rows),
        [((table_rows, 2 * points, LANES), f32)],
        1,
        (numbers, report_cell, report_weight, reports),
        2 * 2 * table_rows * 2 * points * slots * LANES,
        200000,
    )

    anomaly, mean = call(
        functools.partial(anomaly_kernel, tuple(offsets)),
        [((members, cell_count), bf16), ((1, cell_count), f32)],
        1,
        (member[None], *pieces),
        4 * members * cell_count,
        4 * members * cell_count,
    )
    products, forcing = call(
        products_kernel,
        [((points, members, members), f32), ((2 * points, members), f32)],
        0,
        (anomaly, mean, table),
        2 * points * members * members * cell_count,
        2 * members * cell_count + 4 * points * members * members,
    )

    odd = member % 2
    partner = member ^ 1
    other = (member - 1 + 2 * odd) % groups
    inner = (member > 0) & (member < groups - 1)
    other_half = other * slab + (1 - odd) * half
    own_mix = mixing_columns(blending, member, member, groups, points, True)
    first_mix = mixing_columns(partner_blending, partner, member, groups, points, True)
    other_mix = mixing_columns(other_blending, other, member, groups, points, inner)
    second_mix = lax.dynamic_slice_in_dim(other_mix, (1 - odd) * half, half, axis=0)
    own_cells, first_cells, second_cells, column = call(
        transpose_kernel,
        [
            ((slab, members), bf16),
            ((slab, members), bf16),
            ((half, members), bf16),
            ((slab, 8), f32),
        ],
        1,
        (jnp.stack([member * slab, partner * slab, other_half]), anomaly, mean),
        3 * slab * members,
        8 * slab * members,
    )

    transform, to_first, to_second = call(
        functools.partial(transform_kernel, tuple(offsets)),
        [
            ((points, members, members), bf16),
            ((slab, members), bf16),
            ((half, members), bf16),
        ],
        1,
        (
            jnp.stack([member, first_flip, second_flip]),
            *margin_pieces,
            table[table_rows - 2 :],
            products,
            forcing,
            first_cells,
            second_cells,
            first_mix,
            second_mix,
        ),
        2 * 26 * points * members**3,
        4 * points * members * members * 2,
        scratch=[pltpu.VMEM((members, 2 * LANES), bf16)],
    )
    from_other = cross(to_second)
    from_partner = swap(to_first, 1)
    (own,) = call(
        own_kernel,
        [((slab, members), f32)],
        0,
        (transform, own_cells, own_mix, column),
        4 * slab * members * members,
        8 * slab * members,
    )
    upper = jnp.where(odd == 0, from_other.astype(f32), 0.0)
    lower = jnp.where(odd == 1, from_other.astype(f32), 0.0)
    total = own + from_partner.astype(f32) + jnp.concatenate([upper, lower], axis=0)
    return total.astype(bf16)


def solution(mesh):
    return jax.shard_map(
        per_device,
        mesh=mesh,
        in_specs=(
            P("member", "region"),
            P("region", None),
            P("region"),
            P("region", None),
            P("region", "member", None),
            P(None, ("region", "member")),
        ),
        out_specs=P(("region", "member"), None),
        check_vma=False,
    )
```

time: 105 us -> 55.7 us (0.53)
  blocking collectives: 45.6 us -> 0 us
  Pallas kernels: 0 us -> 19.9 us
  matrix products: 19.8 us -> 0 us
  local copies, waits for them, and re-layouts: 19.4 us -> 9.65 us
  starting transfers between devices: 7.71 us -> 13.2 us
  between operations: 1.12 us -> 3.3 us
  waiting for transfers between devices: 7.42 us -> 5.93 us
    all_gather x2 -> x0, blocking collectives: 40 us -> none  [the longest x1 32.6 us: per_device(): pieces = lax.all_gather(border, 'region', axis=1, tiled=True)]
    pallas_call x0 -> x6, Pallas kernels: none -> 19.9 us  [call(): pl.pallas_call(kernel, out_shape=[jax.ShapeDtypeStruct(s, d) for s, d in...]
    dot_general x19 -> x0, matrix products: 19.8 us -> none  [the longest x4 4.92 us: make_transform(): jnp.einsum('aij,ajk->aik', root_iter, current, precision=highest)]
    gather x8 -> x0, local copies, waits for them, and re-layouts: 14.7 us -> none  [the longest x4 8.04 us: per_device(): chosen = jnp.take(stacked, chosen_index, axis=0)]
    ppermute x2 -> x12, starting transfers between devices: 3.57 us -> 13.2 us  [the longest x10 11.6 us: swap(): return lax.ppermute(x, AXES, [(i, i ^ mask) for i in range(devices)])]
    all_to_all x1 -> x0, waiting for transfers between devices: 7.41 us -> none  [per_device(): lax.all_to_all(ensemble, 'member', split_axis=1, concat_axis=0, tiled=True)]
    ppermute x2 -> x12, waiting for transfers between devices: 0.01 us -> 5.93 us  [the longest x10 5.41 us: swap(): return lax.ppermute(x, AXES, [(i, i ^ mask) for i in range(devices)])]
    psum x1 -> x0, blocking collectives: 5.67 us -> none  [per_device(): report_mean = lax.psum(jnp.sum(at_reports, axis=0), 'member') / members]
  transfers between devices with their start and end apart: 3 -> 12, of which waited for: 1 -> 4; matrix products, arithmetic and copies ran while one was open for 2% -> 15% of each run, Pallas kernels for 0% -> 8%
where the time goes in v1:
time: 55.7 us; the launch traced here: 55.2 us
  Pallas kernels  19.9 us (36%)
  starting transfers between devices  13.2 us (24%)
  local copies, waits for them, and re-layouts  9.65 us (17%)
  waiting for transfers between devices  5.93 us (11%)
  between operations  3.3 us (6%)
  other arithmetic  3.15 us (6%)
    pallas_call x6, Pallas kernels, call(): pl.pallas_call(kernel, out_shape=[jax.ShapeDtypeStruct(s, d) for s, d in...  19.9 us
    ppermute x10, starting transfers between devices, swap(): return lax.ppermute(x, AXES, [(i, i ^ mask) for i in range(devices)])  11.6 us
    ppermute x10, waiting for transfers between devices, swap(): return lax.ppermute(x, AXES, [(i, i ^ mask) for i in range(devices)])  5.41 us
    unnamed x17, local copies, waits for them, and re-layouts  4.59 us
    another operation x2, local copies, waits for them, and re-layouts, mixing_columns(): return jnp.stack(rows, axis=0).T  1.74 us
    ppermute x2, starting transfers between devices, cross(): return lax.ppermute(x, AXES, [(i, across(i)) for i in range(devices)])  1.62 us
    slice x1, local copies, waits for them, and re-layouts, per_device(): table[table_rows - 2:]  1.29 us
  transfers between devices with their start and end apart: 12, of which 4 were waited for; matrix products, arithmetic and copies ran while one was open for 15% of the time, Pallas kernels for 8%

profile of v1, /device:TPU:0, one launch (start us, length us, event | category | flops | bytes accessed | tf_op | source)
XLA Modules:
  0.0 55.2 jit_solution(17332736718342686338)
XLA Ops:
  0.0 2.4 %collective-permute-start.5 = (bf16[64,2048]{1,0:T(8,128)(2,1)}, bf16[64,2048]{1,0:T(8,128)(2,1)S(1)}, u32[]{:S(2)}, u32[]{:S(2)}) collective-permute-start(bf16[64,2048]{1,0:T(8,128)(2,1)} %refs_0_.1), channel_id=1, source_target_pairs={{0,3},{1,2},{2,1},{3,0},{4,7},{5,6},{6,5},{7,4},{8,11},{9,10},{10,... | collective-permute-start | bytes 786440 | tf_op jit(solution)/shard_map/ppermute | solution.py:300
  2.4 0.7 %collective-permute-start.6 = (bf16[64,2048]{1,0:T(8,128)(2,1)}, bf16[64,2048]{1,0:T(8,128)(2,1)S(1)}, u32[]{:S(2)}, u32[]{:S(2)}) collective-permute-start(bf16[64,2048]{1,0:T(8,128)(2,1)} %refs_0_.1), channel_id=1, source_target_pairs={{0,1},{1,0},{2,3},{3,2},{4,5},{5,4},{6,7},{7,6},{8,9},{9,8},{10,11... | collective-permute-start | bytes 786440 | tf_op jit(solution)/shard_map/ppermute | solution.py:300
  3.1 0.0 collective-permute-start.8
  3.1 0.1 collective-permute-start.9
  3.2 0.7 %slice_bitcast_fusion = bf16[1,64,128]{2,1,0:T(8,128)(2,1)S(1)} fusion(bf16[64,2048]{1,0:T(8,128)(2,1)} %refs_0_.1), kind=kLoop, calls=%fused_computation.9 | loop fusion | bytes 32768 | tf_op jit(solution)/shard_map/broadcast_in_dim | solution.py:312
  3.9 2.8 %collective-permute-start = (bf16[1,64,128]{2,1,0:T(8,128)(2,1)S(1)}, bf16[1,64,128]{2,1,0:T(8,128)(2,1)S(1)}, u32[]{:S(2)}, u32[]{:S(2)}) collective-permute-start(bf16[1,64,128]{2,1,0:T(8,128)(2,1)S(1)} %slice_bitcast_fusion), channel_id=1, source_target_pairs={{0,17},{1,16},{2,19},{3,18},{4,21},{5,20},{6,23},{7,22},{8,25},{9,... | collective-permute-start | bytes 49160 | tf_op jit(solution)/shard_map/ppermute | solution.py:300
  6.7 0.0 copy-start.7
  6.7 0.7 %copy-done.7 = s32[1,1024]{1,0:T(1,128)S(1)} copy-done((s32[1,1024]{1,0:T(1,128)S(1)}, s32[1,1024]{1,0:T(1,128)}, u32[]{:S(2)}) %copy-start.7) | copy-done | bytes 4120
  7.3 0.7 %fusion.5 = (s32[]{:T(128)}, s32[]{:T(128)}) fusion(s32[]{:T(128)} %axis_index.25, s32[1024]{0:T(1024)S(1)} %bitcast.18), kind=kLoop, calls=%fused_computation.36 | loop fusion | flops 20478 | bytes 4108 | tf_op jit(solution)/shard_map/reduce_min | solution.py:325
  10.5 0.0 copy-start.5
  10.5 0.7 %copy-done.5 = f32[4,512]{1,0:T(4,128)S(1)} copy-done((f32[4,512]{1,0:T(4,128)S(1)}, f32[4,512]{1,0:T(4,128)}, u32[]{:S(2)}) %copy-start.5) | copy-done | bytes 8216
  11.3 0.6 %pad_add_fusion.numbers = s32[3]{0:T(128)} fusion(s32[1]{0:T(128)} %bitcast.3, s32[1]{0:T(128)} %bitcast.2, s32[1]{0:T(128)} %bitcast.numbers), kind=kLoop, calls=%fused_computation.92 | loop fusion | flops 6 | bytes 24 | tf_op jit(solution)/shard_map/stack | solution.py:421
  11.9 0.6 %pad_add_fusion.1.numbers = s32[3]{0:T(128)} fusion(s32[1]{0:T(128)} %bitcast.10, s32[1]{0:T(128)} %bitcast.9, s32[1]{0:T(128)} %bitcast.8), kind=kLoop, calls=%fused_computation.93 | loop fusion | flops 6 | bytes 24 | tf_op jit(solution)/shard_map/stack | solution.py:407
  13.2 0.7 %stack.64.numbers = s32[5]{0:T(128)} concatenate(s32[1]{0:T(128)} %bitcast.5, s32[1]{0:T(128)} %bitcast.6, s32[1]{0:T(128)} %bitcast.7, s32[1]{0:T(128)S(6)} %copy.25, s32[1]{0:T(128)} %constant.137.clone.1), dimensions={0} | concatenate | bytes 40 | tf_op jit(solution)/shard_map/stack | solution.py:360
  13.8 1.9 %shard_map.64.table_ref = f32[18,8,128]{2,1,0:T(8,128)} custom-call(s32[5]{0:T(128)} %stack.64.numbers, s32[1,1024]{1,0:T(1,128)} %cell_ref.1, f32[1,4,1024]{2,1,0:T(4,128)} %weight_ref.1, f32[1,1024]{1,0:T(1,128)} %report_ref.1), custom_call_target="tpu_custom_call" | custom-call | flops 75497472 | bytes 200000 | tf_op jit(solution)/shard_map/pallas_call | solution.py:35
  15.8 1.3 %slice.84.refs_4_ = f32[2,8,128]{2,1,0:T(8,128)} slice(f32[18,8,128]{2,1,0:T(8,128)} %shard_map.64.table_ref), slice={[16:18], [0:8], [0:128]} | slice | bytes 16384 | tf_op jit(solution)/shard_map/slice | solution.py:423
  17.0 0.0 collective-permute-done.9
  17.1 0.0 collective-permute-done.8
  17.2 0.0 collective-permute-done
  17.2 1.8 %collective-permute-start.1 = (bf16[2,64,128]{2,1,0:T(8,128)(2,1)S(1)}, bf16[2,64,128]{2,1,0:T(8,128)(2,1)S(1)}, u32[]{:S(2)}, u32[]{:S(2)}) collective-permute-start(bf16[2,64,128]{2,1,0:T(8,128)(2,1)S(1)} %pad_maximum_fusion.3), channel_id=1, source_target_pairs={{0,9},{1,8},{2,11},{3,10},{4,13},{5,12},{6,15},{7,14},{8,1},{9,0},... | collective-permute-start | bytes 98312 | tf_op jit(solution)/shard_map/ppermute | solution.py:300
  19.0 1.6 %collective-permute-done.1 = bf16[2,64,128]{2,1,0:T(8,128)(2,1)S(1)} collective-permute-done((bf16[2,64,128]{2,1,0:T(8,128)(2,1)S(1)}, bf16[2,64,128]{2,1,0:T(8,128)(2,1)S(1)}, u32[]{:S(2)}, u32[]{:S(2)}) %collective-permute-start.1) | collective-permute-done | bytes 32800 | tf_op jit(solution)/shard_map/ppermute | solution.py:300
  20.6 1.7 %collective-permute-start.2 = (bf16[4,64,128]{2,1,0:T(8,128)(2,1)S(1)}, bf16[4,64,128]{2,1,0:T(8,128)(2,1)S(1)}, u32[]{:S(2)}, u32[]{:S(2)}) collective-permute-start(bf16[4,64,128]{2,1,0:T(8,128)(2,1)S(1)} %pad_maximum_fusion.1), channel_id=1, source_target_pairs={{0,5},{1,4},{2,7},{3,6},{4,1},{5,0},{6,3},{7,2},{8,13},{9,12},{10,... | collective-permute-start | bytes 196616 | tf_op jit(solution)/shard_map/ppermute | solution.py:300
  22.4 2.0 %collective-permute-done.2 = bf16[4,64,128]{2,1,0:T(8,128)(2,1)S(1)} collective-permute-done((bf16[4,64,128]{2,1,0:T(8,128)(2,1)S(1)}, bf16[4,64,128]{2,1,0:T(8,128)(2,1)S(1)}, u32[]{:S(2)}, u32[]{:S(2)}) %collective-permute-start.2) | collective-permute-done | bytes 65568 | tf_op jit(solution)/shard_map/ppermute | solution.py:300
  24.5 0.0 copy-start.4
  24.5 1.7 %collective-permute-start.3 = (bf16[2,64,128]{2,1,0:T(8,128)(2,1)S(1)}, bf16[2,64,128]{2,1,0:T(8,128)(2,1)S(1)}, u32[]{:S(2)}, u32[]{:S(2)}) collective-permute-start(bf16[2,64,128]{2,1,0:T(8,128)(2,1)S(1)} %pad_maximum_fusion.4.refs_0_), channel_id=1, source_target_pairs={{0,3},{1,2},{2,1},{3,0},{4,7},{5,6},{6,5},{7,4},{8,11},{9,10},{10,... | collective-permute-start | bytes 98312 | tf_op jit(solution)/shard_map/ppermute | solution.py:300
  26.2 1.7 %collective-permute-done.3.refs_1_ = bf16[2,64,128]{2,1,0:T(8,128)(2,1)S(1)} collective-permute-done((bf16[2,64,128]{2,1,0:T(8,128)(2,1)S(1)}, bf16[2,64,128]{2,1,0:T(8,128)(2,1)S(1)}, u32[]{:S(2)}, u32[]{:S(2)}) %collective-permute-start.3) | collective-permute-done | bytes 32800 | tf_op jit(solution)/shard_map/ppermute | solution.py:300
  27.9 0.0 copy-start.6
  27.9 0.0 copy-done.4
  27.9 0.6 %copy-done.6 = bf16[2,64,128]{2,1,0:T(8,128)(2,1)} copy-done((bf16[2,64,128]{2,1,0:T(8,128)(2,1)}, bf16[2,64,128]{2,1,0:T(8,128)(2,1)S(1)}, u32[]{:S(2)}) %copy-start.6) | copy-done | bytes 32792
  28.5 0.5 collective-permute-start.4
  29.0 0.0 collective-permute-done.5.refs_1_
  29.0 0.0 copy-start.1
  29.0 0.1 collective-permute-start.7
  29.1 0.1 fusion.4
  29.1 0.9 %copy.21 = f32[4,512]{0,1:T(8,128)} copy(f32[4,512]{1,0:T(4,128)S(1)} %pad_maximum_fusion.5) | data formatting | bytes 16384 | tf_op jit(solution)/shard_map/stack | solution.py:281
  30.0 0.8 %copy.24 = f32[4,256]{0,1:T(8,128)} copy(f32[4,256]{1,0:T(4,128)S(1)} %fusion.4) | data formatting | bytes 8192
  30.8 0.0 collective-permute-done.4
  30.8 0.6 %fusion.28 = (bf16[2,64,128]{2,1,0:T(8,128)(2,1)}, bf16[2,64,128]{2,1,0:T(8,128)(2,1)}) fusion(bf16[4,64,128]{2,1,0:T(8,128)(2,1)S(1)} %collective-permute-done.4), kind=kLoop, calls=%fused_computation.94 | loop fusion | bytes 131072 | tf_op jit(solution)/shard_map/slice | solution.py:356
  31.5 0.0 copy-done.1
  31.5 0.0 collective-permute-done.6.refs_2_
  31.5 0.0 copy-start.2
  31.5 0.0 collective-permute-done.7.refs_3_
  31.5 0.7 %copy-done.2 = bf16[64,2048]{1,0:T(8,128)(2,1)} copy-done((bf16[64,2048]{1,0:T(8,128)(2,1)}, bf16[64,2048]{1,0:T(8,128)(2,1)S(1)}, u32[]{:S(2)}) %copy-start.2) | copy-done | bytes 262168
  32.2 0.0 copy-start.3
  32.2 0.7 %copy-done.3 = bf16[64,2048]{1,0:T(8,128)(2,1)} copy-done((bf16[64,2048]{1,0:T(8,128)(2,1)}, bf16[64,2048]{1,0:T(8,128)(2,1)S(1)}, u32[]{:S(2)}) %copy-start.3) | copy-done | bytes 262168
  32.9 2.6 %shard_map.65 = (bf16[256,2048]{1,0:T(8,128)(2,1)}, f32[1,2048]{1,0:T(1,128)}) custom-call(s32[1]{0:T(128)} %bitcast.numbers, bf16[64,2048]{1,0:T(8,128)(2,1)} %refs_0_.1, bf16[64,2048]{1,0:T(8,128)(2,1)} %copy-done.1, bf16[64,2048]{1,0:T(8,128)(2,1)} %copy-done.2, bf16[64,2048]{1,0:T(8,128)(2,1)} %copy-done.3), custom_call_target="tpu_custom_call" | custom-call | flops 2097152 | bytes 2097152 | tf_op jit(solution)/shard_map/pallas_call | solution.py:35
  35.4 4.0 %shard_map.66 = (f32[4,256,256]{2,1,0:T(8,128)}, f32[8,256]{1,0:T(8,128)}) custom-call(bf16[256,2048]{1,0:T(8,128)(2,1)} %get-tuple-element.16.anomaly_ref, f32[1,2048]{1,0:T(1,128)} %get-tuple-element.17.mean_ref, f32[18,8,128]{2,1,0:T(8,128)} %shard_map.64.table_ref), custom_call_target="tpu_custom_call" | custom-call | flops 1073741824 | bytes 2097152 | tf_op jit(solution)/shard_map/pallas_call | solution.py:35
  39.5 2.3 %shard_map.67 = (bf16[512,256]{1,0:T(8,128)(2,1)}, bf16[512,256]{1,0:T(8,128)(2,1)}, bf16[256,256]{1,0:T(8,128)(2,1)}, f32[512,8]{1,0:T(8,128)}) custom-call(s32[3]{0:T(128)} %pad_add_fusion.1.numbers, bf16[256,2048]{1,0:T(8,128)(2,1)} %get-tuple-element.16.anomaly_ref, f32[1,2048]{1,0:T(1,128)} %get-tuple-element.17.mean_ref), custom_call_target="tpu_custom_call" | custom-call | flops 393216 | bytes 1048576 | tf_op jit(solution)/shard_map/pallas_call | solution.py:35
  41.7 6.7 %shard_map.68 = (bf16[4,256,256]{2,1,0:T(8,128)(2,1)}, bf16[512,256]{1,0:T(8,128)(2,1)}, bf16[256,256]{1,0:T(8,128)(2,1)}) custom-call(s32[3]{0:T(128)} %pad_add_fusion.numbers, bf16[2,64,128]{2,1,0:T(8,128)(2,1)} %copy-done.4, bf16[2,64,128]{2,1,0:T(8,128)(2,1)} %copy-done.6, bf16[2,64,128]{2,1,0:T(8,128)(2,1)} %get-tuple-element.34.refs_2_, ...), custom_call_target="tpu_custom_call" | custom-call | flops 3489660928 | bytes 2097152 | tf_op jit(solution)/shard_map/pallas_call | solution.py:35
  48.5 1.5 %collective-permute-start.11 = (bf16[256,256]{1,0:T(8,128)(2,1)}, bf16[256,256]{1,0:T(8,128)(2,1)S(1)}, u32[]{:S(2)}, u32[]{:S(2)}) collective-permute-start(bf16[256,256]{1,0:T(8,128)(2,1)} %get-tuple-element.26), channel_id=1, source_target_pairs={{0,3},{1,2},{2,1},{3,0},{4,7},{5,6},{6,5},{7,4},{8,11},{9,10},{10,... | collective-permute-start | bytes 393224 | tf_op jit(solution)/shard_map/ppermute | solution.py:308
  50.0 0.1 collective-permute-start.10
  50.1 0.9 %copy.23 = f32[4,512]{0,1:T(8,128)} copy(f32[4,512]{1,0:T(4,128)S(1)} %pad_maximum_fusion.6) | data formatting | bytes 16384 | tf_op jit(solution)/shard_map/stack | solution.py:281
  51.0 2.4 %shard_map.69 = f32[512,256]{1,0:T(8,128)} custom-call(bf16[4,256,256]{2,1,0:T(8,128)(2,1)} %get-tuple-element.22.transform_ref, bf16[512,256]{1,0:T(8,128)(2,1)} %get-tuple-element.23.own_ref, f32[512,4]{1,0:T(8,128)} %bitcast.15, f32[512,8]{1,0:T(8,128)} %get-tuple-element.24.column_ref), custom_call_target="tpu_custom_call" | custom-call | flops 134217728 | bytes 1048576 | tf_op jit(solution)/shard_map/pallas_call | solution.py:35
  53.3 0.0 copy-start
  53.3 0.5 collective-permute-done.11
  53.9 0.0 collective-permute-done.10
  53.9 0.5 copy-done
  54.4 0.8 %fusion = bf16[512,256]{1,0:T(8,128)(2,1)} fusion(f32[256,256]{1,0:T(8,128)S(1)} %get-tuple-element.30, f32[256,256]{1,0:T(8,128)S(1)} %get-tuple-element.29, f32[512,256]{1,0:T(8,128)S(1)} %copy-done, bf16[512,256]{1,0:T(8,128)(2,1)S(1)} %collective-permute-done.10), kind=kLoop, calls=%fused_computation.1 | loop fusion | flops 655360 | bytes 1572864 | tf_op jit(solution)/shard_map/convert_element_type | solution.py:448
  (25 shorter events, 0.4 us)
Async XLA Ops:
  0.0 29.0 %collective-permute-start.5 = (bf16[64,2048]{1,0:T(8,128)(2,1)}, bf16[64,2048]{1,0:T(8,128)(2,1)S(1)}, u32[]{:S(2)}, u32[]{:S(2)}) collective-permute-start(bf16[64,2048]{1,0:T(8,128)(2,1)} %refs_0_.1), channel_id=1, source_target_pairs={{0,3},{1,2},{2,1},{3,0},{4,7},{5,6},{6,5},{7,4},{8,11},{9,10},{10,... | collective-permute-start | bytes 786440 | tf_op jit(solution)/shard_map/ppermute | solution.py:300
  2.4 29.1 %collective-permute-start.6 = (bf16[64,2048]{1,0:T(8,128)(2,1)}, bf16[64,2048]{1,0:T(8,128)(2,1)S(1)}, u32[]{:S(2)}, u32[]{:S(2)}) collective-permute-start(bf16[64,2048]{1,0:T(8,128)(2,1)} %refs_0_.1), channel_id=1, source_target_pairs={{0,1},{1,0},{2,3},{3,2},{4,5},{5,4},{6,7},{7,6},{8,9},{9,8},{10,11... | collective-permute-start | bytes 786440 | tf_op jit(solution)/shard_map/ppermute | solution.py:300
  3.1 14.1 %collective-permute-start.8 = (f32[4,512]{1,0:T(4,128)}, f32[4,512]{1,0:T(4,128)S(1)}, u32[]{:S(2)}, u32[]{:S(2)}) collective-permute-start(f32[4,512]{1,0:T(4,128)} %param.11), channel_id=1, source_target_pairs={{0,1},{1,0},{2,3},{3,2},{4,5},{5,4},{6,7},{7,6},{8,9},{9,8},{10,11... | collective-permute-start | bytes 24584 | tf_op jit(solution)/shard_map/ppermute | solution.py:300
  3.1 14.0 %collective-permute-start.9 = (f32[4,512]{1,0:T(4,128)}, f32[4,512]{1,0:T(4,128)S(1)}, u32[]{:S(2)}, u32[]{:S(2)}) collective-permute-start(f32[4,512]{1,0:T(4,128)} %param.11), channel_id=1, source_target_pairs={{0,3},{1,2},{2,1},{3,0},{4,7},{5,6},{6,5},{7,4},{8,11},{9,10},{10,... | collective-permute-start | bytes 24584 | tf_op jit(solution)/shard_map/ppermute | solution.py:308
  3.9 13.3 %collective-permute-start = (bf16[1,64,128]{2,1,0:T(8,128)(2,1)S(1)}, bf16[1,64,128]{2,1,0:T(8,128)(2,1)S(1)}, u32[]{:S(2)}, u32[]{:S(2)}) collective-permute-start(bf16[1,64,128]{2,1,0:T(8,128)(2,1)S(1)} %slice_bitcast_fusion), channel_id=1, source_target_pairs={{0,17},{1,16},{2,19},{3,18},{4,21},{5,20},{6,23},{7,22},{8,25},{9,... | collective-permute-start | bytes 49160 | tf_op jit(solution)/shard_map/ppermute | solution.py:300
  6.7 0.7 %copy-start.7 = (s32[1,1024]{1,0:T(1,128)S(1)}, s32[1,1024]{1,0:T(1,128)}, u32[]{:S(2)}) copy-start(s32[1,1024]{1,0:T(1,128)} %cell_ref.1) | copy-start | bytes 12292
  10.5 0.7 %copy-start.5 = (f32[4,512]{1,0:T(4,128)S(1)}, f32[4,512]{1,0:T(4,128)}, u32[]{:S(2)}) copy-start(f32[4,512]{1,0:T(4,128)} %param.11) | copy-start | bytes 24580
  17.2 3.4 %collective-permute-start.1 = (bf16[2,64,128]{2,1,0:T(8,128)(2,1)S(1)}, bf16[2,64,128]{2,1,0:T(8,128)(2,1)S(1)}, u32[]{:S(2)}, u32[]{:S(2)}) collective-permute-start(bf16[2,64,128]{2,1,0:T(8,128)(2,1)S(1)} %pad_maximum_fusion.3), channel_id=1, source_target_pairs={{0,9},{1,8},{2,11},{3,10},{4,13},{5,12},{6,15},{7,14},{8,1},{9,0},... | collective-permute-start | bytes 98312 | tf_op jit(solution)/shard_map/ppermute | solution.py:300
  20.6 3.8 %collective-permute-start.2 = (bf16[4,64,128]{2,1,0:T(8,128)(2,1)S(1)}, bf16[4,64,128]{2,1,0:T(8,128)(2,1)S(1)}, u32[]{:S(2)}, u32[]{:S(2)}) collective-permute-start(bf16[4,64,128]{2,1,0:T(8,128)(2,1)S(1)} %pad_maximum_fusion.1), channel_id=1, source_target_pairs={{0,5},{1,4},{2,7},{3,6},{4,1},{5,0},{6,3},{7,2},{8,13},{9,12},{10,... | collective-permute-start | bytes 196616 | tf_op jit(solution)/shard_map/ppermute | solution.py:300
  24.5 3.4 %copy-start.4 = (bf16[2,64,128]{2,1,0:T(8,128)(2,1)}, bf16[2,64,128]{2,1,0:T(8,128)(2,1)S(1)}, u32[]{:S(2)}) copy-start(bf16[2,64,128]{2,1,0:T(8,128)(2,1)S(1)} %pad_maximum_fusion.4.refs_0_) | copy-start | bytes 98308
  24.5 3.4 %collective-permute-start.3 = (bf16[2,64,128]{2,1,0:T(8,128)(2,1)S(1)}, bf16[2,64,128]{2,1,0:T(8,128)(2,1)S(1)}, u32[]{:S(2)}, u32[]{:S(2)}) collective-permute-start(bf16[2,64,128]{2,1,0:T(8,128)(2,1)S(1)} %pad_maximum_fusion.4.refs_0_), channel_id=1, source_target_pairs={{0,3},{1,2},{2,1},{3,0},{4,7},{5,6},{6,5},{7,4},{8,11},{9,10},{10,... | collective-permute-start | bytes 98312 | tf_op jit(solution)/shard_map/ppermute | solution.py:300
  27.9 0.6 %copy-start.6 = (bf16[2,64,128]{2,1,0:T(8,128)(2,1)}, bf16[2,64,128]{2,1,0:T(8,128)(2,1)S(1)}, u32[]{:S(2)}) copy-start(bf16[2,64,128]{2,1,0:T(8,128)(2,1)S(1)} %collective-permute-done.3.refs_1_) | copy-start | bytes 98308
  28.5 2.3 %collective-permute-start.4 = (bf16[4,64,128]{2,1,0:T(8,128)(2,1)S(1)}, bf16[4,64,128]{2,1,0:T(8,128)(2,1)S(1)}, u32[]{:S(2)}, u32[]{:S(2)}) collective-permute-start(bf16[4,64,128]{2,1,0:T(8,128)(2,1)S(1)} %pad_maximum_fusion.2), channel_id=1, source_target_pairs={{0,1},{1,0},{2,3},{3,2},{4,5},{5,4},{6,7},{7,6},{8,9},{9,8},{10,11... | collective-permute-start | bytes 196616 | tf_op jit(solution)/shard_map/ppermute | solution.py:300
  29.0 2.5 %copy-start.1 = (bf16[64,2048]{1,0:T(8,128)(2,1)}, bf16[64,2048]{1,0:T(8,128)(2,1)S(1)}, u32[]{:S(2)}) copy-start(bf16[64,2048]{1,0:T(8,128)(2,1)S(1)} %collective-permute-done.5.refs_1_) | copy-start | bytes 786436
  29.0 2.5 %collective-permute-start.7 = (bf16[64,2048]{1,0:T(8,128)(2,1)S(1)}, bf16[64,2048]{1,0:T(8,128)(2,1)S(1)}, u32[]{:S(2)}, u32[]{:S(2)}) collective-permute-start(bf16[64,2048]{1,0:T(8,128)(2,1)S(1)} %collective-permute-done.5.refs_1_), channel_id=1, source_target_pairs={{0,1},{1,0},{2,3},{3,2},{4,5},{5,4},{6,7},{7,6},{8,9},{9,8},{10,11... | collective-permute-start | bytes 786440 | tf_op jit(solution)/shard_map/ppermute | solution.py:300
  31.5 0.7 %copy-start.2 = (bf16[64,2048]{1,0:T(8,128)(2,1)}, bf16[64,2048]{1,0:T(8,128)(2,1)S(1)}, u32[]{:S(2)}) copy-start(bf16[64,2048]{1,0:T(8,128)(2,1)S(1)} %collective-permute-done.6.refs_2_) | copy-start | bytes 786436
  32.2 0.7 %copy-start.3 = (bf16[64,2048]{1,0:T(8,128)(2,1)}, bf16[64,2048]{1,0:T(8,128)(2,1)S(1)}, u32[]{:S(2)}) copy-start(bf16[64,2048]{1,0:T(8,128)(2,1)S(1)} %collective-permute-done.7.refs_3_) | copy-start | bytes 786436
  48.5 5.4 %collective-permute-start.11 = (bf16[256,256]{1,0:T(8,128)(2,1)}, bf16[256,256]{1,0:T(8,128)(2,1)S(1)}, u32[]{:S(2)}, u32[]{:S(2)}) collective-permute-start(bf16[256,256]{1,0:T(8,128)(2,1)} %get-tuple-element.26), channel_id=1, source_target_pairs={{0,3},{1,2},{2,1},{3,0},{4,7},{5,6},{6,5},{7,4},{8,11},{9,10},{10,... | collective-permute-start | bytes 393224 | tf_op jit(solution)/shard_map/ppermute | solution.py:308
  50.0 3.9 %collective-permute-start.10 = (bf16[512,256]{1,0:T(8,128)(2,1)}, bf16[512,256]{1,0:T(8,128)(2,1)S(1)}, u32[]{:S(2)}, u32[]{:S(2)}) collective-permute-start(bf16[512,256]{1,0:T(8,128)(2,1)} %get-tuple-element.25), channel_id=1, source_target_pairs={{0,1},{1,0},{2,3},{3,2},{4,5},{5,4},{6,7},{7,6},{8,9},{9,8},{10,11... | collective-permute-start | bytes 786440 | tf_op jit(solution)/shard_map/ppermute | solution.py:300
  53.3 1.0 %copy-start = (f32[512,256]{1,0:T(8,128)S(1)}, f32[512,256]{1,0:T(8,128)}, u32[]{:S(2)}) copy-start(f32[512,256]{1,0:T(8,128)} %shard_map.69) | copy-start | bytes 1572868

commit v2 on v1

v2 whole, which is shorter than its diff:
```python
import functools

import jax
import jax.numpy as jnp
from jax import lax
from jax.experimental import pallas as pl
from jax.experimental.pallas import tpu as pltpu
from jax.sharding import PartitionSpec as P

MARGIN = 128
LANES = 128
GRANT = 20 << 20
AXES = ("region", "member")

f32 = jnp.float32
bf16 = jnp.bfloat16

VMEM = pl.BlockSpec(memory_space=pltpu.VMEM)
SMEM = pl.BlockSpec(memory_space=pltpu.SMEM)


def dot_nn(a, b):
    return lax.dot_general(a, b, (((1,), (0,)), ((), ())), preferred_element_type=f32)


def dot_nt(a, b):
    return lax.dot_general(a, b, (((1,), (1,)), ((), ())), preferred_element_type=f32)


def split(x):
    high = x.astype(bf16)
    return high, (x - high.astype(f32)).astype(bf16)


def call(kernel, outs, inputs, flops, moved, smem_in=0, smem_out=0, scratch=()):
    return pl.pallas_call(
        kernel,
        out_shape=[jax.ShapeDtypeStruct(s, d) for s, d in outs],
        in_specs=[SMEM] * smem_in + [VMEM] * (len(inputs) - smem_in),
        out_specs=[VMEM] * (len(outs) - smem_out) + [SMEM] * smem_out,
        scratch_shapes=list(scratch),
        cost_estimate=pl.CostEstimate(flops=flops, bytes_accessed=moved, transcendentals=0),
        compiler_params=pltpu.CompilerParams(vmem_limit_bytes=GRANT),
    )(*inputs)


def parts_of(x, size):
    if size & (size - 1):
        return lax.div(x, size), lax.rem(x, size)
    return lax.shift_right_logical(x, size.bit_length() - 1), x & (size - 1)


def weights_kernel(cells, regions, live_ref, cell_ref, weight_ref, report_ref, table_ref, source_ref):
    region = lax.axis_index("region")
    bits = regions.bit_length() - 1
    points, slots = weight_ref.shape[1:]
    rows = cells // LANES + 2
    holder, within = parts_of(cell_ref[...], cells)
    block, low = parts_of(within, LANES)
    outside = holder != region
    named = holder.astype(f32)
    first = jnp.min(jnp.where(outside, named, float(regions))).astype(jnp.int32)
    second = jnp.max(jnp.where(outside, named, -1.0)).astype(jnp.int32)
    first = jnp.where(first == regions, region, first)
    second = jnp.where(second < 0, region, second)
    for j, source in enumerate((first, second)):
        distance = region ^ source
        place = jnp.int32(0)
        flip = jnp.int32(0)
        for k in range(bits):
            bit = (distance >> k) & 1
            place = place + (bit << (bits - 1 - k))
            flip = flip ^ bit
        source_ref[j] = place
        source_ref[2 + j] = flip
    high = jnp.where(outside, jnp.where(holder == first, rows - 2, rows - 1), block)
    active = lax.broadcasted_iota(jnp.int32, (1, slots), 1) < live_ref[0]
    weights = jnp.where(active, weight_ref[0], 0.0)
    values = jnp.concatenate([weights, weights * report_ref[...]], axis=0)
    low_hot = (lax.broadcasted_iota(jnp.int32, (LANES, slots), 0) == low).astype(f32).astype(bf16)
    chosen = jnp.concatenate(
        [jnp.where(high == row, values, 0.0) for row in range(rows)], axis=0
    )
    first, second = split(chosen)
    total = dot_nt(first, low_hot) + dot_nt(second, low_hot)
    table_ref[...] = total.reshape(rows, 2 * points, LANES)


def pick_kernel(source_ref, near_ref, far_ref, out_ref):
    count = near_ref.shape[0]
    for j in range(2):
        place = source_ref[j]
        inside = jnp.minimum(place, count - 1)
        outside = jnp.maximum(place - count, 0)
        out_ref[j] = jnp.where(place < count, near_ref[inside], far_ref[outside])


def anomaly_kernel(offsets, *refs):
    pieces, (anomaly_ref, mean_ref) = refs[:-2], refs[-2:]
    member = lax.axis_index("member")
    rows = pieces[0].shape[0]
    members = rows * len(pieces)
    total = jnp.sum(pieces[0][...].astype(f32), axis=0, keepdims=True)
    for piece in pieces[1:]:
        total = total + jnp.sum(piece[...].astype(f32), axis=0, keepdims=True)
    mean = total / members
    mean_ref[...] = mean
    for offset, piece in zip(offsets, pieces):
        start = pl.multiple_of((member ^ offset) * rows, rows)
        anomaly_ref[pl.ds(start, rows), :] = (piece[...].astype(f32) - mean).astype(bf16)


def products_kernel(anomaly_ref, mean_ref, table_ref, products_ref, forcing_ref):
    members, cells = anomaly_ref.shape
    points = products_ref.shape[0]
    chunk = min(cells, 2048)
    forcing = None
    for start in range(0, cells, chunk):
        block = anomaly_ref[:, start : start + chunk]
        departures = []
        for a in range(points):
            scaled = []
            for h in range(start // LANES, (start + chunk) // LANES):
                lanes = slice(h * LANES, (h + 1) * LANES)
                scaled.append(
                    (anomaly_ref[:, lanes].astype(f32) * table_ref[h, a : a + 1, :]).astype(bf16)
                )
            part = dot_nt(jnp.concatenate(scaled, axis=1), block)
            if start == 0:
                products_ref[a] = part
            else:
                products_ref[a] += part
        for h in range(start // LANES, (start + chunk) // LANES):
            lanes = slice(h * LANES, (h + 1) * LANES)
            tile = table_ref[h]
            departures.append(tile[points:, :] - tile[:points, :] * mean_ref[:, lanes])
        departure = jnp.concatenate(departures, axis=1)
        first, second = split(jnp.concatenate([departure, departure], axis=0))
        part = dot_nt(first, block) + dot_nt(second, block)
        forcing = part if forcing is None else forcing + part
    forcing_ref[...] = forcing


def cells_kernel(
    row_count, points, anomaly_ref, mean_ref, own_blend, first_blend, second_blend,
    own_ref, first_ref, second_ref, own_mix, first_mix, second_mix, column_ref
):
    member = lax.axis_index("member")
    odd = member & 1
    partner = member ^ 1
    other = member - 1 + 2 * odd
    exists = (other >= 0) & (other < row_count)
    other = jnp.where(exists, other, 0)
    slab = own_ref.shape[0]
    half = slab // 2
    for ref, band in ((own_ref, member), (first_ref, partner)):
        for u in range(2):
            start = pl.multiple_of(band * slab + u * half, half)
            ref[u * half : (u + 1) * half, :] = anomaly_ref[:, pl.ds(start, half)].T
    start = pl.multiple_of(other * slab + (1 - odd) * half, half)
    second_ref[...] = anomaly_ref[:, pl.ds(start, half)].T
    row = mean_ref[:, pl.ds(pl.multiple_of(member * slab, slab), slab)]
    column_ref[...] = jnp.broadcast_to(row, (8, slab)).T
    cell = lax.broadcasted_iota(jnp.int32, (1, slab), 1)
    upper = cell < half
    bases = column_bases(points)
    size = half // len(bases)
    inside = jnp.where(upper, cell, cell - half)
    base = jnp.zeros_like(cell)
    for g in range(1, len(bases)):
        base = base + jnp.where(inside >= g * size, bases[g] - bases[g - 1], 0)

    def columns(blend_ref, band, valid):
        blending = blend_ref[...]
        mixing = blending / jnp.sum(blending, axis=0, keepdims=True)
        tops = [jnp.clip(band - 1 + u, 0, row_count - 2) for u in range(2)]
        step = member - jnp.where(upper, tops[0], tops[1])
        pairs = []
        for c in range(2):
            pair = jnp.where(
                step == 0, mixing[c : c + 1], jnp.where(step == 1, mixing[2 + c : 3 + c], 0.0)
            )
            pairs.append(jnp.where(valid, pair, 0.0))
        rows = [
            jnp.where(base == q, pairs[0], jnp.where(base == q - 1, pairs[1], 0.0))
            for q in range(points)
        ]
        rows = rows + [jnp.zeros_like(rows[0])] * (-points % 8)
        return jnp.concatenate(rows, axis=0)

    own_mix[...] = columns(own_blend, member, True).T
    first_mix[...] = columns(first_blend, partner, True).T
    second = columns(second_blend, other, exists)
    second = jnp.where(odd == 1, second[:, :half], second[:, half:])
    second_mix[...] = second.T


def column_bases(points):
    return [min(max(b - 1 + v, 0), points - 2) for b in range(points) for v in range(2)]


def blended_parts(segments, transforms, points):
    half = segments[0][0].shape[0]
    bases = column_bases(points)
    size = half // len(bases)
    spans = []
    for v in range(points - 1):
        hits = [g for g, b in enumerate(bases) if b == v]
        spans.append((hits[0] * size, (hits[-1] + 1) * size))
    sums = [[None] * (points - 1) for _ in segments]
    for q in range(points):
        where = [v for v in (q - 1, q) if 0 <= v <= points - 2]
        rows = [
            (n, v, cells[spans[v][0] : spans[v][1], :])
            for n, (cells, _) in enumerate(segments)
            for v in where
        ]
        spread = dot_nn(jnp.concatenate([r[2] for r in rows], axis=0), transforms(q))
        at = 0
        for n, v, cells in rows:
            low, high = spans[v]
            term = segments[n][1][low:high, q : q + 1] * spread[at : at + high - low]
            sums[n][v] = term if sums[n][v] is None else sums[n][v] + term
            at += high - low
    return [jnp.concatenate(parts, axis=0) for parts in sums]


def transform_kernel(offsets, source_ref, *refs):
    count = len(offsets)
    pieces = refs[:count]
    (
        table_ref,
        products_ref,
        forcing_ref,
        first_ref,
        second_ref,
        first_mix,
        second_mix,
        transform_ref,
        to_first_ref,
        to_second_ref,
        margin_ref,
    ) = refs[count:]
    member = lax.axis_index("member")
    rows = pieces[0].shape[1]
    members = rows * count
    points = products_ref.shape[0]
    last = table_ref.shape[0]
    for offset, piece in zip(offsets, pieces):
        for j in range(2):
            start = pl.multiple_of((member ^ offset ^ source_ref[2 + j]) * rows, rows)
            margin_ref[pl.ds(start, rows), j * LANES : (j + 1) * LANES] = piece[j]
    values = margin_ref[...].astype(f32)
    mean = jnp.sum(values, axis=0, keepdims=True) / members
    pert = (values - mean).astype(bf16)
    pert_wide = pert.astype(f32)
    tiles = jnp.concatenate([table_ref[last - 2], table_ref[last - 1]], axis=1)
    departure = tiles[points:, :] - tiles[:points, :] * mean
    first, second = split(jnp.concatenate([departure, departure], axis=0))
    forcing = forcing_ref[...] + dot_nt(first, pert) + dot_nt(second, pert)
    forcing = forcing.T
    identity = lax.broadcasted_iota(jnp.int32, (members, members), 0) == lax.broadcasted_iota(
        jnp.int32, (members, members), 1
    )

    def plus(scalar, matrix):
        return matrix + jnp.where(identity, scalar, 0.0)

    def left(x):
        high, low = split(x)
        return jnp.concatenate([high, high, low], axis=1)

    def right(x):
        high, low = split(x)
        return jnp.concatenate([high, low, high], axis=0)

    span = range(points)
    matrix, scale = [], []
    for a in span:
        weighted = (pert_wide * tiles[a : a + 1, :]).astype(bf16)
        full = plus(members - 1.0, products_ref[a] + dot_nt(weighted, pert))
        square = jnp.sum(jnp.sum(full * full, axis=0, keepdims=True), axis=1, keepdims=True)
        frobenius = jnp.sqrt(square)
        matrix.append(full / frobenius)
        scale.append(1.0 / jnp.sqrt(frobenius))
    matrix_left = [left(x) for x in matrix]
    squared = [dot_nn(matrix_left[a], right(matrix[a])) for a in span]
    root = [
        plus(2.25, -2.4375 * matrix[a])
        + dot_nn(
            left(squared[a]),
            right(plus(1.6875, 0.0625 * squared[a] - 0.5625 * matrix[a])),
        )
        for a in span
    ]
    current = [dot_nn(matrix_left[a], right(root[a])) for a in span]
    root_left = [left(x) for x in root]
    middle = [plus(1.5, -0.5 * dot_nn(root_left[a], right(current[a]))) for a in span]
    middle_right = [right(x) for x in middle]
    current = [dot_nn(left(current[a]), middle_right[a]) for a in span]
    root = [dot_nn(root_left[a], middle_right[a]) for a in span]
    root_left = [left(x) for x in root]
    middle = [plus(1.5, -0.5 * dot_nn(root_left[a], right(current[a]))) for a in span]
    root = [dot_nn(root_left[a], right(middle[a])) for a in span]
    for a in span:
        inverse = root[a] * scale[a]
        inner = jnp.sum(inverse * forcing[:, a : a + 1], axis=0, keepdims=True)
        mean_weights = jnp.sum(inverse * inner, axis=1, keepdims=True)
        transform_ref[a] = (mean_weights + jnp.sqrt(members - 1.0) * inverse).astype(bf16)
    half = second_ref.shape[0]
    segments = [
        (first_ref[0:half, :], first_mix[0:half, :]),
        (first_ref[half:, :], first_mix[half:, :]),
        (second_ref[...], second_mix[...]),
    ]
    parts = blended_parts(segments, lambda q: transform_ref[q], points)
    to_first_ref[0:half, :] = parts[0].astype(bf16)
    to_first_ref[half:, :] = parts[1].astype(bf16)
    to_second_ref[...] = parts[2].astype(bf16)


def own_kernel(transform_ref, own_ref, own_mix, column_ref, out_ref):
    points = transform_ref.shape[0]
    half = own_ref.shape[0] // 2
    segments = [
        (own_ref[0:half, :], own_mix[0:half, :]),
        (own_ref[half:, :], own_mix[half:, :]),
    ]
    parts = blended_parts(segments, lambda q: transform_ref[q], points)
    for u in range(2):
        rows = slice(u * half, (u + 1) * half)
        out_ref[rows, :] = parts[u] + column_ref[rows, 0:1]


def per_device(ensemble, reports, report_count, report_cell, report_weight, blending):
    local_members, cell_count = ensemble.shape
    regions = lax.axis_size("region")
    groups = lax.axis_size("member")
    members = local_members * groups
    points = report_weight.shape[1]
    slots = reports.shape[1]
    slab = cell_count // groups
    half = slab // 2
    devices = regions * groups
    region_bits = regions.bit_length() - 1
    member_bits = groups.bit_length() - 1

    def swap(name, x, mask):
        with jax.named_scope(name):
            return lax.ppermute(x, AXES, [(i, i ^ mask) for i in range(devices)])

    def across(i):
        position = i % groups
        other = (position + 1 if position % 2 else position - 1) % groups
        return i - position + other

    def cross(name, x):
        with jax.named_scope(name):
            return lax.ppermute(x, AXES, [(i, across(i)) for i in range(devices)])

    member_masks = [(1 << k) | 1 for k in range(member_bits - 1, 0, -1)] + [1]

    table_rows = cell_count // LANES + 2
    with jax.named_scope("kernel_weights"):
        table, sources = call(
            functools.partial(weights_kernel, cell_count, regions),
            [((table_rows, 2 * points, LANES), f32), ((4,), jnp.int32)],
            (report_count, report_cell, report_weight, reports),
            4 * table_rows * 2 * points * slots * LANES,
            100000,
            smem_in=1,
            smem_out=1,
        )

    near = ensemble[:, :MARGIN][None]
    for step, k in enumerate(range(region_bits - 1, -1, -1)):
        far = swap(f"margin_{step}", near, (groups << k) | 1)
        if k:
            near = jnp.concatenate([near, far], axis=0)
    with jax.named_scope("kernel_pick"):
        (picked,) = call(
            pick_kernel,
            [((2, local_members, MARGIN), bf16)],
            (sources, near, far),
            0,
            100000,
            smem_in=1,
        )
    margins = [picked]
    for step, mask in enumerate(member_masks):
        if step == 0:
            margins = margins + [swap("spread_0", picked, mask)]
        else:
            joined = swap(f"spread_{step}", jnp.concatenate(margins, axis=0), mask)
            margins = margins + [joined[2 * i : 2 * i + 2] for i in range(len(margins))]

    pieces, offsets = [ensemble], [0]
    for step, mask in enumerate(member_masks):
        pieces = pieces + [swap(f"whole_{step}_{i}", x, mask) for i, x in enumerate(pieces)]
        offsets = offsets + [offset ^ mask for offset in offsets]
    partner_blending = swap("blend_partner", blending, 1)
    other_blending = cross("blend_other", blending)

    with jax.named_scope("kernel_anomaly"):
        anomaly, mean = call(
            functools.partial(anomaly_kernel, tuple(offsets)),
            [((members, cell_count), bf16), ((1, cell_count), f32)],
            tuple(pieces),
            4 * members * cell_count,
            4 * members * cell_count,
        )
    with jax.named_scope("kernel_products"):
        products, forcing = call(
            products_kernel,
            [((points, members, members), f32), ((2 * points, members), f32)],
            (anomaly, mean, table),
            2 * points * members * members * cell_count,
            2 * members * cell_count + 4 * points * members * members,
        )
    padded = points + -points % 8
    with jax.named_scope("kernel_cells"):
        own_cells, first_cells, second_cells, own_mix, first_mix, second_mix, column = call(
            functools.partial(cells_kernel, groups, points),
            [
                ((slab, members), bf16),
                ((slab, members), bf16),
                ((half, members), bf16),
                ((slab, padded), f32),
                ((slab, padded), f32),
                ((half, padded), f32),
                ((slab, 8), f32),
            ],
            (anomaly, mean, blending, partner_blending, other_blending),
            3 * slab * members,
            8 * slab * members,
        )
    with jax.named_scope("kernel_transform"):
        transform, to_first, to_second = call(
            functools.partial(transform_kernel, tuple(offsets)),
            [
                ((points, members, members), bf16),
                ((slab, members), bf16),
                ((half, members), bf16),
            ],
            (
                sources,
                *margins,
                table,
                products,
                forcing,
                first_cells,
                second_cells,
                first_mix,
                second_mix,
            ),
            2 * 26 * points * members**3,
            8 * points * members * members,
            smem_in=1,
            scratch=[pltpu.VMEM((members, 2 * LANES), bf16)],
        )
    from_other = cross("back_other", to_second)
    from_partner = swap("back_partner", to_first, 1)
    with jax.named_scope("kernel_own"):
        (own,) = call(
            own_kernel,
            [((slab, members), f32)],
            (transform, own_cells, own_mix, column),
            4 * slab * members * members,
            8 * slab * members,
        )
    odd = lax.axis_index("member") % 2
    upper = jnp.where(odd == 0, from_other.astype(f32), 0.0)
    lower = jnp.where(odd == 1, from_other.astype(f32), 0.0)
    total = own + from_partner.astype(f32) + jnp.concatenate([upper, lower], axis=0)
    return total.astype(bf16)


def solution(mesh):
    return jax.shard_map(
        per_device,
        mesh=mesh,
        in_specs=(
            P("member", "region"),
            P("region", None),
            P("region"),
            P("region", None),
            P("region", "member", None),
            P(None, ("region", "member")),
        ),
        out_specs=P(("region", "member"), None),
        check_vma=False,
    )
```

time: 55.7 us -> 34.9 us (0.63)
  Pallas kernels: 19.9 us -> 9.6 us
  local copies, waits for them, and re-layouts: 9.65 us -> 0.75 us
  between operations: 3.3 us -> 0.82 us
  other arithmetic: 3.15 us -> 0.85 us
  starting transfers between devices: 13.2 us -> 15.2 us
  waiting for transfers between devices: 5.93 us -> 7.5 us
    pallas_call x6 -> x7, Pallas kernels: 19.9 us -> 9.6 us  [call(): pl.pallas_call(kernel, out_shape=[jax.ShapeDtypeStruct(s, d) for s, d in...]
    unnamed x17 -> x10, local copies, waits for them, and re-layouts: 4.59 us -> 0.03 us
    ppermute x2, waiting for transfers between devices: 0.51 us -> 3.85 us  [cross(): return lax.ppermute(x, AXES, [(i, across(i)) for i in range(devices)])]
    another operation x3 -> x0, local copies, waits for them, and re-layouts: 2.4 us -> none  [the longest x2 1.74 us: mixing_columns(): return jnp.stack(rows, axis=0).T]
    slice x2 -> x1, local copies, waits for them, and re-layouts: 1.92 us -> 0.01 us  [per_device(): margins = margins + [joined[2 * i:2 * i + 2] for i in range(len(margins))]]
    ppermute x10, waiting for transfers between devices: 5.41 us -> 3.65 us  [swap(): return lax.ppermute(x, AXES, [(i, i ^ mask) for i in range(devices)])]
    another operation x5 -> x0, other arithmetic: 1.36 us -> none  [the longest x1 0.65 us: per_device(): jnp.stack([member * slab, partner * slab, other_half])]
    ppermute x2, starting transfers between devices: 1.62 us -> 2.76 us  [cross(): return lax.ppermute(x, AXES, [(i, across(i)) for i in range(devices)])]
  transfers between devices with their start and end apart: 12 -> 12, of which waited for: 4 -> 5; matrix products, arithmetic and copies ran while one was open for 15% -> 0% of each run, Pallas kernels for 8% -> 12%
where the time goes in v2:
time: 34.9 us; the launch traced here: 34.7 us
  starting transfers between devices  15.2 us (44%)
  Pallas kernels  9.6 us (28%)
  waiting for transfers between devices  7.5 us (21%)
  other arithmetic  0.85 us (2%)
  between operations  0.82 us (2%)
  local copies, waits for them, and re-layouts  0.75 us (2%)
    ppermute x10, starting transfers between devices, swap(): return lax.ppermute(x, AXES, [(i, i ^ mask) for i in range(devices)])  12.4 us
    pallas_call x7, Pallas kernels, call(): pl.pallas_call(kernel, out_shape=[jax.ShapeDtypeStruct(s, d) for s, d in...  9.6 us
    ppermute x2, waiting for transfers between devices, cross(): return lax.ppermute(x, AXES, [(i, across(i)) for i in range(devices)])  3.85 us
    ppermute x10, waiting for transfers between devices, swap(): return lax.ppermute(x, AXES, [(i, i ^ mask) for i in range(devices)])  3.65 us
    ppermute x2, starting transfers between devices, cross(): return lax.ppermute(x, AXES, [(i, across(i)) for i in range(devices)])  2.76 us
    convert_element_type x1, other arithmetic, per_device(): return total.astype(bf16)  0.79 us
    broadcast_in_dim x1, local copies, waits for them, and re-layouts, per_device(): near = ensemble[:, :MARGIN][None]  0.72 us
  transfers between devices with their start and end apart: 12, of which 5 were waited for; matrix products, arithmetic and copies ran while one was open for 0% of the time, Pallas kernels for 12%

profile of v2, /device:TPU:0, one launch (start us, length us, event | category | flops | bytes accessed | tf_op | source)
XLA Modules:
  0.0 34.7 jit_solution(13664240552044475945)
XLA Ops:
  0.0 0.7 %slice_bitcast_fusion = bf16[1,64,128]{2,1,0:T(8,128)(2,1)S(1)} fusion(bf16[64,2048]{1,0:T(8,128)(2,1)} %refs_0_.1), kind=kLoop, calls=%fused_computation.7 | loop fusion | bytes 32768 | tf_op jit(solution)/shard_map/broadcast_in_dim | solution.py:375
  0.7 3.5 %collective-permute-start = (bf16[1,64,128]{2,1,0:T(8,128)(2,1)S(1)}, bf16[1,64,128]{2,1,0:T(8,128)(2,1)S(1)}, u32[]{:S(2)}, u32[]{:S(2)}) collective-permute-start(bf16[1,64,128]{2,1,0:T(8,128)(2,1)S(1)} %slice_bitcast_fusion), channel_id=1, source_target_pairs={{0,17},{1,16},{2,19},{3,18},{4,21},{5,20},{6,23},{7,22},{8,25},{9,... | collective-permute-start | bytes 49160 | tf_op jit(solution)/shard_map/margin_0/ppermute | solution.py:350
  4.2 1.4 %collective-permute-done = bf16[1,64,128]{2,1,0:T(8,128)(2,1)S(1)} collective-permute-done((bf16[1,64,128]{2,1,0:T(8,128)(2,1)S(1)}, bf16[1,64,128]{2,1,0:T(8,128)(2,1)S(1)}, u32[]{:S(2)}, u32[]{:S(2)}) %collective-permute-start) | collective-permute-done | bytes 16416 | tf_op jit(solution)/shard_map/margin_0/ppermute | solution.py:350
  5.7 0.0 copy-start.2
  5.7 0.0 copy-start.3
  5.7 0.0 copy-start.4
  5.7 2.0 %collective-permute-start.1 = (bf16[2,64,128]{2,1,0:T(8,128)(2,1)S(1)}, bf16[2,64,128]{2,1,0:T(8,128)(2,1)S(1)}, u32[]{:S(2)}, u32[]{:S(2)}) collective-permute-start(bf16[2,64,128]{2,1,0:T(8,128)(2,1)S(1)} %pad_maximum_fusion.2), channel_id=1, source_target_pairs={{0,9},{1,8},{2,11},{3,10},{4,13},{5,12},{6,15},{7,14},{8,1},{9,0},... | collective-permute-start | bytes 98312 | tf_op jit(solution)/shard_map/margin_1/ppermute | solution.py:350
  7.6 1.5 %collective-permute-start.5 = (bf16[64,2048]{1,0:T(8,128)(2,1)}, bf16[64,2048]{1,0:T(8,128)(2,1)S(1)}, u32[]{:S(2)}, u32[]{:S(2)}) collective-permute-start(bf16[64,2048]{1,0:T(8,128)(2,1)} %refs_0_.1), channel_id=1, source_target_pairs={{0,3},{1,2},{2,1},{3,0},{4,7},{5,6},{6,5},{7,4},{8,11},{9,10},{10,... | collective-permute-start | bytes 786440 | tf_op jit(solution)/shard_map/whole_0_0/ppermute | solution.py:350
  9.1 0.1 collective-permute-done.1
  9.3 1.8 %collective-permute-start.2 = (bf16[4,64,128]{2,1,0:T(8,128)(2,1)S(1)}, bf16[4,64,128]{2,1,0:T(8,128)(2,1)S(1)}, u32[]{:S(2)}, u32[]{:S(2)}) collective-permute-start(bf16[4,64,128]{2,1,0:T(8,128)(2,1)S(1)} %pad_maximum_fusion.near_ref), channel_id=1, source_target_pairs={{0,5},{1,4},{2,7},{3,6},{4,1},{5,0},{6,3},{7,2},{8,13},{9,12},{10,... | collective-permute-start | bytes 196616 | tf_op jit(solution)/shard_map/margin_2/ppermute | solution.py:350
  11.7 0.0 copy-done.2
  11.7 0.0 copy-done.3
  11.7 0.0 copy-done.4
  11.7 0.0 copy-start
  11.8 1.0 %kernel_weights.1 = (f32[18,8,128]{2,1,0:T(8,128)S(1)}, s32[4]{0:T(128)S(1)}) custom-call(s32[1]{0:T(128)S(6)} %copy.7.live_ref, s32[1,1024]{1,0:T(1,128)S(1)} %copy-done.3, f32[1,4,1024]{2,1,0:T(4,128)S(1)} %copy-done.2, f32[1,1024]{1,0:T(1,128)S(1)} %copy-done.4), custom_call_target="tpu_custom_call" | custom-call | flops 75497472 | bytes 100000 | tf_op jit(solution)/shard_map/kernel_weights/pallas_call | solution.py:36
  12.8 0.5 %collective-permute-done.2.far_ref = bf16[4,64,128]{2,1,0:T(8,128)(2,1)S(1)} collective-permute-done((bf16[4,64,128]{2,1,0:T(8,128)(2,1)S(1)}, bf16[4,64,128]{2,1,0:T(8,128)(2,1)S(1)}, u32[]{:S(2)}, u32[]{:S(2)}) %collective-permute-start.2) | collective-permute-done | bytes 65568 | tf_op jit(solution)/shard_map/margin_2/ppermute | solution.py:350
  13.3 0.6 %kernel_pick.1.refs_0_ = bf16[2,64,128]{2,1,0:T(8,128)(2,1)S(1)} custom-call(s32[4]{0:T(128)S(1)} %get-tuple-element.21.source_ref, bf16[4,64,128]{2,1,0:T(8,128)(2,1)S(1)} %pad_maximum_fusion.near_ref, bf16[4,64,128]{2,1,0:T(8,128)(2,1)S(1)} %collective-permute-done.2.far_ref), custom_call_target="tpu_custom_call" | custom-call | bytes 100000 | tf_op jit(solution)/shard_map/kernel_pick/pallas_call | solution.py:36
  13.8 0.0 copy-start.1
  13.8 2.2 %collective-permute-start.3 = (bf16[2,64,128]{2,1,0:T(8,128)(2,1)S(1)}, bf16[2,64,128]{2,1,0:T(8,128)(2,1)S(1)}, u32[]{:S(2)}, u32[]{:S(2)}) collective-permute-start(bf16[2,64,128]{2,1,0:T(8,128)(2,1)S(1)} %kernel_pick.1.refs_0_), channel_id=1, source_target_pairs={{0,3},{1,2},{2,1},{3,0},{4,7},{5,6},{6,5},{7,4},{8,11},{9,10},{10,... | collective-permute-start | bytes 98312 | tf_op jit(solution)/shard_map/spread_0/ppermute | solution.py:350
  16.1 1.6 %collective-permute-done.3.refs_1_ = bf16[2,64,128]{2,1,0:T(8,128)(2,1)S(1)} collective-permute-done((bf16[2,64,128]{2,1,0:T(8,128)(2,1)S(1)}, bf16[2,64,128]{2,1,0:T(8,128)(2,1)S(1)}, u32[]{:S(2)}, u32[]{:S(2)}) %collective-permute-start.3) | collective-permute-done | bytes 32800 | tf_op jit(solution)/shard_map/spread_0/ppermute | solution.py:350
  17.7 0.2 collective-permute-start.4
  17.9 0.0 copy-done
  17.9 0.4 %collective-permute-start.6 = (bf16[64,2048]{1,0:T(8,128)(2,1)S(1)}, bf16[64,2048]{1,0:T(8,128)(2,1)S(1)}, u32[]{:S(2)}, u32[]{:S(2)}) collective-permute-start(bf16[64,2048]{1,0:T(8,128)(2,1)S(1)} %copy-done), channel_id=1, source_target_pairs={{0,1},{1,0},{2,3},{3,2},{4,5},{5,4},{6,7},{7,6},{8,9},{9,8},{10,11... | collective-permute-start | bytes 786440 | tf_op jit(solution)/shard_map/whole_1_0/ppermute | solution.py:350
  18.3 0.0 collective-permute-done.5.refs_1_
  18.3 0.2 collective-permute-start.7
  18.4 0.0 copy-done.1
  18.4 0.4 %collective-permute-start.8 = (f32[4,512]{1,0:T(4,128)S(1)}, f32[4,512]{1,0:T(4,128)S(1)}, u32[]{:S(2)}, u32[]{:S(2)}) collective-permute-start(f32[4,512]{1,0:T(4,128)S(1)} %copy-done.1), channel_id=1, source_target_pairs={{0,1},{1,0},{2,3},{3,2},{4,5},{5,4},{6,7},{7,6},{8,9},{9,8},{10,11... | collective-permute-start | bytes 24584 | tf_op jit(solution)/shard_map/blend_partner/ppermute | solution.py:350
  18.8 1.7 %collective-permute-start.9 = (f32[4,512]{1,0:T(4,128)S(1)}, f32[4,512]{1,0:T(4,128)S(1)}, u32[]{:S(2)}, u32[]{:S(2)}) collective-permute-start(f32[4,512]{1,0:T(4,128)S(1)} %copy-done.1), channel_id=1, source_target_pairs={{0,3},{1,2},{2,1},{3,0},{4,7},{5,6},{6,5},{7,4},{8,11},{9,10},{10,... | collective-permute-start | bytes 24584 | tf_op jit(solution)/shard_map/blend_other/ppermute | solution.py:359
  20.5 0.0 collective-permute-done.4
  20.5 0.0 collective-permute-done.6.refs_2_
  20.5 0.0 collective-permute-done.7.refs_3_
  20.6 0.4 %kernel_anomaly.1 = (bf16[256,2048]{1,0:T(8,128)(2,1)S(1)}, f32[1,2048]{1,0:T(1,128)S(1)}) custom-call(bf16[64,2048]{1,0:T(8,128)(2,1)S(1)} %copy-done, bf16[64,2048]{1,0:T(8,128)(2,1)S(1)} %collective-permute-done.5.refs_1_, bf16[64,2048]{1,0:T(8,128)(2,1)S(1)} %collective-permute-done.6.refs_2_, bf16[64,2048]{1,0:T(8,128)(2,1)S(1)} %collective-permute-done.7.refs_3_), custom_call_target="tpu_custom_call" | custom-call | flops 2097152 | bytes 2097152 | tf_op jit(solution)/shard_map/kernel_anomaly/pallas_call | solution.py:36
  21.0 1.8 %kernel_products.1 = (f32[4,256,256]{2,1,0:T(8,128)S(1)}, f32[8,256]{1,0:T(8,128)S(1)}) custom-call(bf16[256,2048]{1,0:T(8,128)(2,1)S(1)} %get-tuple-element.23.anomaly_ref, f32[1,2048]{1,0:T(1,128)S(1)} %get-tuple-element.24.mean_ref, f32[18,8,128]{2,1,0:T(8,128)S(1)} %get-tuple-element.22.table_ref.refs_4_), custom_call_target="tpu_custom_call" | custom-call | flops 1073741824 | bytes 2097152 | tf_op jit(solution)/shard_map/kernel_products/pallas_call | solution.py:36
  22.8 0.0 collective-permute-done.8.first_blend
  22.8 0.0 collective-permute-done.9.second_blend
  22.8 0.5 %kernel_cells.1 = (bf16[512,256]{1,0:T(8,128)(2,1)S(1)}, bf16[512,256]{1,0:T(8,128)(2,1)S(1)}, bf16[256,256]{1,0:T(8,128)(2,1)S(1)}, f32[512,8]{1,0:T(8,128)S(1)...) custom-call(bf16[256,2048]{1,0:T(8,128)(2,1)S(1)} %get-tuple-element.23.anomaly_ref, ...), custom_call_target="tpu_custom_call" | custom-call | flops 393216 | bytes 1048576 | tf_op jit(solution)/shard_map/kernel_cells/pallas_call | solution.py:36
  23.3 5.0 %kernel_transform.1 = (bf16[4,256,256]{2,1,0:T(8,128)(2,1)S(1)}, bf16[512,256]{1,0:T(8,128)(2,1)S(1)}, bf16[256,256]{1,0:T(8,128)(2,1)S(1)}) custom-call(s32[4]{0:T(128)S(1)} %get-tuple-element.21.source_ref, bf16[2,64,128]{2,1,0:T(8,128)(2,1)S(1)} %kernel_pick.1.refs_0_, bf16[2,64,128]{2,1,0:T(8,128)(2,1)S(1)} %collective-permute-done.3.refs_1_, ...), custom_call_target="tpu_custom_call" | custom-call | flops 3489660928 | bytes 2097152 | tf_op jit(solution)/shard_map/kernel_transform/pallas_call | solution.py:36
  28.3 1.0 %collective-permute-start.11 = (bf16[256,256]{1,0:T(8,128)(2,1)S(1)}, bf16[256,256]{1,0:T(8,128)(2,1)S(1)}, u32[]{:S(2)}, u32[]{:S(2)}) collective-permute-start(bf16[256,256]{1,0:T(8,128)(2,1)S(1)} %get-tuple-element.36), channel_id=1, source_target_pairs={{0,3},{1,2},{2,1},{3,0},{4,7},{5,6},{6,5},{7,4},{8,11},{9,10},{10,... | collective-permute-start | bytes 393224 | tf_op jit(solution)/shard_map/back_other/ppermute | solution.py:359
  29.3 0.4 %collective-permute-start.10 = (bf16[512,256]{1,0:T(8,128)(2,1)S(1)}, bf16[512,256]{1,0:T(8,128)(2,1)S(1)}, u32[]{:S(2)}, u32[]{:S(2)}) collective-permute-start(bf16[512,256]{1,0:T(8,128)(2,1)S(1)} %get-tuple-element.35), channel_id=1, source_target_pairs={{0,1},{1,0},{2,3},{3,2},{4,5},{5,4},{6,7},{7,6},{8,9},{9,8},{10,11... | collective-permute-start | bytes 786440 | tf_op jit(solution)/shard_map/back_partner/ppermute | solution.py:350
  29.7 0.3 kernel_own.1
  30.0 3.9 %collective-permute-done.11 = bf16[256,256]{1,0:T(8,128)(2,1)S(1)} collective-permute-done((bf16[256,256]{1,0:T(8,128)(2,1)S(1)}, bf16[256,256]{1,0:T(8,128)(2,1)S(1)}, u32[]{:S(2)}, u32[]{:S(2)}) %collective-permute-start.11) | collective-permute-done | bytes 131104 | tf_op jit(solution)/shard_map/back_other/ppermute | solution.py:359
  33.9 0.0 collective-permute-done.10
  33.9 0.8 %fusion = bf16[512,256]{1,0:T(8,128)(2,1)} fusion(f32[256,256]{1,0:T(8,128)S(1)} %get-tuple-element.38, f32[256,256]{1,0:T(8,128)S(1)} %get-tuple-element.37, f32[512,256]{1,0:T(8,128)S(1)} %kernel_own.1, bf16[512,256]{1,0:T(8,128)(2,1)S(1)} %collective-permute-done.10), kind=kLoop, calls=%fused_computation.1 | loop fusion | flops 655360 | bytes 1572864 | tf_op jit(solution)/shard_map/convert_element_type | solution.py:475
  (5 shorter events, 0.1 us)
Async XLA Ops:
  0.7 4.9 %collective-permute-start = (bf16[1,64,128]{2,1,0:T(8,128)(2,1)S(1)}, bf16[1,64,128]{2,1,0:T(8,128)(2,1)S(1)}, u32[]{:S(2)}, u32[]{:S(2)}) collective-permute-start(bf16[1,64,128]{2,1,0:T(8,128)(2,1)S(1)} %slice_bitcast_fusion), channel_id=1, source_target_pairs={{0,17},{1,16},{2,19},{3,18},{4,21},{5,20},{6,23},{7,22},{8,25},{9,... | collective-permute-start | bytes 49160 | tf_op jit(solution)/shard_map/margin_0/ppermute | solution.py:350
  5.7 6.0 %copy-start.2 = (f32[1,4,1024]{2,1,0:T(4,128)S(1)}, f32[1,4,1024]{2,1,0:T(4,128)}, u32[]{:S(2)}) copy-start(f32[1,4,1024]{2,1,0:T(4,128)} %weight_ref.1) | copy-start | bytes 49156
  5.7 6.1 %copy-start.3 = (s32[1,1024]{1,0:T(1,128)S(1)}, s32[1,1024]{1,0:T(1,128)}, u32[]{:S(2)}) copy-start(s32[1,1024]{1,0:T(1,128)} %cell_ref.1) | copy-start | bytes 12292
  5.7 6.1 %copy-start.4 = (f32[1,1024]{1,0:T(1,128)S(1)}, f32[1,1024]{1,0:T(1,128)}, u32[]{:S(2)}) copy-start(f32[1,1024]{1,0:T(1,128)} %report_ref.1) | copy-start | bytes 12292
  5.7 3.6 %collective-permute-start.1 = (bf16[2,64,128]{2,1,0:T(8,128)(2,1)S(1)}, bf16[2,64,128]{2,1,0:T(8,128)(2,1)S(1)}, u32[]{:S(2)}, u32[]{:S(2)}) collective-permute-start(bf16[2,64,128]{2,1,0:T(8,128)(2,1)S(1)} %pad_maximum_fusion.2), channel_id=1, source_target_pairs={{0,9},{1,8},{2,11},{3,10},{4,13},{5,12},{6,15},{7,14},{8,1},{9,0},... | collective-permute-start | bytes 98312 | tf_op jit(solution)/shard_map/margin_1/ppermute | solution.py:350
  7.6 10.6 %collective-permute-start.5 = (bf16[64,2048]{1,0:T(8,128)(2,1)}, bf16[64,2048]{1,0:T(8,128)(2,1)S(1)}, u32[]{:S(2)}, u32[]{:S(2)}) collective-permute-start(bf16[64,2048]{1,0:T(8,128)(2,1)} %refs_0_.1), channel_id=1, source_target_pairs={{0,3},{1,2},{2,1},{3,0},{4,7},{5,6},{6,5},{7,4},{8,11},{9,10},{10,... | collective-permute-start | bytes 786440 | tf_op jit(solution)/shard_map/whole_0_0/ppermute | solution.py:350
  9.3 4.0 %collective-permute-start.2 = (bf16[4,64,128]{2,1,0:T(8,128)(2,1)S(1)}, bf16[4,64,128]{2,1,0:T(8,128)(2,1)S(1)}, u32[]{:S(2)}, u32[]{:S(2)}) collective-permute-start(bf16[4,64,128]{2,1,0:T(8,128)(2,1)S(1)} %pad_maximum_fusion.near_ref), channel_id=1, source_target_pairs={{0,5},{1,4},{2,7},{3,6},{4,1},{5,0},{6,3},{7,2},{8,13},{9,12},{10,... | collective-permute-start | bytes 196616 | tf_op jit(solution)/shard_map/margin_2/ppermute | solution.py:350
  11.7 6.2 %copy-start = (bf16[64,2048]{1,0:T(8,128)(2,1)S(1)}, bf16[64,2048]{1,0:T(8,128)(2,1)}, u32[]{:S(2)}) copy-start(bf16[64,2048]{1,0:T(8,128)(2,1)} %refs_0_.1) | copy-start | bytes 786436
  13.8 4.6 %copy-start.1 = (f32[4,512]{1,0:T(4,128)S(1)}, f32[4,512]{1,0:T(4,128)}, u32[]{:S(2)}) copy-start(f32[4,512]{1,0:T(4,128)} %own_blend.1) | copy-start | bytes 24580
  13.8 3.9 %collective-permute-start.3 = (bf16[2,64,128]{2,1,0:T(8,128)(2,1)S(1)}, bf16[2,64,128]{2,1,0:T(8,128)(2,1)S(1)}, u32[]{:S(2)}, u32[]{:S(2)}) collective-permute-start(bf16[2,64,128]{2,1,0:T(8,128)(2,1)S(1)} %kernel_pick.1.refs_0_), channel_id=1, source_target_pairs={{0,3},{1,2},{2,1},{3,0},{4,7},{5,6},{6,5},{7,4},{8,11},{9,10},{10,... | collective-permute-start | bytes 98312 | tf_op jit(solution)/shard_map/spread_0/ppermute | solution.py:350
  17.7 2.8 %collective-permute-start.4 = (bf16[4,64,128]{2,1,0:T(8,128)(2,1)S(1)}, bf16[4,64,128]{2,1,0:T(8,128)(2,1)S(1)}, u32[]{:S(2)}, u32[]{:S(2)}) collective-permute-start(bf16[4,64,128]{2,1,0:T(8,128)(2,1)S(1)} %pad_maximum_fusion.1), channel_id=1, source_target_pairs={{0,1},{1,0},{2,3},{3,2},{4,5},{5,4},{6,7},{7,6},{8,9},{9,8},{10,11... | collective-permute-start | bytes 196616 | tf_op jit(solution)/shard_map/spread_1/ppermute | solution.py:350
  17.9 2.6 %collective-permute-start.6 = (bf16[64,2048]{1,0:T(8,128)(2,1)S(1)}, bf16[64,2048]{1,0:T(8,128)(2,1)S(1)}, u32[]{:S(2)}, u32[]{:S(2)}) collective-permute-start(bf16[64,2048]{1,0:T(8,128)(2,1)S(1)} %copy-done), channel_id=1, source_target_pairs={{0,1},{1,0},{2,3},{3,2},{4,5},{5,4},{6,7},{7,6},{8,9},{9,8},{10,11... | collective-permute-start | bytes 786440 | tf_op jit(solution)/shard_map/whole_1_0/ppermute | solution.py:350
  18.3 2.3 %collective-permute-start.7 = (bf16[64,2048]{1,0:T(8,128)(2,1)S(1)}, bf16[64,2048]{1,0:T(8,128)(2,1)S(1)}, u32[]{:S(2)}, u32[]{:S(2)}) collective-permute-start(bf16[64,2048]{1,0:T(8,128)(2,1)S(1)} %collective-permute-done.5.refs_1_), channel_id=1, source_target_pairs={{0,1},{1,0},{2,3},{3,2},{4,5},{5,4},{6,7},{7,6},{8,9},{9,8},{10,11... | collective-permute-start | bytes 786440 | tf_op jit(solution)/shard_map/whole_1_1/ppermute | solution.py:350
  18.4 4.3 %collective-permute-start.8 = (f32[4,512]{1,0:T(4,128)S(1)}, f32[4,512]{1,0:T(4,128)S(1)}, u32[]{:S(2)}, u32[]{:S(2)}) collective-permute-start(f32[4,512]{1,0:T(4,128)S(1)} %copy-done.1), channel_id=1, source_target_pairs={{0,1},{1,0},{2,3},{3,2},{4,5},{5,4},{6,7},{7,6},{8,9},{9,8},{10,11... | collective-permute-start | bytes 24584 | tf_op jit(solution)/shard_map/blend_partner/ppermute | solution.py:350
  18.8 4.0 %collective-permute-start.9 = (f32[4,512]{1,0:T(4,128)S(1)}, f32[4,512]{1,0:T(4,128)S(1)}, u32[]{:S(2)}, u32[]{:S(2)}) collective-permute-start(f32[4,512]{1,0:T(4,128)S(1)} %copy-done.1), channel_id=1, source_target_pairs={{0,3},{1,2},{2,1},{3,0},{4,7},{5,6},{6,5},{7,4},{8,11},{9,10},{10,... | collective-permute-start | bytes 24584 | tf_op jit(solution)/shard_map/blend_other/ppermute | solution.py:359
  28.3 5.6 %collective-permute-start.11 = (bf16[256,256]{1,0:T(8,128)(2,1)S(1)}, bf16[256,256]{1,0:T(8,128)(2,1)S(1)}, u32[]{:S(2)}, u32[]{:S(2)}) collective-permute-start(bf16[256,256]{1,0:T(8,128)(2,1)S(1)} %get-tuple-element.36), channel_id=1, source_target_pairs={{0,3},{1,2},{2,1},{3,0},{4,7},{5,6},{6,5},{7,4},{8,11},{9,10},{10,... | collective-permute-start | bytes 393224 | tf_op jit(solution)/shard_map/back_other/ppermute | solution.py:359
  29.3 4.6 %collective-permute-start.10 = (bf16[512,256]{1,0:T(8,128)(2,1)S(1)}, bf16[512,256]{1,0:T(8,128)(2,1)S(1)}, u32[]{:S(2)}, u32[]{:S(2)}) collective-permute-start(bf16[512,256]{1,0:T(8,128)(2,1)S(1)} %get-tuple-element.35), channel_id=1, source_target_pairs={{0,1},{1,0},{2,3},{3,2},{4,5},{5,4},{6,7},{7,6},{8,9},{9,8},{10,11... | collective-permute-start | bytes 786440 | tf_op jit(solution)/shard_map/back_partner/ppermute | solution.py:350

commit v3 on v2

--- a/solution.py
+++ b/solution.py
@@ -6,6 +6,7 @@
 from jax.experimental import pallas as pl
 from jax.experimental.pallas import tpu as pltpu
 from jax.sharding import PartitionSpec as P
+
 
 MARGIN = 128
 LANES = 128
@@ -50,7 +51,7 @@
     return lax.shift_right_logical(x, size.bit_length() - 1), x & (size - 1)
 
 
-def weights_kernel(cells, regions, live_ref, cell_ref, weight_ref, report_ref, table_ref, source_ref):
+def weights_kernel(cells, regions, live_ref, cell_ref, weight_ref, report_ref, table_ref, place_ref, flip_ref):
     region = lax.axis_index("region")
     bits = regions.bit_length() - 1
     points, slots = weight_ref.shape[1:]
@@ -71,8 +72,8 @@
             bit = (distance >> k) & 1
             place = place + (bit << (bits - 1 - k))
             flip = flip ^ bit
-        source_ref[j] = place
-        source_ref[2 + j] = flip
+        place_ref[j : j + 1, :] = jnp.full((1, LANES), place, jnp.int32)
+        flip_ref[j] = flip
     high = jnp.where(outside, jnp.where(holder == first, rows - 2, rows - 1), block)
     active = lax.broadcasted_iota(jnp.int32, (1, slots), 1) < live_ref[0]
     weights = jnp.where(active, weight_ref[0], 0.0)
@@ -86,13 +87,15 @@
     table_ref[...] = total.reshape(rows, 2 * points, LANES)
 
 
-def pick_kernel(source_ref, near_ref, far_ref, out_ref):
+def pick_kernel(place_ref, near_ref, far_ref, out_ref):
     count = near_ref.shape[0]
     for j in range(2):
-        place = source_ref[j]
-        inside = jnp.minimum(place, count - 1)
-        outside = jnp.maximum(place - count, 0)
-        out_ref[j] = jnp.where(place < count, near_ref[inside], far_ref[outside])
+        place = jnp.broadcast_to(place_ref[j : j + 1, :], near_ref.shape[1:])
+        chosen = jnp.zeros(near_ref.shape[1:], f32)
+        for ref, base in ((near_ref, 0), (far_ref, count)):
+            for i in range(count):
+                chosen = jnp.where(place == base + i, ref[i].astype(f32), chosen)
+        out_ref[j] = chosen.astype(bf16)
 
 
 def anomaly_kernel(offsets, *refs):
@@ -111,7 +114,7 @@
 
 
 def products_kernel(anomaly_ref, mean_ref, table_ref, products_ref, forcing_ref):
-    members, cells = anomaly_ref.shape
+    _, cells = anomaly_ref.shape
     points = products_ref.shape[0]
     chunk = min(cells, 2048)
     forcing = None
@@ -225,7 +228,7 @@
     return [jnp.concatenate(parts, axis=0) for parts in sums]
 
 
-def transform_kernel(offsets, source_ref, *refs):
+def transform_kernel(offsets, flip_ref, *refs):
     count = len(offsets)
     pieces = refs[:count]
     (
@@ -248,7 +251,7 @@
     last = table_ref.shape[0]
     for offset, piece in zip(offsets, pieces):
         for j in range(2):
-            start = pl.multiple_of((member ^ offset ^ source_ref[2 + j]) * rows, rows)
+            start = pl.multiple_of((member ^ offset ^ flip_ref[j]) * rows, rows)
             margin_ref[pl.ds(start, rows), j * LANES : (j + 1) * LANES] = piece[j]
     values = margin_ref[...].astype(f32)
     mean = jnp.sum(values, axis=0, keepdims=True) / members
@@ -266,14 +269,6 @@
     def plus(scalar, matrix):
         return matrix + jnp.where(identity, scalar, 0.0)
 
-    def left(x):
-        high, low = split(x)
-        return jnp.concatenate([high, high, low], axis=1)
-
-    def right(x):
-        high, low = split(x)
-        return jnp.concatenate([high, low, high], axis=0)
-
     span = range(points)
     matrix, scale = [], []
     for a in span:
@@ -283,25 +278,38 @@
         frobenius = jnp.sqrt(square)
         matrix.append(full / frobenius)
         scale.append(1.0 / jnp.sqrt(frobenius))
-    matrix_left = [left(x) for x in matrix]
-    squared = [dot_nn(matrix_left[a], right(matrix[a])) for a in span]
+    low = [x.astype(bf16) for x in matrix]
+    squared = [dot_nn(x, x) for x in low]
     root = [
-        plus(2.25, -2.4375 * matrix[a])
+        1.6875 * squared[a]
+        - 2.4375 * matrix[a]
         + dot_nn(
-            left(squared[a]),
-            right(plus(1.6875, 0.0625 * squared[a] - 0.5625 * matrix[a])),
+            squared[a].astype(bf16), (0.0625 * squared[a] - 0.5625 * matrix[a]).astype(bf16)
         )
         for a in span
     ]
-    current = [dot_nn(matrix_left[a], right(root[a])) for a in span]
-    root_left = [left(x) for x in root]
-    middle = [plus(1.5, -0.5 * dot_nn(root_left[a], right(current[a]))) for a in span]
-    middle_right = [right(x) for x in middle]
-    current = [dot_nn(left(current[a]), middle_right[a]) for a in span]
-    root = [dot_nn(root_left[a], middle_right[a]) for a in span]
-    root_left = [left(x) for x in root]
-    middle = [plus(1.5, -0.5 * dot_nn(root_left[a], right(current[a]))) for a in span]
-    root = [dot_nn(root_left[a], right(middle[a])) for a in span]
+    root_low = [x.astype(bf16) for x in root]
+    current = [2.25 * matrix[a] + dot_nn(low[a], root_low[a]) for a in span]
+    current_low = [x.astype(bf16) for x in current]
+    middle = [
+        plus(0.125, -1.125 * current[a] - 0.5 * dot_nn(root_low[a], current_low[a])) for a in span
+    ]
+    middle_low = [x.astype(bf16) for x in middle]
+    root = [
+        plus(0.34375, 1.375 * root[a] + 2.25 * middle[a] + dot_nn(root_low[a], middle_low[a]))
+        for a in span
+    ]
+    current = [1.375 * current[a] + dot_nn(current_low[a], middle_low[a]) for a in span]
+    root_low = [x.astype(bf16) for x in root]
+    middle = [
+        plus(0.25, -1.375 * current[a] - 0.5 * dot_nn(root_low[a], current[a].astype(bf16)))
+        for a in span
+    ]
+    root = [
+        plus(3.4375, 1.25 * root[a] + 2.75 * middle[a])
+        + dot_nn(root_low[a], middle[a].astype(bf16))
+        for a in span
+    ]
     for a in span:
         inverse = root[a] * scale[a]
         inner = jnp.sum(inverse * forcing[:, a : a + 1], axis=0, keepdims=True)
@@ -345,129 +353,124 @@
     region_bits = regions.bit_length() - 1
     member_bits = groups.bit_length() - 1
 
-    def swap(name, x, mask):
-        with jax.named_scope(name):
-            return lax.ppermute(x, AXES, [(i, i ^ mask) for i in range(devices)])
+    def swap(x, mask):
+        return lax.ppermute(x, AXES, [(i, i ^ mask) for i in range(devices)])
 
     def across(i):
         position = i % groups
-        other = (position + 1 if position % 2 else position - 1) % groups
-        return i - position + other
-
-    def cross(name, x):
-        with jax.named_scope(name):
-            return lax.ppermute(x, AXES, [(i, across(i)) for i in range(devices)])
+        if position in (0, groups - 1):
+            return (i + groups * (1 - 2 * (i // groups % 2))) if regions > 1 else i
+        return i + (1 if position % 2 else -1)
+
+    def cross(x):
+        return lax.ppermute(x, AXES, [(i, across(i)) for i in range(devices)])
 
     member_masks = [(1 << k) | 1 for k in range(member_bits - 1, 0, -1)] + [1]
 
     table_rows = cell_count // LANES + 2
-    with jax.named_scope("kernel_weights"):
-        table, sources = call(
-            functools.partial(weights_kernel, cell_count, regions),
-            [((table_rows, 2 * points, LANES), f32), ((4,), jnp.int32)],
-            (report_count, report_cell, report_weight, reports),
-            4 * table_rows * 2 * points * slots * LANES,
-            100000,
-            smem_in=1,
-            smem_out=1,
-        )
+    table, places, flips = call(
+        functools.partial(weights_kernel, cell_count, regions),
+        [
+            ((table_rows, 2 * points, LANES), f32),
+            ((2, LANES), jnp.int32),
+            ((2,), jnp.int32),
+        ],
+        (report_count, report_cell, report_weight, reports),
+        4 * table_rows * 2 * points * slots * LANES,
+        100000,
+        smem_in=1,
+        smem_out=1,
+    )
 
     near = ensemble[:, :MARGIN][None]
-    for step, k in enumerate(range(region_bits - 1, -1, -1)):
-        far = swap(f"margin_{step}", near, (groups << k) | 1)
+    for k in range(region_bits - 1, -1, -1):
+        far = swap(near, (groups << k) | 1)
         if k:
             near = jnp.concatenate([near, far], axis=0)
-    with jax.named_scope("kernel_pick"):
-        (picked,) = call(
-            pick_kernel,
-            [((2, local_members, MARGIN), bf16)],
-            (sources, near, far),
-            0,
-            100000,
-            smem_in=1,
-        )
+    (picked,) = call(
+        pick_kernel,
+        [((2, local_members, MARGIN), bf16)],
+        (places, near, far),
+        0,
+        100000,
+    )
     margins = [picked]
     for step, mask in enumerate(member_masks):
         if step == 0:
-            margins = margins + [swap("spread_0", picked, mask)]
+            margins = margins + [swap(picked, mask)]
         else:
-            joined = swap(f"spread_{step}", jnp.concatenate(margins, axis=0), mask)
+            joined = swap(jnp.concatenate(margins, axis=0), mask)
             margins = margins + [joined[2 * i : 2 * i + 2] for i in range(len(margins))]
 
     pieces, offsets = [ensemble], [0]
-    for step, mask in enumerate(member_masks):
-        pieces = pieces + [swap(f"whole_{step}_{i}", x, mask) for i, x in enumerate(pieces)]
+    for mask in member_masks:
+        pieces = pieces + [swap(x, mask) for x in pieces]
         offsets = offsets + [offset ^ mask for offset in offsets]
-    partner_blending = swap("blend_partner", blending, 1)
-    other_blending = cross("blend_other", blending)
-
-    with jax.named_scope("kernel_anomaly"):
-        anomaly, mean = call(
-            functools.partial(anomaly_kernel, tuple(offsets)),
-            [((members, cell_count), bf16), ((1, cell_count), f32)],
-            tuple(pieces),
-            4 * members * cell_count,
-            4 * members * cell_count,
-        )
-    with jax.named_scope("kernel_products"):
-        products, forcing = call(
-            products_kernel,
-            [((points, members, members), f32), ((2 * points, members), f32)],
-            (anomaly, mean, table),
-            2 * points * members * members * cell_count,
-            2 * members * cell_count + 4 * points * members * members,
-        )
+    partner_blending = swap(blending, 1)
+    other_blending = cross(blending)
+
+    anomaly, mean = call(
+        functools.partial(anomaly_kernel, tuple(offsets)),
+        [((members, cell_count), bf16), ((1, cell_count), f32)],
+        tuple(pieces),
+        4 * members * cell_count,
+        4 * members * cell_count,
+    )
+    products, forcing = call(
+        products_kernel,
+        [((points, members, members), f32), ((2 * points, members), f32)],
+        (anomaly, mean, table),
+        2 * points * members * members * cell_count,
+        2 * members * cell_count + 4 * points * members * members,
+    )
     padded = points + -points % 8
-    with jax.named_scope("kernel_cells"):
-        own_cells, first_cells, second_cells, own_mix, first_mix, second_mix, column = call(
-            functools.partial(cells_kernel, groups, points),
-            [
-                ((slab, members), bf16),
-                ((slab, members), bf16),
-                ((half, members), bf16),
-                ((slab, padded), f32),
-                ((slab, padded), f32),
-                ((half, padded), f32),
-                ((slab, 8), f32),
-            ],
-            (anomaly, mean, blending, partner_blending, other_blending),
-            3 * slab * members,
-            8 * slab * members,
-        )
-    with jax.named_scope("kernel_transform"):
-        transform, to_first, to_second = call(
-            functools.partial(transform_kernel, tuple(offsets)),
-            [
-                ((points, members, members), bf16),
-                ((slab, members), bf16),
-                ((half, members), bf16),
-            ],
-            (
-                sources,
-                *margins,
-                table,
-                products,
-                forcing,
-                first_cells,
-                second_cells,
-                first_mix,
-                second_mix,
-            ),
-            2 * 26 * points * members**3,
-            8 * points * members * members,
-            smem_in=1,
-            scratch=[pltpu.VMEM((members, 2 * LANES), bf16)],
-        )
-    from_other = cross("back_other", to_second)
-    from_partner = swap("back_partner", to_first, 1)
-    with jax.named_scope("kernel_own"):
-        (own,) = call(
-            own_kernel,
-            [((slab, members), f32)],
-            (transform, own_cells, own_mix, column),
-            4 * slab * members * members,
-            8 * slab * members,
-        )
+    own_cells, first_cells, second_cells, own_mix, first_mix, second_mix, column = call(
+        functools.partial(cells_kernel, groups, points),
+        [
+            ((slab, members), bf16),
+            ((slab, members), bf16),
+            ((half, members), bf16),
+            ((slab, padded), f32),
+            ((slab, padded), f32),
+            ((half, padded), f32),
+            ((slab, 8), f32),
+        ],
+        (anomaly, mean, blending, partner_blending, other_blending),
+        3 * slab * members,
+        8 * slab * members,
+    )
+    transform, to_first, to_second = call(
+        functools.partial(transform_kernel, tuple(offsets)),
+        [
+            ((points, members, members), bf16),
+            ((slab, members), bf16),
+            ((half, members), bf16),
+        ],
+        (
+            flips,
+            *margins,
+            table,
+            products,
+            forcing,
+            first_cells,
+            second_cells,
+            first_mix,
+            second_mix,
+        ),
+        2 * 26 * points * members**3,
+        8 * points * members * members,
+        smem_in=1,
+        scratch=[pltpu.VMEM((members, 2 * LANES), bf16)],
+    )
+    from_other = cross(to_second)
+    from_partner = swap(to_first, 1)
+    (own,) = call(
+        own_kernel,
+        [((slab, members), f32)],
+        (transform, own_cells, own_mix, column),
+        4 * slab * members * members,
+        8 * slab * members,
+    )
     odd = lax.axis_index("member") % 2
     upper = jnp.where(odd == 0, from_other.astype(f32), 0.0)
     lower = jnp.where(odd == 1, from_other.astype(f32), 0.0)

time: 34.9 us -> 32.2 us (0.923)
  Pallas kernels: 9.6 us -> 7.49 us
  waiting for transfers between devices: 7.5 us -> 6.93 us
    pallas_call x7, Pallas kernels: 9.6 us -> 7.49 us  [call(): pl.pallas_call(kernel, out_shape=[jax.ShapeDtypeStruct(s, d) for s, d in...]
    ppermute x2, waiting for transfers between devices: 3.85 us -> 3.27 us  [cross(): return lax.ppermute(x, AXES, [(i, across(i)) for i in range(devices)])]
    ppermute x2, starting transfers between devices: 2.76 us -> 3.17 us  [cross(): return lax.ppermute(x, AXES, [(i, across(i)) for i in range(devices)])]
    ppermute x10, starting transfers between devices: 12.4 us -> 12.1 us  [swap(): return lax.ppermute(x, AXES, [(i, i ^ mask) for i in range(devices)])]
  transfers between devices with their start and end apart: 12 -> 12, of which waited for: 5 -> 5; matrix products, arithmetic and copies ran while one was open for 0% -> 0% of each run, Pallas kernels for 12% -> 11%
where the time goes in v3:
time: 32.2 us; the launch traced here: 32.1 us
  starting transfers between devices  15.2 us (47%)
  Pallas kernels  7.49 us (23%)
  waiting for transfers between devices  6.93 us (22%)
  other arithmetic  0.85 us (3%)
  between operations  0.82 us (3%)
  local copies, waits for them, and re-layouts  0.75 us (2%)
    ppermute x10, starting transfers between devices, swap(): return lax.ppermute(x, AXES, [(i, i ^ mask) for i in range(devices)])  12.1 us
    pallas_call x7, Pallas kernels, call(): pl.pallas_call(kernel, out_shape=[jax.ShapeDtypeStruct(s, d) for s, d in...  7.49 us
    ppermute x10, waiting for transfers between devices, swap(): return lax.ppermute(x, AXES, [(i, i ^ mask) for i in range(devices)])  3.65 us
    ppermute x2, waiting for transfers between devices, cross(): return lax.ppermute(x, AXES, [(i, across(i)) for i in range(devices)])  3.27 us
    ppermute x2, starting transfers between devices, cross(): return lax.ppermute(x, AXES, [(i, across(i)) for i in range(devices)])  3.17 us
    convert_element_type x1, other arithmetic, per_device(): return total.astype(bf16)  0.79 us
    broadcast_in_dim x1, local copies, waits for them, and re-layouts, per_device(): near = ensemble[:, :MARGIN][None]  0.72 us
  transfers between devices with their start and end apart: 12, of which 5 were waited for; matrix products, arithmetic and copies ran while one was open for 0% of the time, Pallas kernels for 11%

profile of v3, /device:TPU:0, one launch (start us, length us, event | category | flops | bytes accessed | tf_op | source)
XLA Modules:
  0.0 32.1 jit_solution(1203103159459175110)
XLA Ops:
  0.0 0.7 %slice_bitcast_fusion = bf16[1,64,128]{2,1,0:T(8,128)(2,1)S(1)} fusion(bf16[64,2048]{1,0:T(8,128)(2,1)} %refs_0_.1), kind=kLoop, calls=%fused_computation.7 | loop fusion | bytes 32768 | tf_op jit(solution)/shard_map/broadcast_in_dim | solution.py:385
  0.7 3.5 %collective-permute-start = (bf16[1,64,128]{2,1,0:T(8,128)(2,1)S(1)}, bf16[1,64,128]{2,1,0:T(8,128)(2,1)S(1)}, u32[]{:S(2)}, u32[]{:S(2)}) collective-permute-start(bf16[1,64,128]{2,1,0:T(8,128)(2,1)S(1)} %slice_bitcast_fusion), channel_id=1, source_target_pairs={{0,17},{1,16},{2,19},{3,18},{4,21},{5,20},{6,23},{7,22},{8,25},{9,... | collective-permute-start | bytes 49160 | tf_op jit(solution)/shard_map/ppermute | solution.py:357
  4.2 1.4 %collective-permute-done = bf16[1,64,128]{2,1,0:T(8,128)(2,1)S(1)} collective-permute-done((bf16[1,64,128]{2,1,0:T(8,128)(2,1)S(1)}, bf16[1,64,128]{2,1,0:T(8,128)(2,1)S(1)}, u32[]{:S(2)}, u32[]{:S(2)}) %collective-permute-start) | collective-permute-done | bytes 16416 | tf_op jit(solution)/shard_map/ppermute | solution.py:357
  5.7 0.0 copy-start.2
  5.7 0.0 copy-start.3
  5.7 0.0 copy-start.4
  5.7 2.0 %collective-permute-start.1 = (bf16[2,64,128]{2,1,0:T(8,128)(2,1)S(1)}, bf16[2,64,128]{2,1,0:T(8,128)(2,1)S(1)}, u32[]{:S(2)}, u32[]{:S(2)}) collective-permute-start(bf16[2,64,128]{2,1,0:T(8,128)(2,1)S(1)} %pad_maximum_fusion.2), channel_id=1, source_target_pairs={{0,9},{1,8},{2,11},{3,10},{4,13},{5,12},{6,15},{7,14},{8,1},{9,0},... | collective-permute-start | bytes 98312 | tf_op jit(solution)/shard_map/ppermute | solution.py:357
  7.6 1.5 %collective-permute-start.5 = (bf16[64,2048]{1,0:T(8,128)(2,1)}, bf16[64,2048]{1,0:T(8,128)(2,1)S(1)}, u32[]{:S(2)}, u32[]{:S(2)}) collective-permute-start(bf16[64,2048]{1,0:T(8,128)(2,1)} %refs_0_.1), channel_id=1, source_target_pairs={{0,3},{1,2},{2,1},{3,0},{4,7},{5,6},{6,5},{7,4},{8,11},{9,10},{10,... | collective-permute-start | bytes 786440 | tf_op jit(solution)/shard_map/ppermute | solution.py:357
  9.1 0.1 collective-permute-done.1
  9.3 1.8 %collective-permute-start.2 = (bf16[4,64,128]{2,1,0:T(8,128)(2,1)S(1)}, bf16[4,64,128]{2,1,0:T(8,128)(2,1)S(1)}, u32[]{:S(2)}, u32[]{:S(2)}) collective-permute-start(bf16[4,64,128]{2,1,0:T(8,128)(2,1)S(1)} %pad_maximum_fusion.near_ref), channel_id=1, source_target_pairs={{0,5},{1,4},{2,7},{3,6},{4,1},{5,0},{6,3},{7,2},{8,13},{9,12},{10,... | collective-permute-start | bytes 196616 | tf_op jit(solution)/shard_map/ppermute | solution.py:357
  11.7 0.0 copy-done.2
  11.7 0.0 copy-done.3
  11.7 0.0 copy-done.4
  11.7 0.0 copy-start
  11.8 1.0 %shard_map.64 = (f32[18,8,128]{2,1,0:T(8,128)S(1)}, s32[2,128]{1,0:T(2,128)S(1)}, s32[2]{0:T(128)S(1)}) custom-call(s32[1]{0:T(128)S(6)} %copy.7.live_ref, s32[1,1024]{1,0:T(1,128)S(1)} %copy-done.3, f32[1,4,1024]{2,1,0:T(4,128)S(1)} %copy-done.2, f32[1,1024]{1,0:T(1,128)S(1)} %copy-done.4), custom_call_target="tpu_custom_call" | custom-call | flops 75497472 | bytes 100000 | tf_op jit(solution)/shard_map/pallas_call | solution.py:37
  12.8 0.5 %collective-permute-done.2.far_ref = bf16[4,64,128]{2,1,0:T(8,128)(2,1)S(1)} collective-permute-done((bf16[4,64,128]{2,1,0:T(8,128)(2,1)S(1)}, bf16[4,64,128]{2,1,0:T(8,128)(2,1)S(1)}, u32[]{:S(2)}, u32[]{:S(2)}) %collective-permute-start.2) | collective-permute-done | bytes 65568 | tf_op jit(solution)/shard_map/ppermute | solution.py:357
  13.3 0.0 copy-start.1
  13.3 2.2 %collective-permute-start.3 = (bf16[2,64,128]{2,1,0:T(8,128)(2,1)S(1)}, bf16[2,64,128]{2,1,0:T(8,128)(2,1)S(1)}, u32[]{:S(2)}, u32[]{:S(2)}) collective-permute-start(bf16[2,64,128]{2,1,0:T(8,128)(2,1)S(1)} %shard_map.65.refs_0_), channel_id=1, source_target_pairs={{0,3},{1,2},{2,1},{3,0},{4,7},{5,6},{6,5},{7,4},{8,11},{9,10},{10,... | collective-permute-start | bytes 98312 | tf_op jit(solution)/shard_map/ppermute | solution.py:357
  15.5 1.6 %collective-permute-done.3.refs_1_ = bf16[2,64,128]{2,1,0:T(8,128)(2,1)S(1)} collective-permute-done((bf16[2,64,128]{2,1,0:T(8,128)(2,1)S(1)}, bf16[2,64,128]{2,1,0:T(8,128)(2,1)S(1)}, u32[]{:S(2)}, u32[]{:S(2)}) %collective-permute-start.3) | collective-permute-done | bytes 32800 | tf_op jit(solution)/shard_map/ppermute | solution.py:357
  17.2 0.2 collective-permute-start.4
  17.4 0.0 copy-done
  17.4 0.4 %collective-permute-start.6 = (bf16[64,2048]{1,0:T(8,128)(2,1)S(1)}, bf16[64,2048]{1,0:T(8,128)(2,1)S(1)}, u32[]{:S(2)}, u32[]{:S(2)}) collective-permute-start(bf16[64,2048]{1,0:T(8,128)(2,1)S(1)} %copy-done), channel_id=1, source_target_pairs={{0,1},{1,0},{2,3},{3,2},{4,5},{5,4},{6,7},{7,6},{8,9},{9,8},{10,11... | collective-permute-start | bytes 786440 | tf_op jit(solution)/shard_map/ppermute | solution.py:357
  17.8 0.0 collective-permute-done.5.refs_1_
  17.8 0.2 collective-permute-start.7
  17.9 0.0 copy-done.1
  17.9 0.4 %collective-permute-start.8 = (f32[4,512]{1,0:T(4,128)S(1)}, f32[4,512]{1,0:T(4,128)S(1)}, u32[]{:S(2)}, u32[]{:S(2)}) collective-permute-start(f32[4,512]{1,0:T(4,128)S(1)} %copy-done.1), channel_id=1, source_target_pairs={{0,1},{1,0},{2,3},{3,2},{4,5},{5,4},{6,7},{7,6},{8,9},{9,8},{10,11... | collective-permute-start | bytes 24584 | tf_op jit(solution)/shard_map/ppermute | solution.py:357
  18.3 1.7 %collective-permute-start.9 = (f32[4,512]{1,0:T(4,128)S(1)}, f32[4,512]{1,0:T(4,128)S(1)}, u32[]{:S(2)}, u32[]{:S(2)}) collective-permute-start(f32[4,512]{1,0:T(4,128)S(1)} %copy-done.1), channel_id=1, source_target_pairs={{0,4},{1,2},{2,1},{3,7},{4,0},{5,6},{6,5},{7,3},{8,12},{9,10},{10,... | collective-permute-start | bytes 24584 | tf_op jit(solution)/shard_map/ppermute | solution.py:366
  20.0 0.0 collective-permute-done.4
  20.0 0.0 collective-permute-done.6.refs_2_
  20.0 0.0 collective-permute-done.7.refs_3_
  20.0 0.4 %shard_map.66 = (bf16[256,2048]{1,0:T(8,128)(2,1)S(1)}, f32[1,2048]{1,0:T(1,128)S(1)}) custom-call(bf16[64,2048]{1,0:T(8,128)(2,1)S(1)} %copy-done, bf16[64,2048]{1,0:T(8,128)(2,1)S(1)} %collective-permute-done.5.refs_1_, bf16[64,2048]{1,0:T(8,128)(2,1)S(1)} %collective-permute-done.6.refs_2_, bf16[64,2048]{1,0:T(8,128)(2,1)S(1)} %collective-permute-done.7.refs_3_), custom_call_target="tpu_custom_call" | custom-call | flops 2097152 | bytes 2097152 | tf_op jit(solution)/shard_map/pallas_call | solution.py:37
  20.5 1.8 %shard_map.67 = (f32[4,256,256]{2,1,0:T(8,128)S(1)}, f32[8,256]{1,0:T(8,128)S(1)}) custom-call(bf16[256,2048]{1,0:T(8,128)(2,1)S(1)} %get-tuple-element.25.anomaly_ref, f32[1,2048]{1,0:T(1,128)S(1)} %get-tuple-element.26.mean_ref, f32[18,8,128]{2,1,0:T(8,128)S(1)} %get-tuple-element.24.table_ref.refs_4_), custom_call_target="tpu_custom_call" | custom-call | flops 1073741824 | bytes 2097152 | tf_op jit(solution)/shard_map/pallas_call | solution.py:37
  22.2 0.0 collective-permute-done.8.first_blend
  22.3 0.0 collective-permute-done.9.second_blend
  22.3 0.5 %shard_map.68 = (bf16[512,256]{1,0:T(8,128)(2,1)S(1)}, bf16[512,256]{1,0:T(8,128)(2,1)S(1)}, bf16[256,256]{1,0:T(8,128)(2,1)S(1)}, f32[512,8]{1,0:T(8,128)S(1)},...) custom-call(bf16[256,2048]{1,0:T(8,128)(2,1)S(1)} %get-tuple-element.25.anomaly_ref, ...), custom_call_target="tpu_custom_call" | custom-call | flops 393216 | bytes 1048576 | tf_op jit(solution)/shard_map/pallas_call | solution.py:37
  22.8 3.4 %shard_map.69 = (bf16[4,256,256]{2,1,0:T(8,128)(2,1)S(1)}, bf16[512,256]{1,0:T(8,128)(2,1)S(1)}, bf16[256,256]{1,0:T(8,128)(2,1)S(1)}) custom-call(s32[2]{0:T(128)S(1)} %get-tuple-element.22.flip_ref, bf16[2,64,128]{2,1,0:T(8,128)(2,1)S(1)} %shard_map.65.refs_0_, bf16[2,64,128]{2,1,0:T(8,128)(2,1)S(1)} %collective-permute-done.3.refs_1_, ...), custom_call_target="tpu_custom_call" | custom-call | flops 3489660928 | bytes 2097152 | tf_op jit(solution)/shard_map/pallas_call | solution.py:37
  26.2 1.4 %collective-permute-start.11 = (bf16[256,256]{1,0:T(8,128)(2,1)S(1)}, bf16[256,256]{1,0:T(8,128)(2,1)S(1)}, u32[]{:S(2)}, u32[]{:S(2)}) collective-permute-start(bf16[256,256]{1,0:T(8,128)(2,1)S(1)} %get-tuple-element.38), channel_id=1, source_target_pairs={{0,4},{1,2},{2,1},{3,7},{4,0},{5,6},{6,5},{7,3},{8,12},{9,10},{10,... | collective-permute-start | bytes 393224 | tf_op jit(solution)/shard_map/ppermute | solution.py:366
  27.6 0.0 collective-permute-start.10
  27.6 0.3 shard_map.70
  28.0 3.3 %collective-permute-done.11 = bf16[256,256]{1,0:T(8,128)(2,1)S(1)} collective-permute-done((bf16[256,256]{1,0:T(8,128)(2,1)S(1)}, bf16[256,256]{1,0:T(8,128)(2,1)S(1)}, u32[]{:S(2)}, u32[]{:S(2)}) %collective-permute-start.11) | collective-permute-done | bytes 131104 | tf_op jit(solution)/shard_map/ppermute | solution.py:366
  31.3 0.0 collective-permute-done.10
  31.3 0.8 %fusion = bf16[512,256]{1,0:T(8,128)(2,1)} fusion(f32[256,256]{1,0:T(8,128)S(1)} %get-tuple-element.40, f32[256,256]{1,0:T(8,128)S(1)} %get-tuple-element.39, f32[512,256]{1,0:T(8,128)S(1)} %shard_map.70, bf16[512,256]{1,0:T(8,128)(2,1)S(1)} %collective-permute-done.10), kind=kLoop, calls=%fused_computation.1 | loop fusion | flops 655360 | bytes 1572864 | tf_op jit(solution)/shard_map/convert_element_type | solution.py:478
  (6 shorter events, 0.1 us)
Async XLA Ops:
  0.7 4.9 %collective-permute-start = (bf16[1,64,128]{2,1,0:T(8,128)(2,1)S(1)}, bf16[1,64,128]{2,1,0:T(8,128)(2,1)S(1)}, u32[]{:S(2)}, u32[]{:S(2)}) collective-permute-start(bf16[1,64,128]{2,1,0:T(8,128)(2,1)S(1)} %slice_bitcast_fusion), channel_id=1, source_target_pairs={{0,17},{1,16},{2,19},{3,18},{4,21},{5,20},{6,23},{7,22},{8,25},{9,... | collective-permute-start | bytes 49160 | tf_op jit(solution)/shard_map/ppermute | solution.py:357
  5.7 6.0 %copy-start.2 = (f32[1,4,1024]{2,1,0:T(4,128)S(1)}, f32[1,4,1024]{2,1,0:T(4,128)}, u32[]{:S(2)}) copy-start(f32[1,4,1024]{2,1,0:T(4,128)} %weight_ref.1) | copy-start | bytes 49156
  5.7 6.1 %copy-start.3 = (s32[1,1024]{1,0:T(1,128)S(1)}, s32[1,1024]{1,0:T(1,128)}, u32[]{:S(2)}) copy-start(s32[1,1024]{1,0:T(1,128)} %cell_ref.1) | copy-start | bytes 12292
  5.7 6.1 %copy-start.4 = (f32[1,1024]{1,0:T(1,128)S(1)}, f32[1,1024]{1,0:T(1,128)}, u32[]{:S(2)}) copy-start(f32[1,1024]{1,0:T(1,128)} %report_ref.1) | copy-start | bytes 12292
  5.7 3.6 %collective-permute-start.1 = (bf16[2,64,128]{2,1,0:T(8,128)(2,1)S(1)}, bf16[2,64,128]{2,1,0:T(8,128)(2,1)S(1)}, u32[]{:S(2)}, u32[]{:S(2)}) collective-permute-start(bf16[2,64,128]{2,1,0:T(8,128)(2,1)S(1)} %pad_maximum_fusion.2), channel_id=1, source_target_pairs={{0,9},{1,8},{2,11},{3,10},{4,13},{5,12},{6,15},{7,14},{8,1},{9,0},... | collective-permute-start | bytes 98312 | tf_op jit(solution)/shard_map/ppermute | solution.py:357
  7.6 10.1 %collective-permute-start.5 = (bf16[64,2048]{1,0:T(8,128)(2,1)}, bf16[64,2048]{1,0:T(8,128)(2,1)S(1)}, u32[]{:S(2)}, u32[]{:S(2)}) collective-permute-start(bf16[64,2048]{1,0:T(8,128)(2,1)} %refs_0_.1), channel_id=1, source_target_pairs={{0,3},{1,2},{2,1},{3,0},{4,7},{5,6},{6,5},{7,4},{8,11},{9,10},{10,... | collective-permute-start | bytes 786440 | tf_op jit(solution)/shard_map/ppermute | solution.py:357
  9.3 4.0 %collective-permute-start.2 = (bf16[4,64,128]{2,1,0:T(8,128)(2,1)S(1)}, bf16[4,64,128]{2,1,0:T(8,128)(2,1)S(1)}, u32[]{:S(2)}, u32[]{:S(2)}) collective-permute-start(bf16[4,64,128]{2,1,0:T(8,128)(2,1)S(1)} %pad_maximum_fusion.near_ref), channel_id=1, source_target_pairs={{0,5},{1,4},{2,7},{3,6},{4,1},{5,0},{6,3},{7,2},{8,13},{9,12},{10,... | collective-permute-start | bytes 196616 | tf_op jit(solution)/shard_map/ppermute | solution.py:357
  11.7 5.7 %copy-start = (bf16[64,2048]{1,0:T(8,128)(2,1)S(1)}, bf16[64,2048]{1,0:T(8,128)(2,1)}, u32[]{:S(2)}) copy-start(bf16[64,2048]{1,0:T(8,128)(2,1)} %refs_0_.1) | copy-start | bytes 786436
  13.3 4.6 %copy-start.1 = (f32[4,512]{1,0:T(4,128)S(1)}, f32[4,512]{1,0:T(4,128)}, u32[]{:S(2)}) copy-start(f32[4,512]{1,0:T(4,128)} %own_blend.1) | copy-start | bytes 24580
  13.3 3.9 %collective-permute-start.3 = (bf16[2,64,128]{2,1,0:T(8,128)(2,1)S(1)}, bf16[2,64,128]{2,1,0:T(8,128)(2,1)S(1)}, u32[]{:S(2)}, u32[]{:S(2)}) collective-permute-start(bf16[2,64,128]{2,1,0:T(8,128)(2,1)S(1)} %shard_map.65.refs_0_), channel_id=1, source_target_pairs={{0,3},{1,2},{2,1},{3,0},{4,7},{5,6},{6,5},{7,4},{8,11},{9,10},{10,... | collective-permute-start | bytes 98312 | tf_op jit(solution)/shard_map/ppermute | solution.py:357
  17.2 2.8 %collective-permute-start.4 = (bf16[4,64,128]{2,1,0:T(8,128)(2,1)S(1)}, bf16[4,64,128]{2,1,0:T(8,128)(2,1)S(1)}, u32[]{:S(2)}, u32[]{:S(2)}) collective-permute-start(bf16[4,64,128]{2,1,0:T(8,128)(2,1)S(1)} %pad_maximum_fusion.1), channel_id=1, source_target_pairs={{0,1},{1,0},{2,3},{3,2},{4,5},{5,4},{6,7},{7,6},{8,9},{9,8},{10,11... | collective-permute-start | bytes 196616 | tf_op jit(solution)/shard_map/ppermute | solution.py:357
  17.4 2.6 %collective-permute-start.6 = (bf16[64,2048]{1,0:T(8,128)(2,1)S(1)}, bf16[64,2048]{1,0:T(8,128)(2,1)S(1)}, u32[]{:S(2)}, u32[]{:S(2)}) collective-permute-start(bf16[64,2048]{1,0:T(8,128)(2,1)S(1)} %copy-done), channel_id=1, source_target_pairs={{0,1},{1,0},{2,3},{3,2},{4,5},{5,4},{6,7},{7,6},{8,9},{9,8},{10,11... | collective-permute-start | bytes 786440 | tf_op jit(solution)/shard_map/ppermute | solution.py:357
  17.8 2.3 %collective-permute-start.7 = (bf16[64,2048]{1,0:T(8,128)(2,1)S(1)}, bf16[64,2048]{1,0:T(8,128)(2,1)S(1)}, u32[]{:S(2)}, u32[]{:S(2)}) collective-permute-start(bf16[64,2048]{1,0:T(8,128)(2,1)S(1)} %collective-permute-done.5.refs_1_), channel_id=1, source_target_pairs={{0,1},{1,0},{2,3},{3,2},{4,5},{5,4},{6,7},{7,6},{8,9},{9,8},{10,11... | collective-permute-start | bytes 786440 | tf_op jit(solution)/shard_map/ppermute | solution.py:357
  17.9 4.3 %collective-permute-start.8 = (f32[4,512]{1,0:T(4,128)S(1)}, f32[4,512]{1,0:T(4,128)S(1)}, u32[]{:S(2)}, u32[]{:S(2)}) collective-permute-start(f32[4,512]{1,0:T(4,128)S(1)} %copy-done.1), channel_id=1, source_target_pairs={{0,1},{1,0},{2,3},{3,2},{4,5},{5,4},{6,7},{7,6},{8,9},{9,8},{10,11... | collective-permute-start | bytes 24584 | tf_op jit(solution)/shard_map/ppermute | solution.py:357
  18.3 4.0 %collective-permute-start.9 = (f32[4,512]{1,0:T(4,128)S(1)}, f32[4,512]{1,0:T(4,128)S(1)}, u32[]{:S(2)}, u32[]{:S(2)}) collective-permute-start(f32[4,512]{1,0:T(4,128)S(1)} %copy-done.1), channel_id=1, source_target_pairs={{0,4},{1,2},{2,1},{3,7},{4,0},{5,6},{6,5},{7,3},{8,12},{9,10},{10,... | collective-permute-start | bytes 24584 | tf_op jit(solution)/shard_map/ppermute | solution.py:366
  26.2 5.0 %collective-permute-start.11 = (bf16[256,256]{1,0:T(8,128)(2,1)S(1)}, bf16[256,256]{1,0:T(8,128)(2,1)S(1)}, u32[]{:S(2)}, u32[]{:S(2)}) collective-permute-start(bf16[256,256]{1,0:T(8,128)(2,1)S(1)} %get-tuple-element.38), channel_id=1, source_target_pairs={{0,4},{1,2},{2,1},{3,7},{4,0},{5,6},{6,5},{7,3},{8,12},{9,10},{10,... | collective-permute-start | bytes 393224 | tf_op jit(solution)/shard_map/ppermute | solution.py:366
  27.6 3.6 %collective-permute-start.10 = (bf16[512,256]{1,0:T(8,128)(2,1)S(1)}, bf16[512,256]{1,0:T(8,128)(2,1)S(1)}, u32[]{:S(2)}, u32[]{:S(2)}) collective-permute-start(bf16[512,256]{1,0:T(8,128)(2,1)S(1)} %get-tuple-element.37), channel_id=1, source_target_pairs={{0,1},{1,0},{2,3},{3,2},{4,5},{5,4},{6,7},{7,6},{8,9},{9,8},{10,11... | collective-permute-start | bytes 786440 | tf_op jit(solution)/shard_map/ppermute | solution.py:357

commit v4 on v3

--- a/solution.py
+++ b/solution.py
@@ -11,6 +11,8 @@
 MARGIN = 128
 LANES = 128
 GRANT = 20 << 20
+GANG = 2
+LAG = 1
 AXES = ("region", "member")
 
 f32 = jnp.float32
@@ -49,6 +51,11 @@
     if size & (size - 1):
         return lax.div(x, size), lax.rem(x, size)
     return lax.shift_right_logical(x, size.bit_length() - 1), x & (size - 1)
+
+
+def same_position(size):
+    shape = (size, size)
+    return lax.broadcasted_iota(jnp.int32, shape, 0) == lax.broadcasted_iota(jnp.int32, shape, 1)
 
 
 def weights_kernel(cells, regions, live_ref, cell_ref, weight_ref, report_ref, table_ref, place_ref, flip_ref):
@@ -75,7 +82,7 @@
         place_ref[j : j + 1, :] = jnp.full((1, LANES), place, jnp.int32)
         flip_ref[j] = flip
     high = jnp.where(outside, jnp.where(holder == first, rows - 2, rows - 1), block)
-    active = lax.broadcasted_iota(jnp.int32, (1, slots), 1) < live_ref[0]
+    active = lax.broadcasted_iota(jnp.int32, (1, slots), 1) < live_ref[...]
     weights = jnp.where(active, weight_ref[0], 0.0)
     values = jnp.concatenate([weights, weights * report_ref[...]], axis=0)
     low_hot = (lax.broadcasted_iota(jnp.int32, (LANES, slots), 0) == low).astype(f32).astype(bf16)
@@ -113,35 +120,45 @@
         anomaly_ref[pl.ds(start, rows), :] = (piece[...].astype(f32) - mean).astype(bf16)
 
 
-def products_kernel(anomaly_ref, mean_ref, table_ref, products_ref, forcing_ref):
-    _, cells = anomaly_ref.shape
-    points = products_ref.shape[0]
+def products_kernel(chosen, anomaly_ref, mean_ref, table_ref, products_ref, *forcing_ref):
+    members, cells = anomaly_ref.shape
+    points = table_ref.shape[1] // 2
     chunk = min(cells, 2048)
     forcing = None
     for start in range(0, cells, chunk):
         block = anomaly_ref[:, start : start + chunk]
-        departures = []
-        for a in range(points):
-            scaled = []
-            for h in range(start // LANES, (start + chunk) // LANES):
-                lanes = slice(h * LANES, (h + 1) * LANES)
-                scaled.append(
-                    (anomaly_ref[:, lanes].astype(f32) * table_ref[h, a : a + 1, :]).astype(bf16)
-                )
-            part = dot_nt(jnp.concatenate(scaled, axis=1), block)
-            if start == 0:
-                products_ref[a] = part
+        blocks = range(start // LANES, (start + chunk) // LANES)
+        scaled = []
+        for a in chosen:
+            weighted = [
+                anomaly_ref[:, h * LANES : (h + 1) * LANES]
+                * table_ref[h, a : a + 1, :].astype(bf16)
+                for h in blocks
+            ]
+            scaled.append(jnp.concatenate(weighted, axis=1))
+        if forcing_ref:
+            departures = []
+            for h in blocks:
+                tile = table_ref[h]
+                mean = mean_ref[:, h * LANES : (h + 1) * LANES]
+                departures.append(tile[points:, :] - tile[:points, :] * mean)
+            departure = jnp.concatenate(departures, axis=1)
+            first, second = split(jnp.concatenate([departure, departure], axis=0))
+            scaled.append(jnp.concatenate([first, second], axis=0))
+        part = dot_nt(jnp.concatenate(scaled, axis=0), block)
+        for i in range(len(chosen)):
+            rows = part[i * members : (i + 1) * members]
+            if start:
+                products_ref[i] += rows
             else:
-                products_ref[a] += part
-        for h in range(start // LANES, (start + chunk) // LANES):
-            lanes = slice(h * LANES, (h + 1) * LANES)
-            tile = table_ref[h]
-            departures.append(tile[points:, :] - tile[:points, :] * mean_ref[:, lanes])
-        departure = jnp.concatenate(departures, axis=1)
-        first, second = split(jnp.concatenate([departure, departure], axis=0))
-        part = dot_nt(first, block) + dot_nt(second, block)
-        forcing = part if forcing is None else forcing + part
-    forcing_ref[...] = forcing
+                diagonal = jnp.where(same_position(members), members - 1.0, 0.0)
+                products_ref[i] = rows + diagonal
+        if forcing_ref:
+            rest = part[len(chosen) * members :]
+            rest = rest[: 2 * points] + rest[2 * points :]
+            forcing = rest if forcing is None else forcing + rest
+    if forcing_ref:
+        forcing_ref[0][...] = forcing
 
 
 def cells_kernel(
@@ -233,22 +250,22 @@
     pieces = refs[:count]
     (
         table_ref,
-        products_ref,
+        low_products_ref,
+        high_products_ref,
         forcing_ref,
-        first_ref,
         second_ref,
-        first_mix,
         second_mix,
         transform_ref,
-        to_first_ref,
         to_second_ref,
         margin_ref,
     ) = refs[count:]
     member = lax.axis_index("member")
     rows = pieces[0].shape[1]
     members = rows * count
-    points = products_ref.shape[0]
     last = table_ref.shape[0]
+    products_refs = (low_products_ref, high_products_ref)
+    half_points = low_products_ref.shape[0]
+    points = 2 * half_points
     for offset, piece in zip(offsets, pieces):
         for j in range(2):
             start = pl.multiple_of((member ^ offset ^ flip_ref[j]) * rows, rows)
@@ -256,75 +273,80 @@
     values = margin_ref[...].astype(f32)
     mean = jnp.sum(values, axis=0, keepdims=True) / members
     pert = (values - mean).astype(bf16)
-    pert_wide = pert.astype(f32)
     tiles = jnp.concatenate([table_ref[last - 2], table_ref[last - 1]], axis=1)
     departure = tiles[points:, :] - tiles[:points, :] * mean
     first, second = split(jnp.concatenate([departure, departure], axis=0))
     forcing = forcing_ref[...] + dot_nt(first, pert) + dot_nt(second, pert)
     forcing = forcing.T
-    identity = lax.broadcasted_iota(jnp.int32, (members, members), 0) == lax.broadcasted_iota(
-        jnp.int32, (members, members), 1
-    )
-
-    def plus(scalar, matrix):
-        return matrix + jnp.where(identity, scalar, 0.0)
-
-    span = range(points)
-    matrix, scale = [], []
-    for a in span:
-        weighted = (pert_wide * tiles[a : a + 1, :]).astype(bf16)
-        full = plus(members - 1.0, products_ref[a] + dot_nt(weighted, pert))
+
+    def steps(a):
+        weighted = pert * tiles[a : a + 1, :].astype(bf16)
+        full = products_refs[a // half_points][a % half_points] + dot_nt(weighted, pert)
+        yield
         square = jnp.sum(jnp.sum(full * full, axis=0, keepdims=True), axis=1, keepdims=True)
-        frobenius = jnp.sqrt(square)
-        matrix.append(full / frobenius)
-        scale.append(1.0 / jnp.sqrt(frobenius))
-    low = [x.astype(bf16) for x in matrix]
-    squared = [dot_nn(x, x) for x in low]
-    root = [
-        1.6875 * squared[a]
-        - 2.4375 * matrix[a]
-        + dot_nn(
-            squared[a].astype(bf16), (0.0625 * squared[a] - 0.5625 * matrix[a]).astype(bf16)
-        )
-        for a in span
-    ]
-    root_low = [x.astype(bf16) for x in root]
-    current = [2.25 * matrix[a] + dot_nn(low[a], root_low[a]) for a in span]
-    current_low = [x.astype(bf16) for x in current]
-    middle = [
-        plus(0.125, -1.125 * current[a] - 0.5 * dot_nn(root_low[a], current_low[a])) for a in span
-    ]
-    middle_low = [x.astype(bf16) for x in middle]
-    root = [
-        plus(0.34375, 1.375 * root[a] + 2.25 * middle[a] + dot_nn(root_low[a], middle_low[a]))
-        for a in span
-    ]
-    current = [1.375 * current[a] + dot_nn(current_low[a], middle_low[a]) for a in span]
-    root_low = [x.astype(bf16) for x in root]
-    middle = [
-        plus(0.25, -1.375 * current[a] - 0.5 * dot_nn(root_low[a], current[a].astype(bf16)))
-        for a in span
-    ]
-    root = [
-        plus(3.4375, 1.25 * root[a] + 2.75 * middle[a])
-        + dot_nn(root_low[a], middle[a].astype(bf16))
-        for a in span
-    ]
-    for a in span:
-        inverse = root[a] * scale[a]
-        inner = jnp.sum(inverse * forcing[:, a : a + 1], axis=0, keepdims=True)
-        mean_weights = jnp.sum(inverse * inner, axis=1, keepdims=True)
-        transform_ref[a] = (mean_weights + jnp.sqrt(members - 1.0) * inverse).astype(bf16)
-    half = second_ref.shape[0]
+        norm = lax.rsqrt(square)
+        h = full * (norm * (1.0 / 3.0))
+        h_low = h.astype(bf16)
+        yield
+        w = h - dot_nn(h_low, h_low)
+        w_more = 2.25 * w
+        e = h + w_more
+        w_low = w.astype(bf16)
+        yield
+        e = dot_nn(w_more.astype(bf16), h_low + w_low) - e
+        e_low = e.astype(bf16)
+        yield
+        y = 5.0625 * (h + dot_nn(h_low, e_low))
+        y_low = y.astype(bf16)
+        yield
+        g = y + dot_nn(e_low, y_low)
+        g_low = g.astype(bf16)
+        e = e - g
+        yield
+        both = dot_nn(jnp.concatenate([y_low, e_low], axis=0), g_low)
+        y = 2.25 * (y - both[:members])
+        y_low = y.astype(bf16)
+        e = e - both[members:]
+        e_low = e.astype(bf16)
+        yield
+        g = y + dot_nn(e_low, y_low)
+        g_low = g.astype(bf16)
+        e = e - g
+        yield
+        e = e - dot_nn(g_low, e_low)
+        e = e + identity
+        scale = 5.0625 * jnp.sqrt(norm)
+        inner = jnp.sum(e * forcing[:, a : a + 1], axis=0, keepdims=True)
+        outer = jnp.sum(e * inner, axis=1, keepdims=True)
+        yield
+        transform_ref[a] = (
+            scale * scale * outer + (jnp.sqrt(members - 1.0) * scale) * e
+        ).astype(bf16)
+
+    identity = jnp.where(same_position(members), 1.0, 0.0)
+    running = [steps(a) for a in range(points)]
+    tick = 0
+    while any(running):
+        for a in range(points):
+            if running[a] and tick >= LAG * (a // GANG) and next(running[a], True):
+                running[a] = None
+        tick += 1
+    (part,) = blended_parts(
+        [(second_ref[...], second_mix[...])], lambda q: transform_ref[q], points
+    )
+    to_second_ref[...] = part.astype(bf16)
+
+
+def partner_kernel(transform_ref, first_ref, first_mix, to_first_ref):
+    points = transform_ref.shape[0]
+    half = first_ref.shape[0] // 2
     segments = [
         (first_ref[0:half, :], first_mix[0:half, :]),
         (first_ref[half:, :], first_mix[half:, :]),
-        (second_ref[...], second_mix[...]),
     ]
     parts = blended_parts(segments, lambda q: transform_ref[q], points)
-    to_first_ref[0:half, :] = parts[0].astype(bf16)
-    to_first_ref[half:, :] = parts[1].astype(bf16)
-    to_second_ref[...] = parts[2].astype(bf16)
+    for u in range(2):
+        to_first_ref[u * half : (u + 1) * half, :] = parts[u].astype(bf16)
 
 
 def own_kernel(transform_ref, own_ref, own_mix, column_ref, out_ref):
@@ -375,10 +397,9 @@
             ((2, LANES), jnp.int32),
             ((2,), jnp.int32),
         ],
-        (report_count, report_cell, report_weight, reports),
+        (report_count[None], report_cell, report_weight, reports),
         4 * table_rows * 2 * points * slots * LANES,
         100000,
-        smem_in=1,
         smem_out=1,
     )
 
@@ -407,7 +428,11 @@
         pieces = pieces + [swap(x, mask) for x in pieces]
         offsets = offsets + [offset ^ mask for offset in offsets]
     partner_blending = swap(blending, 1)
-    other_blending = cross(blending)
+    other_blending = lax.ppermute(
+        blending,
+        "member",
+        [(i, (i + (1 if i % 2 else -1)) % groups) for i in range(groups)],
+    )
 
     anomaly, mean = call(
         functools.partial(anomaly_kernel, tuple(offsets)),
@@ -416,13 +441,18 @@
         4 * members * cell_count,
         4 * members * cell_count,
     )
-    products, forcing = call(
-        products_kernel,
-        [((points, members, members), f32), ((2 * points, members), f32)],
-        (anomaly, mean, table),
-        2 * points * members * members * cell_count,
-        2 * members * cell_count + 4 * points * members * members,
-    )
+    products = []
+    for part in range(2):
+        chosen = range(part * points // 2, (part + 1) * points // 2)
+        outs = [((len(chosen), members, members), f32)]
+        products += call(
+            functools.partial(products_kernel, tuple(chosen)),
+            outs + ([] if part else [((2 * points, members), f32)]),
+            (anomaly, mean, table),
+            points * members * members * cell_count,
+            2 * members * cell_count + 2 * points * members * members,
+        )
+    low_products, forcing, high_products = products
     padded = points + -points % 8
     own_cells, first_cells, second_cells, own_mix, first_mix, second_mix, column = call(
         functools.partial(cells_kernel, groups, points),
@@ -439,30 +469,23 @@
         3 * slab * members,
         8 * slab * members,
     )
-    transform, to_first, to_second = call(
+    transform, to_second = call(
         functools.partial(transform_kernel, tuple(offsets)),
-        [
-            ((points, members, members), bf16),
-            ((slab, members), bf16),
-            ((half, members), bf16),
-        ],
-        (
-            flips,
-            *margins,
-            table,
-            products,
-            forcing,
-            first_cells,
-            second_cells,
-            first_mix,
-            second_mix,
-        ),
-        2 * 26 * points * members**3,
+        [((points, members, members), bf16), ((half, members), bf16)],
+        (flips, *margins, table, low_products, high_products, forcing, second_cells, second_mix),
+        2 * 10 * points * members**3,
         8 * points * members * members,
         smem_in=1,
         scratch=[pltpu.VMEM((members, 2 * LANES), bf16)],
     )
     from_other = cross(to_second)
+    (to_first,) = call(
+        partner_kernel,
+        [((slab, members), bf16)],
+        (transform, first_cells, first_mix),
+        4 * slab * members * members,
+        8 * slab * members,
+    )
     from_partner = swap(to_first, 1)
     (own,) = call(
         own_kernel,

time: 32.2 us -> 31.7 us (0.984)
  waiting for transfers between devices: 6.93 us -> 6.37 us
    ppermute x0 -> x1, starting transfers between devices: none -> 1.72 us  [per_device(): lax.ppermute(blending, 'member', [(i, (i + (1 if i % 2 else -1)) % groups...]
    ppermute x2 -> x1, starting transfers between devices: 3.17 us -> 1.58 us  [cross(): return lax.ppermute(x, AXES, [(i, across(i)) for i in range(devices)])]
    ppermute x2 -> x1, waiting for transfers between devices: 3.27 us -> 2.72 us  [cross(): return lax.ppermute(x, AXES, [(i, across(i)) for i in range(devices)])]
    pallas_call x7 -> x9, Pallas kernels: 7.49 us -> 7.24 us  [call(): pl.pallas_call(kernel, out_shape=[jax.ShapeDtypeStruct(s, d) for s, d in...]
where the time goes in v4:
time: 31.7 us; the launch traced here: 31.5 us
  starting transfers between devices  15.5 us (49%)
  Pallas kernels  7.24 us (23%)
  waiting for transfers between devices  6.37 us (20%)
  other arithmetic  0.85 us (3%)
  between operations  0.85 us (3%)
  local copies, waits for them, and re-layouts  0.75 us (2%)
    ppermute x10, starting transfers between devices, swap(): return lax.ppermute(x, AXES, [(i, i ^ mask) for i in range(devices)])  12.1 us
    pallas_call x9, Pallas kernels, call(): pl.pallas_call(kernel, out_shape=[jax.ShapeDtypeStruct(s, d) for s, d in...  7.24 us
    ppermute x10, waiting for transfers between devices, swap(): return lax.ppermute(x, AXES, [(i, i ^ mask) for i in range(devices)])  3.65 us
    ppermute x1, waiting for transfers between devices, cross(): return lax.ppermute(x, AXES, [(i, across(i)) for i in range(devices)])  2.72 us
    ppermute x1, starting transfers between devices, per_device(): lax.ppermute(blending, 'member', [(i, (i + (1 if i % 2 else -1)) % groups...  1.72 us
    ppermute x1, starting transfers between devices, cross(): return lax.ppermute(x, AXES, [(i, across(i)) for i in range(devices)])  1.58 us
    convert_element_type x1, other arithmetic, per_device(): return total.astype(bf16)  0.79 us
    broadcast_in_dim x1, local copies, waits for them, and re-layouts, per_device(): near = ensemble[:, :MARGIN][None]  0.72 us
  transfers between devices with their start and end apart: 12, of which 5 were waited for; matrix products, arithmetic and copies ran while one was open for 0% of the time, Pallas kernels for 11%

profile of v4, /device:TPU:0, one launch (start us, length us, event | category | flops | bytes accessed | tf_op | source)
XLA Modules:
  0.0 31.5 jit_solution(12178631824677538759)
XLA Ops:
  0.0 0.7 %slice_bitcast_fusion = bf16[1,64,128]{2,1,0:T(8,128)(2,1)S(1)} fusion(bf16[64,2048]{1,0:T(8,128)(2,1)} %refs_0_.1), kind=kLoop, calls=%fused_computation.7 | loop fusion | bytes 32768 | tf_op jit(solution)/shard_map/broadcast_in_dim | solution.py:406
  0.7 3.5 %collective-permute-start = (bf16[1,64,128]{2,1,0:T(8,128)(2,1)S(1)}, bf16[1,64,128]{2,1,0:T(8,128)(2,1)S(1)}, u32[]{:S(2)}, u32[]{:S(2)}) collective-permute-start(bf16[1,64,128]{2,1,0:T(8,128)(2,1)S(1)} %slice_bitcast_fusion), channel_id=1, source_target_pairs={{0,17},{1,16},{2,19},{3,18},{4,21},{5,20},{6,23},{7,22},{8,25},{9,... | collective-permute-start | bytes 49160 | tf_op jit(solution)/shard_map/ppermute | solution.py:379
  4.2 1.4 %collective-permute-done = bf16[1,64,128]{2,1,0:T(8,128)(2,1)S(1)} collective-permute-done((bf16[1,64,128]{2,1,0:T(8,128)(2,1)S(1)}, bf16[1,64,128]{2,1,0:T(8,128)(2,1)S(1)}, u32[]{:S(2)}, u32[]{:S(2)}) %collective-permute-start) | collective-permute-done | bytes 16416 | tf_op jit(solution)/shard_map/ppermute | solution.py:379
  5.7 0.0 copy-start.2
  5.7 0.0 copy-start.3
  5.7 0.0 copy-start.4
  5.7 2.0 %collective-permute-start.1 = (bf16[2,64,128]{2,1,0:T(8,128)(2,1)S(1)}, bf16[2,64,128]{2,1,0:T(8,128)(2,1)S(1)}, u32[]{:S(2)}, u32[]{:S(2)}) collective-permute-start(bf16[2,64,128]{2,1,0:T(8,128)(2,1)S(1)} %pad_maximum_fusion.2), channel_id=1, source_target_pairs={{0,9},{1,8},{2,11},{3,10},{4,13},{5,12},{6,15},{7,14},{8,1},{9,0},... | collective-permute-start | bytes 98312 | tf_op jit(solution)/shard_map/ppermute | solution.py:379
  7.6 1.5 %collective-permute-start.5 = (bf16[64,2048]{1,0:T(8,128)(2,1)}, bf16[64,2048]{1,0:T(8,128)(2,1)S(1)}, u32[]{:S(2)}, u32[]{:S(2)}) collective-permute-start(bf16[64,2048]{1,0:T(8,128)(2,1)} %refs_0_.1), channel_id=1, source_target_pairs={{0,3},{1,2},{2,1},{3,0},{4,7},{5,6},{6,5},{7,4},{8,11},{9,10},{10,... | collective-permute-start | bytes 786440 | tf_op jit(solution)/shard_map/ppermute | solution.py:379
  9.1 0.1 collective-permute-done.1
  9.3 1.8 %collective-permute-start.2 = (bf16[4,64,128]{2,1,0:T(8,128)(2,1)S(1)}, bf16[4,64,128]{2,1,0:T(8,128)(2,1)S(1)}, u32[]{:S(2)}, u32[]{:S(2)}) collective-permute-start(bf16[4,64,128]{2,1,0:T(8,128)(2,1)S(1)} %pad_maximum_fusion.near_ref), channel_id=1, source_target_pairs={{0,5},{1,4},{2,7},{3,6},{4,1},{5,0},{6,3},{7,2},{8,13},{9,12},{10,... | collective-permute-start | bytes 196616 | tf_op jit(solution)/shard_map/ppermute | solution.py:379
  11.7 0.0 copy-done.2
  11.7 0.0 copy-done.3
  11.7 0.0 copy-done.4
  11.7 0.0 copy-start
  11.8 1.0 %shard_map.64 = (f32[18,8,128]{2,1,0:T(8,128)S(1)}, s32[2,128]{1,0:T(2,128)S(1)}, s32[2]{0:T(128)S(1)}) custom-call(s32[1,1]{1,0:T(1,128)} %bitcast.3.live_ref, s32[1,1024]{1,0:T(1,128)S(1)} %copy-done.3, f32[1,4,1024]{2,1,0:T(4,128)S(1)} %copy-done.2, f32[1,1024]{1,0:T(1,128)S(1)} %copy-done.4), custom_call_target="tpu_custom_call" | custom-call | flops 75497472 | bytes 100000 | tf_op jit(solution)/shard_map/pallas_call | solution.py:39
  12.8 0.5 %collective-permute-done.2.far_ref = bf16[4,64,128]{2,1,0:T(8,128)(2,1)S(1)} collective-permute-done((bf16[4,64,128]{2,1,0:T(8,128)(2,1)S(1)}, bf16[4,64,128]{2,1,0:T(8,128)(2,1)S(1)}, u32[]{:S(2)}, u32[]{:S(2)}) %collective-permute-start.2) | collective-permute-done | bytes 65568 | tf_op jit(solution)/shard_map/ppermute | solution.py:379
  13.3 0.0 copy-start.1
  13.3 2.2 %collective-permute-start.3 = (bf16[2,64,128]{2,1,0:T(8,128)(2,1)S(1)}, bf16[2,64,128]{2,1,0:T(8,128)(2,1)S(1)}, u32[]{:S(2)}, u32[]{:S(2)}) collective-permute-start(bf16[2,64,128]{2,1,0:T(8,128)(2,1)S(1)} %shard_map.65.refs_0_), channel_id=1, source_target_pairs={{0,3},{1,2},{2,1},{3,0},{4,7},{5,6},{6,5},{7,4},{8,11},{9,10},{10,... | collective-permute-start | bytes 98312 | tf_op jit(solution)/shard_map/ppermute | solution.py:379
  15.5 1.6 %collective-permute-done.3.refs_1_ = bf16[2,64,128]{2,1,0:T(8,128)(2,1)S(1)} collective-permute-done((bf16[2,64,128]{2,1,0:T(8,128)(2,1)S(1)}, bf16[2,64,128]{2,1,0:T(8,128)(2,1)S(1)}, u32[]{:S(2)}, u32[]{:S(2)}) %collective-permute-start.3) | collective-permute-done | bytes 32800 | tf_op jit(solution)/shard_map/ppermute | solution.py:379
  17.2 0.2 collective-permute-start.4
  17.4 0.0 copy-done
  17.4 0.4 %collective-permute-start.6 = (bf16[64,2048]{1,0:T(8,128)(2,1)S(1)}, bf16[64,2048]{1,0:T(8,128)(2,1)S(1)}, u32[]{:S(2)}, u32[]{:S(2)}) collective-permute-start(bf16[64,2048]{1,0:T(8,128)(2,1)S(1)} %copy-done), channel_id=1, source_target_pairs={{0,1},{1,0},{2,3},{3,2},{4,5},{5,4},{6,7},{7,6},{8,9},{9,8},{10,11... | collective-permute-start | bytes 786440 | tf_op jit(solution)/shard_map/ppermute | solution.py:379
  17.8 0.0 collective-permute-done.5.refs_1_
  17.8 0.2 collective-permute-start.7
  17.9 0.0 copy-done.1
  17.9 0.4 %collective-permute-start.8 = (f32[4,512]{1,0:T(4,128)S(1)}, f32[4,512]{1,0:T(4,128)S(1)}, u32[]{:S(2)}, u32[]{:S(2)}) collective-permute-start(f32[4,512]{1,0:T(4,128)S(1)} %copy-done.1), channel_id=1, source_target_pairs={{0,1},{1,0},{2,3},{3,2},{4,5},{5,4},{6,7},{7,6},{8,9},{9,8},{10,11... | collective-permute-start | bytes 24584 | tf_op jit(solution)/shard_map/ppermute | solution.py:379
  18.3 1.7 %collective-permute-start.9 = (f32[4,512]{1,0:T(4,128)S(1)}, f32[4,512]{1,0:T(4,128)S(1)}, u32[]{:S(2)}, u32[]{:S(2)}) collective-permute-start(f32[4,512]{1,0:T(4,128)S(1)} %copy-done.1), channel_id=1, source_target_pairs={{0,3},{1,2},{2,1},{3,0},{4,7},{5,6},{6,5},{7,4},{8,11},{9,10},{10,... | collective-permute-start | bytes 24584 | tf_op jit(solution)/shard_map/ppermute | solution.py:431
  20.0 0.0 collective-permute-done.4
  20.0 0.0 collective-permute-done.6.refs_2_
  20.0 0.0 collective-permute-done.7.refs_3_
  20.0 0.4 %shard_map.66 = (bf16[256,2048]{1,0:T(8,128)(2,1)S(1)}, f32[1,2048]{1,0:T(1,128)S(1)}) custom-call(bf16[64,2048]{1,0:T(8,128)(2,1)S(1)} %copy-done, bf16[64,2048]{1,0:T(8,128)(2,1)S(1)} %collective-permute-done.5.refs_1_, bf16[64,2048]{1,0:T(8,128)(2,1)S(1)} %collective-permute-done.6.refs_2_, bf16[64,2048]{1,0:T(8,128)(2,1)S(1)} %collective-permute-done.7.refs_3_), custom_call_target="tpu_custom_call" | custom-call | flops 2097152 | bytes 2097152 | tf_op jit(solution)/shard_map/pallas_call | solution.py:39
  20.5 0.8 %shard_map.67 = (f32[2,256,256]{2,1,0:T(8,128)S(1)}, f32[8,256]{1,0:T(8,128)S(1)}) custom-call(bf16[256,2048]{1,0:T(8,128)(2,1)S(1)} %get-tuple-element.24.anomaly_ref, f32[1,2048]{1,0:T(1,128)S(1)} %get-tuple-element.25.mean_ref, f32[18,8,128]{2,1,0:T(8,128)S(1)} %get-tuple-element.23.table_ref.refs_4_), custom_call_target="tpu_custom_call" | custom-call | flops 536870912 | bytes 1572864 | tf_op jit(solution)/shard_map/pallas_call | solution.py:39
  21.2 0.7 %shard_map.68.refs_6_ = f32[2,256,256]{2,1,0:T(8,128)S(1)} custom-call(bf16[256,2048]{1,0:T(8,128)(2,1)S(1)} %get-tuple-element.24.anomaly_ref, f32[1,2048]{1,0:T(1,128)S(1)} %get-tuple-element.25.mean_ref, f32[18,8,128]{2,1,0:T(8,128)S(1)} %get-tuple-element.23.table_ref.refs_4_), custom_call_target="tpu_custom_call" | custom-call | flops 536870912 | bytes 1572864 | tf_op jit(solution)/shard_map/pallas_call | solution.py:39
  22.0 0.0 collective-permute-done.8.first_blend
  22.0 0.0 collective-permute-done.9.second_blend
  22.0 0.5 %shard_map.69 = (bf16[512,256]{1,0:T(8,128)(2,1)S(1)}, bf16[512,256]{1,0:T(8,128)(2,1)S(1)}, bf16[256,256]{1,0:T(8,128)(2,1)S(1)}, f32[512,8]{1,0:T(8,128)S(1)},...) custom-call(bf16[256,2048]{1,0:T(8,128)(2,1)S(1)} %get-tuple-element.24.anomaly_ref, ...), custom_call_target="tpu_custom_call" | custom-call | flops 393216 | bytes 1048576 | tf_op jit(solution)/shard_map/pallas_call | solution.py:39
  22.5 3.1 %shard_map.70 = (bf16[4,256,256]{2,1,0:T(8,128)(2,1)S(1)}, bf16[256,256]{1,0:T(8,128)(2,1)S(1)}) custom-call(s32[2]{0:T(128)S(1)} %get-tuple-element.21.flip_ref, bf16[2,64,128]{2,1,0:T(8,128)(2,1)S(1)} %shard_map.65.refs_0_, bf16[2,64,128]{2,1,0:T(8,128)(2,1)S(1)} %collective-permute-done.3.refs_1_, bf16[2,64,128]{2,1,0:T(8,128)(2,1)S(1)} %get-tuple-element.40.refs_2_, ...), custom_call_target="tpu_custom_call" | custom-call | flops 1342177280 | bytes 2097152 | tf_op jit(solution)/shard_map/pallas_call | solution.py:39
  25.6 1.6 %collective-permute-start.11 = (bf16[256,256]{1,0:T(8,128)(2,1)S(1)}, bf16[256,256]{1,0:T(8,128)(2,1)S(1)}, u32[]{:S(2)}, u32[]{:S(2)}) collective-permute-start(bf16[256,256]{1,0:T(8,128)(2,1)S(1)} %get-tuple-element.36), channel_id=1, source_target_pairs={{0,4},{1,2},{2,1},{3,7},{4,0},{5,6},{6,5},{7,3},{8,12},{9,10},{10,... | collective-permute-start | bytes 393224 | tf_op jit(solution)/shard_map/ppermute | solution.py:388
  27.2 0.3 shard_map.72
  27.5 0.1 collective-permute-start.10
  27.6 0.3 shard_map.71
  27.9 2.7 %collective-permute-done.11 = bf16[256,256]{1,0:T(8,128)(2,1)S(1)} collective-permute-done((bf16[256,256]{1,0:T(8,128)(2,1)S(1)}, bf16[256,256]{1,0:T(8,128)(2,1)S(1)}, u32[]{:S(2)}, u32[]{:S(2)}) %collective-permute-start.11) | collective-permute-done | bytes 131104 | tf_op jit(solution)/shard_map/ppermute | solution.py:388
  30.7 0.0 collective-permute-done.10
  30.7 0.8 %fusion = bf16[512,256]{1,0:T(8,128)(2,1)} fusion(f32[256,256]{1,0:T(8,128)S(1)} %get-tuple-element.38, f32[256,256]{1,0:T(8,128)S(1)} %get-tuple-element.37, f32[512,256]{1,0:T(8,128)S(1)} %shard_map.71, bf16[512,256]{1,0:T(8,128)(2,1)S(1)} %collective-permute-done.10), kind=kLoop, calls=%fused_computation.1 | loop fusion | flops 655360 | bytes 1572864 | tf_op jit(solution)/shard_map/convert_element_type | solution.py:501
  (6 shorter events, 0.1 us)
Async XLA Ops:
  0.7 4.9 %collective-permute-start = (bf16[1,64,128]{2,1,0:T(8,128)(2,1)S(1)}, bf16[1,64,128]{2,1,0:T(8,128)(2,1)S(1)}, u32[]{:S(2)}, u32[]{:S(2)}) collective-permute-start(bf16[1,64,128]{2,1,0:T(8,128)(2,1)S(1)} %slice_bitcast_fusion), channel_id=1, source_target_pairs={{0,17},{1,16},{2,19},{3,18},{4,21},{5,20},{6,23},{7,22},{8,25},{9,... | collective-permute-start | bytes 49160 | tf_op jit(solution)/shard_map/ppermute | solution.py:379
  5.7 6.0 %copy-start.2 = (f32[1,4,1024]{2,1,0:T(4,128)S(1)}, f32[1,4,1024]{2,1,0:T(4,128)}, u32[]{:S(2)}) copy-start(f32[1,4,1024]{2,1,0:T(4,128)} %weight_ref.1) | copy-start | bytes 49156
  5.7 6.1 %copy-start.3 = (s32[1,1024]{1,0:T(1,128)S(1)}, s32[1,1024]{1,0:T(1,128)}, u32[]{:S(2)}) copy-start(s32[1,1024]{1,0:T(1,128)} %cell_ref.1) | copy-start | bytes 12292
  5.7 6.1 %copy-start.4 = (f32[1,1024]{1,0:T(1,128)S(1)}, f32[1,1024]{1,0:T(1,128)}, u32[]{:S(2)}) copy-start(f32[1,1024]{1,0:T(1,128)} %report_ref.1) | copy-start | bytes 12292
  5.7 3.6 %collective-permute-start.1 = (bf16[2,64,128]{2,1,0:T(8,128)(2,1)S(1)}, bf16[2,64,128]{2,1,0:T(8,128)(2,1)S(1)}, u32[]{:S(2)}, u32[]{:S(2)}) collective-permute-start(bf16[2,64,128]{2,1,0:T(8,128)(2,1)S(1)} %pad_maximum_fusion.2), channel_id=1, source_target_pairs={{0,9},{1,8},{2,11},{3,10},{4,13},{5,12},{6,15},{7,14},{8,1},{9,0},... | collective-permute-start | bytes 98312 | tf_op jit(solution)/shard_map/ppermute | solution.py:379
  7.6 10.1 %collective-permute-start.5 = (bf16[64,2048]{1,0:T(8,128)(2,1)}, bf16[64,2048]{1,0:T(8,128)(2,1)S(1)}, u32[]{:S(2)}, u32[]{:S(2)}) collective-permute-start(bf16[64,2048]{1,0:T(8,128)(2,1)} %refs_0_.1), channel_id=1, source_target_pairs={{0,3},{1,2},{2,1},{3,0},{4,7},{5,6},{6,5},{7,4},{8,11},{9,10},{10,... | collective-permute-start | bytes 786440 | tf_op jit(solution)/shard_map/ppermute | solution.py:379
  9.3 4.0 %collective-permute-start.2 = (bf16[4,64,128]{2,1,0:T(8,128)(2,1)S(1)}, bf16[4,64,128]{2,1,0:T(8,128)(2,1)S(1)}, u32[]{:S(2)}, u32[]{:S(2)}) collective-permute-start(bf16[4,64,128]{2,1,0:T(8,128)(2,1)S(1)} %pad_maximum_fusion.near_ref), channel_id=1, source_target_pairs={{0,5},{1,4},{2,7},{3,6},{4,1},{5,0},{6,3},{7,2},{8,13},{9,12},{10,... | collective-permute-start | bytes 196616 | tf_op jit(solution)/shard_map/ppermute | solution.py:379
  11.7 5.7 %copy-start = (bf16[64,2048]{1,0:T(8,128)(2,1)S(1)}, bf16[64,2048]{1,0:T(8,128)(2,1)}, u32[]{:S(2)}) copy-start(bf16[64,2048]{1,0:T(8,128)(2,1)} %refs_0_.1) | copy-start | bytes 786436
  13.3 4.6 %copy-start.1 = (f32[4,512]{1,0:T(4,128)S(1)}, f32[4,512]{1,0:T(4,128)}, u32[]{:S(2)}) copy-start(f32[4,512]{1,0:T(4,128)} %own_blend.1) | copy-start | bytes 24580
  13.3 3.9 %collective-permute-start.3 = (bf16[2,64,128]{2,1,0:T(8,128)(2,1)S(1)}, bf16[2,64,128]{2,1,0:T(8,128)(2,1)S(1)}, u32[]{:S(2)}, u32[]{:S(2)}) collective-permute-start(bf16[2,64,128]{2,1,0:T(8,128)(2,1)S(1)} %shard_map.65.refs_0_), channel_id=1, source_target_pairs={{0,3},{1,2},{2,1},{3,0},{4,7},{5,6},{6,5},{7,4},{8,11},{9,10},{10,... | collective-permute-start | bytes 98312 | tf_op jit(solution)/shard_map/ppermute | solution.py:379
  17.2 2.8 %collective-permute-start.4 = (bf16[4,64,128]{2,1,0:T(8,128)(2,1)S(1)}, bf16[4,64,128]{2,1,0:T(8,128)(2,1)S(1)}, u32[]{:S(2)}, u32[]{:S(2)}) collective-permute-start(bf16[4,64,128]{2,1,0:T(8,128)(2,1)S(1)} %pad_maximum_fusion.1), channel_id=1, source_target_pairs={{0,1},{1,0},{2,3},{3,2},{4,5},{5,4},{6,7},{7,6},{8,9},{9,8},{10,11... | collective-permute-start | bytes 196616 | tf_op jit(solution)/shard_map/ppermute | solution.py:379
  17.4 2.6 %collective-permute-start.6 = (bf16[64,2048]{1,0:T(8,128)(2,1)S(1)}, bf16[64,2048]{1,0:T(8,128)(2,1)S(1)}, u32[]{:S(2)}, u32[]{:S(2)}) collective-permute-start(bf16[64,2048]{1,0:T(8,128)(2,1)S(1)} %copy-done), channel_id=1, source_target_pairs={{0,1},{1,0},{2,3},{3,2},{4,5},{5,4},{6,7},{7,6},{8,9},{9,8},{10,11... | collective-permute-start | bytes 786440 | tf_op jit(solution)/shard_map/ppermute | solution.py:379
  17.8 2.3 %collective-permute-start.7 = (bf16[64,2048]{1,0:T(8,128)(2,1)S(1)}, bf16[64,2048]{1,0:T(8,128)(2,1)S(1)}, u32[]{:S(2)}, u32[]{:S(2)}) collective-permute-start(bf16[64,2048]{1,0:T(8,128)(2,1)S(1)} %collective-permute-done.5.refs_1_), channel_id=1, source_target_pairs={{0,1},{1,0},{2,3},{3,2},{4,5},{5,4},{6,7},{7,6},{8,9},{9,8},{10,11... | collective-permute-start | bytes 786440 | tf_op jit(solution)/shard_map/ppermute | solution.py:379
  17.9 4.1 %collective-permute-start.8 = (f32[4,512]{1,0:T(4,128)S(1)}, f32[4,512]{1,0:T(4,128)S(1)}, u32[]{:S(2)}, u32[]{:S(2)}) collective-permute-start(f32[4,512]{1,0:T(4,128)S(1)} %copy-done.1), channel_id=1, source_target_pairs={{0,1},{1,0},{2,3},{3,2},{4,5},{5,4},{6,7},{7,6},{8,9},{9,8},{10,11... | collective-permute-start | bytes 24584 | tf_op jit(solution)/shard_map/ppermute | solution.py:379
  18.3 3.7 %collective-permute-start.9 = (f32[4,512]{1,0:T(4,128)S(1)}, f32[4,512]{1,0:T(4,128)S(1)}, u32[]{:S(2)}, u32[]{:S(2)}) collective-permute-start(f32[4,512]{1,0:T(4,128)S(1)} %copy-done.1), channel_id=1, source_target_pairs={{0,3},{1,2},{2,1},{3,0},{4,7},{5,6},{6,5},{7,4},{8,11},{9,10},{10,... | collective-permute-start | bytes 24584 | tf_op jit(solution)/shard_map/ppermute | solution.py:431
  25.6 5.0 %collective-permute-start.11 = (bf16[256,256]{1,0:T(8,128)(2,1)S(1)}, bf16[256,256]{1,0:T(8,128)(2,1)S(1)}, u32[]{:S(2)}, u32[]{:S(2)}) collective-permute-start(bf16[256,256]{1,0:T(8,128)(2,1)S(1)} %get-tuple-element.36), channel_id=1, source_target_pairs={{0,4},{1,2},{2,1},{3,7},{4,0},{5,6},{6,5},{7,3},{8,12},{9,10},{10,... | collective-permute-start | bytes 393224 | tf_op jit(solution)/shard_map/ppermute | solution.py:388
  27.5 3.2 %collective-permute-start.10 = (bf16[512,256]{1,0:T(8,128)(2,1)S(1)}, bf16[512,256]{1,0:T(8,128)(2,1)S(1)}, u32[]{:S(2)}, u32[]{:S(2)}) collective-permute-start(bf16[512,256]{1,0:T(8,128)(2,1)S(1)} %shard_map.72), channel_id=1, source_target_pairs={{0,1},{1,0},{2,3},{3,2},{4,5},{5,4},{6,7},{7,6},{8,9},{9,8},{10,11... | collective-permute-start | bytes 786440 | tf_op jit(solution)/shard_map/ppermute | solution.py:379

commit v5 on v4

v5 whole, which is shorter than its diff:
```python
import functools

import jax
import jax.numpy as jnp
from jax import lax
from jax.experimental import pallas as pl
from jax.experimental.pallas import tpu as pltpu
from jax.sharding import PartitionSpec as P


MARGIN = 128
LANES = 128
GRANT = 20 << 20
GANG = 2
LAG = 1
AXES = ("region", "member")

f32 = jnp.float32
bf16 = jnp.bfloat16

VMEM = pl.BlockSpec(memory_space=pltpu.VMEM)
SMEM = pl.BlockSpec(memory_space=pltpu.SMEM)


def dot_nn(a, b):
    return lax.dot_general(a, b, (((1,), (0,)), ((), ())), preferred_element_type=f32)


def dot_nt(a, b):
    return lax.dot_general(a, b, (((1,), (1,)), ((), ())), preferred_element_type=f32)


def split(x):
    high = x.astype(bf16)
    return high, (x - high.astype(f32)).astype(bf16)


def call(kernel, outs, inputs, flops, moved, smem_in=0, smem_out=0, scratch=()):
    return pl.pallas_call(
        kernel,
        out_shape=[jax.ShapeDtypeStruct(s, d) for s, d in outs],
        in_specs=[SMEM] * smem_in + [VMEM] * (len(inputs) - smem_in),
        out_specs=[VMEM] * (len(outs) - smem_out) + [SMEM] * smem_out,
        scratch_shapes=list(scratch),
        cost_estimate=pl.CostEstimate(flops=flops, bytes_accessed=moved, transcendentals=0),
        compiler_params=pltpu.CompilerParams(vmem_limit_bytes=GRANT),
    )(*inputs)


def parts_of(x, size):
    if size & (size - 1):
        return lax.div(x, size), lax.rem(x, size)
    return lax.shift_right_logical(x, size.bit_length() - 1), x & (size - 1)


def same_position(size):
    shape = (size, size)
    return lax.broadcasted_iota(jnp.int32, shape, 0) == lax.broadcasted_iota(jnp.int32, shape, 1)


def extra_rows(row_count):
    pairs = row_count // 2
    return 0 if pairs == 1 else 1 if pairs == 2 else 2


def extra_place(slot, row_count):
    member = lax.axis_index("member")
    pair = member >> 1
    right = jnp.where(pair == 0, 1, 0) if row_count == 4 else jnp.int32(slot)
    row = 2 * pair - 1 + 3 * right
    exists = (row >= 0) & (row < row_count)
    return right, row, exists, (member & 1) == right


def summed(weights, reports, high, low_hot, weight_table, report_table):
    rows, padded, _ = weight_table.shape
    points, slots = weights.shape
    weights = weights.astype(bf16).astype(f32)
    scaled = weights * reports
    scaled_high = scaled.astype(bf16).astype(f32)
    values = jnp.concatenate([weights, scaled_high, scaled - scaled_high], axis=0)
    if -3 * points % 8:
        values = jnp.concatenate([values, jnp.zeros((-3 * points % 8, slots), f32)], axis=0)
    size = values.shape[0]
    chosen = [jnp.where(high == row, values, 0.0) for row in range(rows)]
    total = dot_nt(jnp.concatenate(chosen, axis=0).astype(bf16), low_hot)
    total = total.reshape(rows, size, LANES)
    weight_table[:, 0:points, :] = total[:, 0:points]
    report_table[:, 0:points, :] = total[:, points : 2 * points] + total[:, 2 * points : 3 * points]
    if padded > points:
        empty = jnp.zeros((rows, padded - points, LANES), f32)
        weight_table[:, points:, :] = empty
        report_table[:, points:, :] = empty


def weights_kernel(
    cells, regions, live_ref, cell_ref, weight_ref, report_ref,
    weight_table, report_table, high_ref, low_ref, place_ref, flip_ref
):
    region = lax.axis_index("region")
    bits = regions.bit_length() - 1
    slots = weight_ref.shape[2]
    rows = cells // LANES + 2
    holder, within = parts_of(cell_ref[...], cells)
    block, low = parts_of(within, LANES)
    outside = holder != region
    named = holder.astype(f32)
    first = jnp.min(jnp.where(outside, named, float(regions))).astype(jnp.int32)
    second = jnp.max(jnp.where(outside, named, -1.0)).astype(jnp.int32)
    first = jnp.where(first == regions, region, first)
    second = jnp.where(second < 0, region, second)
    for j, source in enumerate((first, second)):
        distance = region ^ source
        place = jnp.int32(0)
        flip = jnp.int32(0)
        for k in range(bits):
            bit = (distance >> k) & 1
            place = place + (bit << (bits - 1 - k))
            flip = flip ^ bit
        place_ref[j : j + 1, :] = jnp.full((1, LANES), place, jnp.int32)
        flip_ref[j] = flip
    high = jnp.where(outside, jnp.where(holder == first, rows - 2, rows - 1), block)
    active = lax.broadcasted_iota(jnp.int32, (1, slots), 1) < live_ref[...]
    high = jnp.where(active, high, -1)
    low_hot = (lax.broadcasted_iota(jnp.int32, (LANES, slots), 0) == low).astype(f32).astype(bf16)
    high_ref[...] = high
    low_ref[...] = low_hot
    summed(weight_ref[0], report_ref[...], high, low_hot, weight_table, report_table)


def extra_kernel(
    row_count, high_ref, low_ref, report_ref, across_ref, back_ref, weight_table, report_table
):
    odd = lax.axis_index("member") & 1
    points = across_ref.shape[1]
    weights = []
    for slot in range(extra_rows(row_count)):
        _, _, exists, needed = extra_place(slot, row_count)
        wanted = jnp.where(needed, across_ref[0], back_ref[0])
        wanted = jnp.where(odd == 1, wanted[points // 2 :], wanted[: points // 2])
        weights.append(jnp.where(exists, wanted, 0.0))
    weights = jnp.concatenate(weights, axis=0)
    summed(weights, report_ref[...], high_ref[...], low_ref[...], weight_table, report_table)


def pick_kernel(place_ref, near_ref, far_ref, out_ref):
    count = near_ref.shape[0]
    for j in range(2):
        place = jnp.broadcast_to(place_ref[j : j + 1, :], near_ref.shape[1:])
        chosen = jnp.zeros(near_ref.shape[1:], f32)
        for ref, base in ((near_ref, 0), (far_ref, count)):
            for i in range(count):
                chosen = jnp.where(place == base + i, ref[i].astype(f32), chosen)
        out_ref[j] = chosen.astype(bf16)


def anomaly_kernel(offsets, *refs):
    pieces, (anomaly_ref, mean_ref) = refs[:-2], refs[-2:]
    member = lax.axis_index("member")
    rows = pieces[0].shape[0]
    members = rows * len(pieces)
    total = jnp.sum(pieces[0][...].astype(f32), axis=0, keepdims=True)
    for piece in pieces[1:]:
        total = total + jnp.sum(piece[...].astype(f32), axis=0, keepdims=True)
    mean = total / members
    mean_ref[...] = mean
    for offset, piece in zip(offsets, pieces):
        start = pl.multiple_of((member ^ offset) * rows, rows)
        anomaly_ref[pl.ds(start, rows), :] = (piece[...].astype(f32) - mean).astype(bf16)


def products_kernel(chosen, forced, anomaly_ref, mean_ref, *refs):
    tables, (products_ref, forcing_ref) = refs[:-2], refs[-2:]
    members, cells = anomaly_ref.shape
    points = forcing_ref.shape[0]
    chunk = min(cells, 2048)
    for start in range(0, cells, chunk):
        block = anomaly_ref[:, start : start + chunk]
        blocks = range(start // LANES, (start + chunk) // LANES)
        scaled = []
        for t, a in chosen:
            weighted = [
                anomaly_ref[:, h * LANES : (h + 1) * LANES]
                * tables[2 * t][h, a : a + 1, :].astype(bf16)
                for h in blocks
            ]
            scaled.append(jnp.concatenate(weighted, axis=1))
        departures = []
        for h in blocks:
            mean = mean_ref[:, h * LANES : (h + 1) * LANES]
            departures.append(tables[2 * forced + 1][h] - tables[2 * forced][h] * mean)
        scaled += list(split(jnp.concatenate(departures, axis=1)))
        part = dot_nt(jnp.concatenate(scaled, axis=0), block)
        for i in range(len(chosen)):
            rows = part[i * members : (i + 1) * members]
            if start:
                products_ref[i] += rows
            else:
                diagonal = jnp.where(same_position(members), members - 1.0, 0.0)
                products_ref[i] = rows + diagonal
        rest = part[len(chosen) * members :]
        rest = rest[:points] + rest[points:]
        forcing_ref[...] = rest if start == 0 else forcing_ref[...] + rest


def mixing_rows(blend_ref, band, row, valid, row_count, points):
    blending = blend_ref[...]
    slab = blending.shape[1]
    half = slab // 2
    mixing = blending / jnp.sum(blending, axis=0, keepdims=True)
    cell = lax.broadcasted_iota(jnp.int32, (1, slab), 1)
    upper = cell < half
    bases = column_bases(points)
    size = half // len(bases)
    inside = jnp.where(upper, cell, cell - half)
    base = jnp.zeros_like(cell)
    for g in range(1, len(bases)):
        base = base + jnp.where(inside >= g * size, bases[g] - bases[g - 1], 0)
    tops = [jnp.clip(band - 1 + u, 0, row_count - 2) for u in range(2)]
    step = row - jnp.where(upper, tops[0], tops[1])
    pairs = []
    for c in range(2):
        pair = jnp.where(
            step == 0, mixing[c : c + 1], jnp.where(step == 1, mixing[2 + c : 3 + c], 0.0)
        )
        pairs.append(jnp.where(valid, pair, 0.0))
    return [
        jnp.where(base == q, pairs[0], jnp.where(base == q - 1, pairs[1], 0.0))
        for q in range(points)
    ]


def stacked(rows):
    rows = rows + [jnp.zeros_like(rows[0])] * (-len(rows) % 8)
    return jnp.concatenate(rows, axis=0).T


def band_cells(partner, row_count, points, anomaly_ref, blend_ref, cells_ref, mix_ref, extra_refs):
    member = lax.axis_index("member")
    band = member ^ 1 if partner else member
    slab = cells_ref.shape[0]
    half = slab // 2
    for u in range(2):
        start = pl.multiple_of(band * slab + u * half, half)
        cells_ref[u * half : (u + 1) * half, :] = anomaly_ref[:, pl.ds(start, half)].T
    mix_ref[...] = stacked(mixing_rows(blend_ref, band, member, True, row_count, points))
    few = points // 2
    for slot, ref in enumerate(extra_refs):
        right, row, exists, needed = extra_place(slot, row_count)
        valid = exists & (needed != partner)
        rows = mixing_rows(blend_ref, band, row, valid, row_count, points)
        rows = [jnp.where(right == 1, x[:, half:], x[:, :half]) for x in rows]
        odd = (member & 1) == 1
        ref[...] = stacked([jnp.where(odd, rows[few + j], rows[j]) for j in range(few)])


def partner_cells_kernel(row_count, points, anomaly_ref, blend_ref, cells_ref, mix_ref, *extra_refs):
    band_cells(True, row_count, points, anomaly_ref, blend_ref, cells_ref, mix_ref, extra_refs)


def blended_band(row_count, points, transform_ref, cells_ref, mix_ref, extra_refs, sum_ref):
    half = cells_ref.shape[0] // 2
    halves = [slice(u * half, (u + 1) * half) for u in range(2)]
    parts = blended_parts(
        [(cells_ref[rows, :], mix_ref[rows, :]) for rows in halves],
        lambda q: transform_ref[q],
        points,
    )
    for rows, part in zip(halves, parts):
        sum_ref[rows, :] += part
    few = points // 2
    for slot, ref in enumerate(extra_refs):
        right = extra_place(slot, row_count)[0]
        rows = pl.ds(pl.multiple_of(right * half, half), half)
        cells = cells_ref[rows, :]
        part = None
        for j in range(few):
            term = ref[:, j : j + 1] * dot_nn(cells, transform_ref[points + slot * few + j])
            part = term if part is None else part + term
        sum_ref[rows, :] += part


def column_bases(points):
    return [min(max(b - 1 + v, 0), points - 2) for b in range(points) for v in range(2)]


def blended_parts(segments, transforms, points):
    half = segments[0][0].shape[0]
    bases = column_bases(points)
    size = half // len(bases)
    spans = []
    for v in range(points - 1):
        hits = [g for g, b in enumerate(bases) if b == v]
        spans.append((hits[0] * size, (hits[-1] + 1) * size))
    sums = [[None] * (points - 1) for _ in segments]
    for q in range(points):
        where = [v for v in (q - 1, q) if 0 <= v <= points - 2]
        rows = [
            (n, v, cells[spans[v][0] : spans[v][1], :])
            for n, (cells, _) in enumerate(segments)
            for v in where
        ]
        spread = dot_nn(jnp.concatenate([r[2] for r in rows], axis=0), transforms(q))
        at = 0
        for n, v, cells in rows:
            low, high = spans[v]
            term = segments[n][1][low:high, q : q + 1] * spread[at : at + high - low]
            sums[n][v] = term if sums[n][v] is None else sums[n][v] + term
            at += high - low
    return [jnp.concatenate(parts, axis=0) for parts in sums]


def transform_kernel(offsets, row_count, points, flip_ref, *refs):
    count = len(offsets)
    kinds = 2 if extra_rows(row_count) else 1
    pieces, tables, refs = refs[:count], refs[count : count + 2 * kinds], refs[count + 2 * kinds :]
    products_refs, forcing_refs, refs = refs[:2], refs[2 : 2 + kinds], refs[2 + kinds :]
    cells_ref, mix_ref, *extra_refs, transform_ref, out_ref, margin_ref, sum_ref = refs
    member = lax.axis_index("member")
    rows = pieces[0].shape[1]
    members = rows * count
    last = tables[0].shape[0]
    half_points = products_refs[0].shape[0]
    all_points = 2 * half_points
    for offset, piece in zip(offsets, pieces):
        for j in range(2):
            start = pl.multiple_of((member ^ offset ^ flip_ref[j]) * rows, rows)
            margin_ref[pl.ds(start, rows), j * LANES : (j + 1) * LANES] = piece[j]
    values = margin_ref[...].astype(f32)
    mean = jnp.sum(values, axis=0, keepdims=True) / members
    pert = (values - mean).astype(bf16)
    tiles, departures = [], []
    for kind in range(kinds):
        weights, reports = (
            jnp.concatenate([table[last - 2], table[last - 1]], axis=1)
            for table in tables[2 * kind : 2 * kind + 2]
        )
        tiles.append(weights)
        departures += list(split(reports - weights * mean))
    rest = dot_nt(jnp.concatenate(departures, axis=0), pert)
    forcings = []
    for kind in range(kinds):
        size = tiles[kind].shape[0]
        part = rest[:size] + rest[size : 2 * size]
        rest = rest[2 * size :]
        forcings.append((forcing_refs[kind][...] + part).T)

    def steps(a):
        kind, place = (0, a) if a < points else (1, a - points)
        weighted = pert * tiles[kind][place : place + 1, :].astype(bf16)
        full = products_refs[a // half_points][a % half_points] + dot_nt(weighted, pert)
        full_low = full.astype(bf16)
        yield
        square = jnp.sum(jnp.sum(full * full, axis=0, keepdims=True), axis=1, keepdims=True)
        norm = lax.rsqrt(square)
        matrix = full * norm
        low = matrix.astype(bf16)
        squared = dot_nn(full_low, full_low) * (norm * norm)
        squared_low = squared.astype(bf16)
        e = 0.75 * squared - (13 / 12) * matrix
        yield
        e = e + dot_nn(squared_low, (1 / 36) * squared_low - 0.25 * low)
        e_low = e.astype(bf16)
        yield
        y = matrix + dot_nn(low, e_low)
        y_low = y.astype(bf16)
        yield
        p = y + dot_nn(y_low, e_low)
        p_low = p.astype(bf16)
        yield
        squared = dot_nn(p_low, p_low)
        squared_low = squared.astype(bf16)
        f = (0.75 * 5.0625**2) * squared - (13 / 12 * 5.0625) * p
        yield
        f = f + dot_nn(
            squared_low, (5.0625**4 / 36) * squared_low - (0.25 * 5.0625**3) * p_low
        )
        e = e + f
        yield
        e = e + dot_nn(e_low, f.astype(bf16)) + identity
        scale = 5.0625 * jnp.sqrt(norm)
        inner = jnp.sum(e * forcings[kind][:, place : place + 1], axis=0, keepdims=True)
        outer = jnp.sum(e * inner, axis=1, keepdims=True)
        yield
        transform_ref[a] = (
            scale * scale * outer + (jnp.sqrt(members - 1.0) * scale) * e
        ).astype(bf16)

    identity = jnp.where(same_position(members), 1.0, 0.0)
    running = [steps(a) for a in range(all_points)]
    tick = 0
    while any(running):
        for a in range(all_points):
            if running[a] and tick >= LAG * (a // GANG) and next(running[a], True):
                running[a] = None
        tick += 1
    sum_ref[...] = jnp.zeros(sum_ref.shape, f32)
    blended_band(row_count, points, transform_ref, cells_ref, mix_ref, extra_refs, sum_ref)
    out_ref[...] = sum_ref[...].astype(bf16)


def own_kernel(
    row_count, points, transform_ref, anomaly_ref, mean_ref, blend_ref, out_ref,
    cells_ref, mix_ref, *extra_refs
):
    member = lax.axis_index("member")
    slab = out_ref.shape[0]
    band_cells(False, row_count, points, anomaly_ref, blend_ref, cells_ref, mix_ref, extra_refs)
    row = mean_ref[:, pl.ds(pl.multiple_of(member * slab, slab), slab)]
    column = jnp.broadcast_to(row, (8, slab)).T
    out_ref[...] = jnp.broadcast_to(column[:, 0:1], out_ref.shape)
    blended_band(row_count, points, transform_ref, cells_ref, mix_ref, extra_refs, out_ref)


def per_device(ensemble, reports, report_count, report_cell, report_weight, blending):
    local_members, cell_count = ensemble.shape
    regions = lax.axis_size("region")
    groups = lax.axis_size("member")
    members = local_members * groups
    points = report_weight.shape[1]
    slots = reports.shape[1]
    slab = cell_count // groups
    half = slab // 2
    devices = regions * groups
    region_bits = regions.bit_length() - 1
    member_bits = groups.bit_length() - 1

    def swap(x, mask):
        return lax.ppermute(x, AXES, [(i, i ^ mask) for i in range(devices)])

    member_masks = [(1 << k) | 1 for k in range(member_bits - 1, 0, -1)] + [1]

    table_rows = cell_count // LANES + 2
    extra_count = extra_rows(groups)
    few = points // 2
    all_points = points + extra_count * few

    def tables_of(count):
        return [((table_rows, count + -count % 8, LANES), f32)] * 2

    *own_tables, highs, lows, places, flips = call(
        functools.partial(weights_kernel, cell_count, regions),
        [
            *tables_of(points),
            ((1, slots), jnp.int32),
            ((LANES, slots), bf16),
            ((2, LANES), jnp.int32),
            ((2,), jnp.int32),
        ],
        (report_count[None], report_cell, report_weight, reports),
        6 * table_rows * points * slots * LANES,
        100000,
        smem_out=1,
    )
    tables = own_tables
    if extra_count:
        ring = [(i, (i + (1 if i % 2 else -1)) % groups) for i in range(groups)]
        across = lax.ppermute(report_weight, "member", ring)
        back = swap(across, 1)
        extra_tables = call(
            functools.partial(extra_kernel, groups),
            tables_of(extra_count * few),
            (highs, lows, reports, across, back),
            6 * table_rows * extra_count * few * slots * LANES,
            100000,
        )
        tables = [*own_tables, *extra_tables]

    near = ensemble[:, :MARGIN][None]
    for k in range(region_bits - 1, -1, -1):
        far = swap(near, (groups << k) | 1)
        if k:
            near = jnp.concatenate([near, far], axis=0)
    (picked,) = call(
        pick_kernel,
        [((2, local_members, MARGIN), bf16)],
        (places, near, far),
        0,
        100000,
    )
    margins = [picked]
    for step, mask in enumerate(member_masks):
        if step == 0:
            margins = margins + [swap(picked, mask)]
        else:
            joined = swap(jnp.concatenate(margins, axis=0), mask)
            margins = margins + [joined[2 * i : 2 * i + 2] for i in range(len(margins))]

    pieces, offsets = [ensemble], [0]
    for mask in member_masks:
        pieces = pieces + [swap(x, mask) for x in pieces]
        offsets = offsets + [offset ^ mask for offset in offsets]
    partner_blending = swap(blending, 1)

    anomaly, mean = call(
        functools.partial(anomaly_kernel, tuple(offsets)),
        [((members, cell_count), bf16), ((1, cell_count), f32)],
        tuple(pieces),
        4 * members * cell_count,
        4 * members * cell_count,
    )
    items = [(0, a) for a in range(points)] + [(1, a) for a in range(all_points - points)]
    share = all_points // 2
    products, forcings = [], []
    for part in range(2):
        chosen = tuple(items[part * share : (part + 1) * share])
        forced = part if extra_count else 0
        used = tables if part else own_tables
        product, forcing = call(
            functools.partial(products_kernel, chosen, forced),
            [((share, members, members), f32), ((used[2 * forced].shape[1], members), f32)],
            (anomaly, mean, *used),
            2 * share * members * members * cell_count,
            2 * members * cell_count + 4 * share * members * members,
        )
        products.append(product)
        forcings.append(forcing)
    forcings = forcings if extra_count else forcings[:1]
    band = [
        ((slab, members), bf16),
        ((slab, points + -points % 8), f32),
        *[((half, few + -few % 8), f32)] * extra_count,
    ]
    partner_band = call(
        functools.partial(partner_cells_kernel, groups, points),
        band,
        (anomaly, partner_blending),
        3 * slab * members,
        4 * slab * members,
    )
    transform, to_partner = call(
        functools.partial(transform_kernel, tuple(offsets), groups, points),
        [((all_points, members, members), bf16), ((slab, members), bf16)],
        (
            flips,
            *margins,
            *tables,
            *products,
            *forcings,
            *partner_band,
        ),
        2 * 8 * all_points * members**3,
        8 * all_points * members * members,
        smem_in=1,
        scratch=[
            pltpu.VMEM((members, 2 * LANES), bf16),
            pltpu.VMEM((slab, members), f32),
        ],
    )
    from_partner = swap(to_partner, 1)
    (own,) = call(
        functools.partial(own_kernel, groups, points),
        [((slab, members), f32)],
        (transform, anomaly, mean, blending),
        4 * slab * members * members,
        8 * slab * members,
        scratch=[pltpu.VMEM(*x) for x in band],
    )
    return (own + from_partner.astype(f32)).astype(bf16)


def solution(mesh):
    return jax.shard_map(
        per_device,
        mesh=mesh,
        in_specs=(
            P("member", "region"),
            P("region", None),
            P("region"),
            P("region", None),
            P("region", "member", None),
            P(None, ("region", "member")),
        ),
        out_specs=P(("region", "member"), None),
        check_vma=False,
    )
```

time: 31.7 us -> 31.2 us (0.984)
  Pallas kernels: 7.24 us -> 8.47 us
  starting transfers between devices: 15.5 us -> 14.3 us
  waiting for transfers between devices: 6.37 us -> 5.88 us
    ppermute x2 -> x1, waiting for transfers between devices: 2.72 us -> 0.98 us  [per_device(): across = lax.ppermute(report_weight, 'member', ring)]
    ppermute x2 -> x1, starting transfers between devices: 3.3 us -> 1.66 us  [per_device(): across = lax.ppermute(report_weight, 'member', ring)]
    ppermute x10 -> x11, waiting for transfers between devices: 3.65 us -> 4.89 us  [swap(): return lax.ppermute(x, AXES, [(i, i ^ mask) for i in range(devices)])]
    pallas_call x9, Pallas kernels: 7.24 us -> 8.47 us  [call(): pl.pallas_call(kernel, out_shape=[jax.ShapeDtypeStruct(s, d) for s, d in...]
    ppermute x10 -> x11, starting transfers between devices: 12.1 us -> 12.6 us  [swap(): return lax.ppermute(x, AXES, [(i, i ^ mask) for i in range(devices)])]
  transfers between devices with their start and end apart: 12 -> 12, of which waited for: 5 -> 7; matrix products, arithmetic and copies ran while one was open for 0% -> 0% of each run, Pallas kernels for 11% -> 14%
where the time goes in v5:
time: 31.2 us; the launch traced here: 31 us
  starting transfers between devices  14.3 us (46%)
  Pallas kernels  8.47 us (27%)
  waiting for transfers between devices  5.88 us (19%)
  between operations  0.82 us (3%)
  other arithmetic  0.78 us (2%)
  local copies, waits for them, and re-layouts  0.75 us (2%)
    ppermute x11, starting transfers between devices, swap(): return lax.ppermute(x, AXES, [(i, i ^ mask) for i in range(devices)])  12.6 us
    pallas_call x9, Pallas kernels, call(): pl.pallas_call(kernel, out_shape=[jax.ShapeDtypeStruct(s, d) for s, d in...  8.47 us
    ppermute x11, waiting for transfers between devices, swap(): return lax.ppermute(x, AXES, [(i, i ^ mask) for i in range(devices)])  4.89 us
    ppermute x1, starting transfers between devices, per_device(): across = lax.ppermute(report_weight, 'member', ring)  1.66 us
    ppermute x1, waiting for transfers between devices, per_device(): across = lax.ppermute(report_weight, 'member', ring)  0.98 us
    convert_element_type x1, other arithmetic, per_device(): return (own + from_partner.astype(f32)).astype(bf16)  0.76 us
    broadcast_in_dim x1, local copies, waits for them, and re-layouts, per_device(): near = ensemble[:, :MARGIN][None]  0.72 us
  transfers between devices with their start and end apart: 12, of which 7 were waited for; matrix products, arithmetic and copies ran while one was open for 0% of the time, Pallas kernels for 14%

profile of v5, /device:TPU:0, one launch (start us, length us, event | category | flops | bytes accessed | tf_op | source)
XLA Modules:
  0.0 31.0 jit_solution(16463401765487999257)
XLA Ops:
  0.0 0.7 %slice_bitcast_fusion = bf16[1,64,128]{2,1,0:T(8,128)(2,1)S(1)} fusion(bf16[64,2048]{1,0:T(8,128)(2,1)} %refs_0_.1), kind=kLoop, calls=%fused_computation.4 | loop fusion | bytes 32768 | tf_op jit(solution)/shard_map/broadcast_in_dim | solution.py:469
  0.7 3.5 %collective-permute-start = (bf16[1,64,128]{2,1,0:T(8,128)(2,1)S(1)}, bf16[1,64,128]{2,1,0:T(8,128)(2,1)S(1)}, u32[]{:S(2)}, u32[]{:S(2)}) collective-permute-start(bf16[1,64,128]{2,1,0:T(8,128)(2,1)S(1)} %slice_bitcast_fusion), channel_id=1, source_target_pairs={{0,17},{1,16},{2,19},{3,18},{4,21},{5,20},{6,23},{7,22},{8,25},{9,... | collective-permute-start | bytes 49160 | tf_op jit(solution)/shard_map/ppermute | solution.py:429
  4.2 1.4 %collective-permute-done = bf16[1,64,128]{2,1,0:T(8,128)(2,1)S(1)} collective-permute-done((bf16[1,64,128]{2,1,0:T(8,128)(2,1)S(1)}, bf16[1,64,128]{2,1,0:T(8,128)(2,1)S(1)}, u32[]{:S(2)}, u32[]{:S(2)}) %collective-permute-start) | collective-permute-done | bytes 16416 | tf_op jit(solution)/shard_map/ppermute | solution.py:429
  5.7 0.0 copy-start.2
  5.7 0.0 copy-start.3
  5.7 0.0 copy-start.4
  5.7 2.0 %collective-permute-start.1 = (bf16[2,64,128]{2,1,0:T(8,128)(2,1)S(1)}, bf16[2,64,128]{2,1,0:T(8,128)(2,1)S(1)}, u32[]{:S(2)}, u32[]{:S(2)}) collective-permute-start(bf16[2,64,128]{2,1,0:T(8,128)(2,1)S(1)} %pad_maximum_fusion.2), channel_id=1, source_target_pairs={{0,9},{1,8},{2,11},{3,10},{4,13},{5,12},{6,15},{7,14},{8,1},{9,0},... | collective-permute-start | bytes 98312 | tf_op jit(solution)/shard_map/ppermute | solution.py:429
  7.6 1.5 %collective-permute-start.7 = (bf16[64,2048]{1,0:T(8,128)(2,1)}, bf16[64,2048]{1,0:T(8,128)(2,1)S(1)}, u32[]{:S(2)}, u32[]{:S(2)}) collective-permute-start(bf16[64,2048]{1,0:T(8,128)(2,1)} %refs_0_.1), channel_id=1, source_target_pairs={{0,3},{1,2},{2,1},{3,0},{4,7},{5,6},{6,5},{7,4},{8,11},{9,10},{10,... | collective-permute-start | bytes 786440 | tf_op jit(solution)/shard_map/ppermute | solution.py:429
  9.1 0.1 collective-permute-done.1
  9.3 0.0 copy-start
  9.3 1.8 %collective-permute-start.2 = (bf16[4,64,128]{2,1,0:T(8,128)(2,1)S(1)}, bf16[4,64,128]{2,1,0:T(8,128)(2,1)S(1)}, u32[]{:S(2)}, u32[]{:S(2)}) collective-permute-start(bf16[4,64,128]{2,1,0:T(8,128)(2,1)S(1)} %pad_maximum_fusion.near_ref), channel_id=1, source_target_pairs={{0,5},{1,4},{2,7},{3,6},{4,1},{5,0},{6,3},{7,2},{8,13},{9,12},{10,... | collective-permute-start | bytes 196616 | tf_op jit(solution)/shard_map/ppermute | solution.py:429
  11.7 0.0 copy-done.2
  11.7 0.0 copy-done.3
  11.7 0.0 copy-done.4
  11.8 1.0 %shard_map.64 = (f32[18,8,128]{2,1,0:T(8,128)S(1)}, f32[18,8,128]{2,1,0:T(8,128)S(1)}, s32[1,1024]{1,0:T(1,128)S(1)}, bf16[128,1024]{1,0:T(8,128)(2,1)S(1)}, s32[2,128]{1,0:T(2,128)S(1)}, /*index=5*/s32[2]{0:T(128)S(1)}) custom-call(s32[1,1]{1,0:T(1,128)} %bitcast.3.live_ref, s32[1,1024]{1,0:T(1,128)S(1)} %copy-done.4, f32[1,4,1024]{2,1,0:T(4,128)S(1)} %copy-done.3, ...), custom_call_target="tpu_custom_call" | custom-call | flops 56623104 | bytes 100000 | tf_op jit(solution)/shard_map/pallas_call | solution.py:39
  12.7 0.5 %collective-permute-done.2.far_ref = bf16[4,64,128]{2,1,0:T(8,128)(2,1)S(1)} collective-permute-done((bf16[4,64,128]{2,1,0:T(8,128)(2,1)S(1)}, bf16[4,64,128]{2,1,0:T(8,128)(2,1)S(1)}, u32[]{:S(2)}, u32[]{:S(2)}) %collective-permute-start.2) | collective-permute-done | bytes 65568 | tf_op jit(solution)/shard_map/ppermute | solution.py:429
  13.3 0.0 copy-start.1
  13.3 2.2 %collective-permute-start.3 = (bf16[2,64,128]{2,1,0:T(8,128)(2,1)S(1)}, bf16[2,64,128]{2,1,0:T(8,128)(2,1)S(1)}, u32[]{:S(2)}, u32[]{:S(2)}) collective-permute-start(bf16[2,64,128]{2,1,0:T(8,128)(2,1)S(1)} %shard_map.65.refs_0_), channel_id=1, source_target_pairs={{0,3},{1,2},{2,1},{3,0},{4,7},{5,6},{6,5},{7,4},{8,11},{9,10},{10,... | collective-permute-start | bytes 98312 | tf_op jit(solution)/shard_map/ppermute | solution.py:429
  15.6 1.6 %collective-permute-done.3.refs_1_ = bf16[2,64,128]{2,1,0:T(8,128)(2,1)S(1)} collective-permute-done((bf16[2,64,128]{2,1,0:T(8,128)(2,1)S(1)}, bf16[2,64,128]{2,1,0:T(8,128)(2,1)S(1)}, u32[]{:S(2)}, u32[]{:S(2)}) %collective-permute-start.3) | collective-permute-done | bytes 32800 | tf_op jit(solution)/shard_map/ppermute | solution.py:429
  17.2 0.2 collective-permute-start.4
  17.4 1.7 %collective-permute-start.5 = (f32[1,4,1024]{2,1,0:T(4,128)S(1)}, f32[1,4,1024]{2,1,0:T(4,128)S(1)}, u32[]{:S(2)}, u32[]{:S(2)}) collective-permute-start(f32[1,4,1024]{2,1,0:T(4,128)S(1)} %copy-done.3), channel_id=1, source_target_pairs={{0,3},{1,2},{2,1},{3,0},{4,7},{5,6},{6,5},{7,4},{8,11},{9,10},{10,... | collective-permute-start | bytes 49160 | tf_op jit(solution)/shard_map/ppermute | solution.py:458
  19.1 0.0 copy-done
  19.1 0.4 %collective-permute-start.8 = (bf16[64,2048]{1,0:T(8,128)(2,1)S(1)}, bf16[64,2048]{1,0:T(8,128)(2,1)S(1)}, u32[]{:S(2)}, u32[]{:S(2)}) collective-permute-start(bf16[64,2048]{1,0:T(8,128)(2,1)S(1)} %copy-done), channel_id=1, source_target_pairs={{0,1},{1,0},{2,3},{3,2},{4,5},{5,4},{6,7},{7,6},{8,9},{9,8},{10,11... | collective-permute-start | bytes 786440 | tf_op jit(solution)/shard_map/ppermute | solution.py:429
  19.5 0.0 collective-permute-done.7.refs_1_
  19.5 0.1 collective-permute-start.9
  19.6 1.0 %collective-permute-done.5.across_ref = f32[1,4,1024]{2,1,0:T(4,128)S(1)} collective-permute-done((f32[1,4,1024]{2,1,0:T(4,128)S(1)}, f32[1,4,1024]{2,1,0:T(4,128)S(1)}, u32[]{:S(2)}, u32[]{:S(2)}) %collective-permute-start.5) | collective-permute-done | bytes 16416 | tf_op jit(solution)/shard_map/ppermute | solution.py:458
  20.6 0.4 %collective-permute-start.6 = (f32[1,4,1024]{2,1,0:T(4,128)S(1)}, f32[1,4,1024]{2,1,0:T(4,128)S(1)}, u32[]{:S(2)}, u32[]{:S(2)}) collective-permute-start(f32[1,4,1024]{2,1,0:T(4,128)S(1)} %collective-permute-done.5.across_ref), channel_id=1, source_target_pairs={{0,1},{1,0},{2,3},{3,2},{4,5},{5,4},{6,7},{7,6},{8,9},{9,8},{10,11... | collective-permute-start | bytes 49160 | tf_op jit(solution)/shard_map/ppermute | solution.py:429
  20.9 0.0 copy-done.1
  20.9 0.1 collective-permute-start.10
  21.1 0.7 %collective-permute-done.6.back_ref = f32[1,4,1024]{2,1,0:T(4,128)S(1)} collective-permute-done((f32[1,4,1024]{2,1,0:T(4,128)S(1)}, f32[1,4,1024]{2,1,0:T(4,128)S(1)}, u32[]{:S(2)}, u32[]{:S(2)}) %collective-permute-start.6) | collective-permute-done | bytes 16416 | tf_op jit(solution)/shard_map/ppermute | solution.py:429
  21.8 0.3 shard_map.66
  22.0 0.0 collective-permute-done.4
  22.1 0.0 collective-permute-done.8.refs_2_
  22.1 0.0 collective-permute-done.9.refs_3_
  22.1 0.4 %shard_map.67 = (bf16[256,2048]{1,0:T(8,128)(2,1)S(1)}, f32[1,2048]{1,0:T(1,128)S(1)}) custom-call(bf16[64,2048]{1,0:T(8,128)(2,1)S(1)} %copy-done, bf16[64,2048]{1,0:T(8,128)(2,1)S(1)} %collective-permute-done.7.refs_1_, bf16[64,2048]{1,0:T(8,128)(2,1)S(1)} %collective-permute-done.8.refs_2_, bf16[64,2048]{1,0:T(8,128)(2,1)S(1)} %collective-permute-done.9.refs_3_), custom_call_target="tpu_custom_call" | custom-call | flops 2097152 | bytes 2097152 | tf_op jit(solution)/shard_map/pallas_call | solution.py:39
  22.5 1.0 %shard_map.68 = (f32[3,256,256]{2,1,0:T(8,128)S(1)}, f32[8,256]{1,0:T(8,128)S(1)}) custom-call(bf16[256,2048]{1,0:T(8,128)(2,1)S(1)} %get-tuple-element.32.anomaly_ref, f32[1,2048]{1,0:T(1,128)S(1)} %get-tuple-element.33.mean_ref, f32[18,8,128]{2,1,0:T(8,128)S(1)} %get-tuple-element.26.refs_0_.refs_4_, f32[18,8,128]{2,1,0:T(8,128)S(1)} %get-tuple-element.27.refs_1_.refs_5_), custom_call_target="tpu_custom_call" | custom-call | flops 805306368 | bytes 1835008 | tf_op jit(solution)/shard_map/pallas_call | solution.py:39
  23.6 1.0 %shard_map.69 = (f32[3,256,256]{2,1,0:T(8,128)S(1)}, f32[8,256]{1,0:T(8,128)S(1)}) custom-call(bf16[256,2048]{1,0:T(8,128)(2,1)S(1)} %get-tuple-element.32.anomaly_ref, f32[1,2048]{1,0:T(1,128)S(1)} %get-tuple-element.33.mean_ref, f32[18,8,128]{2,1,0:T(8,128)S(1)} %get-tuple-element.26.refs_0_.refs_4_, f32[18,8,128]{2,1,0:T(8,128)S(1)} %get-tuple-element.27.refs_1_.refs_5_, ...), custom_call_target="tpu_custom_call" | custom-call | flops 805306368 | bytes 1835008 | tf_op jit(solution)/shard_map/pallas_call | solution.py:39
  24.6 0.0 collective-permute-done.10.blend_ref
  24.6 0.3 shard_map.70
  24.9 3.8 %shard_map.71 = (bf16[6,256,256]{2,1,0:T(8,128)(2,1)S(1)}, bf16[512,256]{1,0:T(8,128)(2,1)S(1)}) custom-call(s32[2]{0:T(128)S(1)} %get-tuple-element.24.flip_ref, bf16[2,64,128]{2,1,0:T(8,128)(2,1)S(1)} %shard_map.65.refs_0_, bf16[2,64,128]{2,1,0:T(8,128)(2,1)S(1)} %collective-permute-done.3.refs_1_, bf16[2,64,128]{2,1,0:T(8,128)(2,1)S(1)} %get-tuple-element.44.refs_2_, ...), custom_call_target="tpu_custom_call" | custom-call | flops 1610612736 | bytes 3145728 | tf_op jit(solution)/shard_map/pallas_call | solution.py:39
  28.6 0.4 %collective-permute-start.11 = (bf16[512,256]{1,0:T(8,128)(2,1)S(1)}, bf16[512,256]{1,0:T(8,128)(2,1)S(1)}, u32[]{:S(2)}, u32[]{:S(2)}) collective-permute-start(bf16[512,256]{1,0:T(8,128)(2,1)S(1)} %get-tuple-element.42), channel_id=1, source_target_pairs={{0,1},{1,0},{2,3},{3,2},{4,5},{5,4},{6,7},{7,6},{8,9},{9,8},{10,11... | collective-permute-start | bytes 786440 | tf_op jit(solution)/shard_map/ppermute | solution.py:429
  29.1 0.7 %shard_map.72 = f32[512,256]{1,0:T(8,128)S(1)} custom-call(bf16[6,256,256]{2,1,0:T(8,128)(2,1)S(1)} %get-tuple-element.41.transform_ref, bf16[256,2048]{1,0:T(8,128)(2,1)S(1)} %get-tuple-element.32.anomaly_ref, f32[1,2048]{1,0:T(1,128)S(1)} %get-tuple-element.33.mean_ref, f32[4,512]{1,0:T(4,128)S(1)} %copy-done.1), custom_call_target="tpu_custom_call" | custom-call | flops 134217728 | bytes 1048576 | tf_op jit(solution)/shard_map/pallas_call | solution.py:39
  29.7 0.5 %collective-permute-done.11 = bf16[512,256]{1,0:T(8,128)(2,1)S(1)} collective-permute-done((bf16[512,256]{1,0:T(8,128)(2,1)S(1)}, bf16[512,256]{1,0:T(8,128)(2,1)S(1)}, u32[]{:S(2)}, u32[]{:S(2)}) %collective-permute-start.11) | collective-permute-done | bytes 262176 | tf_op jit(solution)/shard_map/ppermute | solution.py:429
  30.2 0.8 %add_convert_fusion = bf16[512,256]{1,0:T(8,128)(2,1)} fusion(f32[512,256]{1,0:T(8,128)S(1)} %shard_map.72, bf16[512,256]{1,0:T(8,128)(2,1)S(1)} %collective-permute-done.11), kind=kLoop, calls=%fused_computation | loop fusion | flops 393216 | bytes 1048576 | tf_op jit(solution)/shard_map/convert_element_type | solution.py:559
  (5 shorter events, 0.1 us)
Async XLA Ops:
  0.7 4.9 %collective-permute-start = (bf16[1,64,128]{2,1,0:T(8,128)(2,1)S(1)}, bf16[1,64,128]{2,1,0:T(8,128)(2,1)S(1)}, u32[]{:S(2)}, u32[]{:S(2)}) collective-permute-start(bf16[1,64,128]{2,1,0:T(8,128)(2,1)S(1)} %slice_bitcast_fusion), channel_id=1, source_target_pairs={{0,17},{1,16},{2,19},{3,18},{4,21},{5,20},{6,23},{7,22},{8,25},{9,... | collective-permute-start | bytes 49160 | tf_op jit(solution)/shard_map/ppermute | solution.py:429
  5.7 6.1 %copy-start.2 = (f32[1,1024]{1,0:T(1,128)S(1)}, f32[1,1024]{1,0:T(1,128)}, u32[]{:S(2)}) copy-start(f32[1,1024]{1,0:T(1,128)} %report_ref.3) | copy-start | bytes 12292
  5.7 6.1 %copy-start.3 = (f32[1,4,1024]{2,1,0:T(4,128)S(1)}, f32[1,4,1024]{2,1,0:T(4,128)}, u32[]{:S(2)}) copy-start(f32[1,4,1024]{2,1,0:T(4,128)} %weight_ref.1) | copy-start | bytes 49156
  5.7 6.1 %copy-start.4 = (s32[1,1024]{1,0:T(1,128)S(1)}, s32[1,1024]{1,0:T(1,128)}, u32[]{:S(2)}) copy-start(s32[1,1024]{1,0:T(1,128)} %cell_ref.1) | copy-start | bytes 12292
  5.7 3.6 %collective-permute-start.1 = (bf16[2,64,128]{2,1,0:T(8,128)(2,1)S(1)}, bf16[2,64,128]{2,1,0:T(8,128)(2,1)S(1)}, u32[]{:S(2)}, u32[]{:S(2)}) collective-permute-start(bf16[2,64,128]{2,1,0:T(8,128)(2,1)S(1)} %pad_maximum_fusion.2), channel_id=1, source_target_pairs={{0,9},{1,8},{2,11},{3,10},{4,13},{5,12},{6,15},{7,14},{8,1},{9,0},... | collective-permute-start | bytes 98312 | tf_op jit(solution)/shard_map/ppermute | solution.py:429
  7.6 11.8 %collective-permute-start.7 = (bf16[64,2048]{1,0:T(8,128)(2,1)}, bf16[64,2048]{1,0:T(8,128)(2,1)S(1)}, u32[]{:S(2)}, u32[]{:S(2)}) collective-permute-start(bf16[64,2048]{1,0:T(8,128)(2,1)} %refs_0_.1), channel_id=1, source_target_pairs={{0,3},{1,2},{2,1},{3,0},{4,7},{5,6},{6,5},{7,4},{8,11},{9,10},{10,... | collective-permute-start | bytes 786440 | tf_op jit(solution)/shard_map/ppermute | solution.py:429
  9.3 9.8 %copy-start = (bf16[64,2048]{1,0:T(8,128)(2,1)S(1)}, bf16[64,2048]{1,0:T(8,128)(2,1)}, u32[]{:S(2)}) copy-start(bf16[64,2048]{1,0:T(8,128)(2,1)} %refs_0_.1) | copy-start | bytes 786436
  9.3 4.0 %collective-permute-start.2 = (bf16[4,64,128]{2,1,0:T(8,128)(2,1)S(1)}, bf16[4,64,128]{2,1,0:T(8,128)(2,1)S(1)}, u32[]{:S(2)}, u32[]{:S(2)}) collective-permute-start(bf16[4,64,128]{2,1,0:T(8,128)(2,1)S(1)} %pad_maximum_fusion.near_ref), channel_id=1, source_target_pairs={{0,5},{1,4},{2,7},{3,6},{4,1},{5,0},{6,3},{7,2},{8,13},{9,12},{10,... | collective-permute-start | bytes 196616 | tf_op jit(solution)/shard_map/ppermute | solution.py:429
  13.3 7.6 %copy-start.1 = (f32[4,512]{1,0:T(4,128)S(1)}, f32[4,512]{1,0:T(4,128)}, u32[]{:S(2)}) copy-start(f32[4,512]{1,0:T(4,128)} %blend_ref.1) | copy-start | bytes 24580
  13.3 3.9 %collective-permute-start.3 = (bf16[2,64,128]{2,1,0:T(8,128)(2,1)S(1)}, bf16[2,64,128]{2,1,0:T(8,128)(2,1)S(1)}, u32[]{:S(2)}, u32[]{:S(2)}) collective-permute-start(bf16[2,64,128]{2,1,0:T(8,128)(2,1)S(1)} %shard_map.65.refs_0_), channel_id=1, source_target_pairs={{0,3},{1,2},{2,1},{3,0},{4,7},{5,6},{6,5},{7,4},{8,11},{9,10},{10,... | collective-permute-start | bytes 98312 | tf_op jit(solution)/shard_map/ppermute | solution.py:429
  17.2 4.9 %collective-permute-start.4 = (bf16[4,64,128]{2,1,0:T(8,128)(2,1)S(1)}, bf16[4,64,128]{2,1,0:T(8,128)(2,1)S(1)}, u32[]{:S(2)}, u32[]{:S(2)}) collective-permute-start(bf16[4,64,128]{2,1,0:T(8,128)(2,1)S(1)} %pad_maximum_fusion.1), channel_id=1, source_target_pairs={{0,1},{1,0},{2,3},{3,2},{4,5},{5,4},{6,7},{7,6},{8,9},{9,8},{10,11... | collective-permute-start | bytes 196616 | tf_op jit(solution)/shard_map/ppermute | solution.py:429
  17.4 3.2 %collective-permute-start.5 = (f32[1,4,1024]{2,1,0:T(4,128)S(1)}, f32[1,4,1024]{2,1,0:T(4,128)S(1)}, u32[]{:S(2)}, u32[]{:S(2)}) collective-permute-start(f32[1,4,1024]{2,1,0:T(4,128)S(1)} %copy-done.3), channel_id=1, source_target_pairs={{0,3},{1,2},{2,1},{3,0},{4,7},{5,6},{6,5},{7,4},{8,11},{9,10},{10,... | collective-permute-start | bytes 49160 | tf_op jit(solution)/shard_map/ppermute | solution.py:458
  19.1 3.0 %collective-permute-start.8 = (bf16[64,2048]{1,0:T(8,128)(2,1)S(1)}, bf16[64,2048]{1,0:T(8,128)(2,1)S(1)}, u32[]{:S(2)}, u32[]{:S(2)}) collective-permute-start(bf16[64,2048]{1,0:T(8,128)(2,1)S(1)} %copy-done), channel_id=1, source_target_pairs={{0,1},{1,0},{2,3},{3,2},{4,5},{5,4},{6,7},{7,6},{8,9},{9,8},{10,11... | collective-permute-start | bytes 786440 | tf_op jit(solution)/shard_map/ppermute | solution.py:429
  19.5 2.6 %collective-permute-start.9 = (bf16[64,2048]{1,0:T(8,128)(2,1)S(1)}, bf16[64,2048]{1,0:T(8,128)(2,1)S(1)}, u32[]{:S(2)}, u32[]{:S(2)}) collective-permute-start(bf16[64,2048]{1,0:T(8,128)(2,1)S(1)} %collective-permute-done.7.refs_1_), channel_id=1, source_target_pairs={{0,1},{1,0},{2,3},{3,2},{4,5},{5,4},{6,7},{7,6},{8,9},{9,8},{10,11... | collective-permute-start | bytes 786440 | tf_op jit(solution)/shard_map/ppermute | solution.py:429
  20.6 1.2 %collective-permute-start.6 = (f32[1,4,1024]{2,1,0:T(4,128)S(1)}, f32[1,4,1024]{2,1,0:T(4,128)S(1)}, u32[]{:S(2)}, u32[]{:S(2)}) collective-permute-start(f32[1,4,1024]{2,1,0:T(4,128)S(1)} %collective-permute-done.5.across_ref), channel_id=1, source_target_pairs={{0,1},{1,0},{2,3},{3,2},{4,5},{5,4},{6,7},{7,6},{8,9},{9,8},{10,11... | collective-permute-start | bytes 49160 | tf_op jit(solution)/shard_map/ppermute | solution.py:429
  20.9 3.7 %collective-permute-start.10 = (f32[4,512]{1,0:T(4,128)S(1)}, f32[4,512]{1,0:T(4,128)S(1)}, u32[]{:S(2)}, u32[]{:S(2)}) collective-permute-start(f32[4,512]{1,0:T(4,128)S(1)} %copy-done.1), channel_id=1, source_target_pairs={{0,1},{1,0},{2,3},{3,2},{4,5},{5,4},{6,7},{7,6},{8,9},{9,8},{10,11... | collective-permute-start | bytes 24584 | tf_op jit(solution)/shard_map/ppermute | solution.py:429
  28.6 1.6 %collective-permute-start.11 = (bf16[512,256]{1,0:T(8,128)(2,1)S(1)}, bf16[512,256]{1,0:T(8,128)(2,1)S(1)}, u32[]{:S(2)}, u32[]{:S(2)}) collective-permute-start(bf16[512,256]{1,0:T(8,128)(2,1)S(1)} %get-tuple-element.42), channel_id=1, source_target_pairs={{0,1},{1,0},{2,3},{3,2},{4,5},{5,4},{6,7},{7,6},{8,9},{9,8},{10,11... | collective-permute-start | bytes 786440 | tf_op jit(solution)/shard_map/ppermute | solution.py:429
